TPU v7x, 128 devices: a whole 4x4x4 slice. The times are simulated.
128 devices in a mesh: col: 32 (over z, y_hi, x), row: 4 (over y_lo, core).
Axes of the slice: x: 4, y: 4 (y_hi: 2, y_lo: 2; y = y_hi * 2 + y_lo), z: 4, core: 2. Of those that a mesh axis runs over, the one named last changes fastest.
Arguments:
- diffs: float32 [32768, 8192], P(('col', 'row')), as said below
- pairing: int32 [64], replicated, may hold values from 0 to 63, each once
Outputs:
- rotated: float32 [32, 4, 256, 8192], P(None, 'row', None, 'col')
Inputs may be any that keep to these rules, and one draw needn't show every extreme that they name: `pairing`: a permutation: every block index appears once. `diffs`: token rows with finite entries.
All inputs are finite; a program needn't handle non-finite values.
Results may differ from a plain program's by a relative error of at most 0.00025.
Values sent between devices are 32-bit elements; how exact they have to be, the bound alone decides.
No kernel may reach another device: no remote copies, remote signals or barrier semaphores. Data moves between devices by JAX's collectives and lax.ppermute only.
A program may use at most 128 MiB of HBM per device.

v0:
```python
import jax
import jax.numpy as jnp
from jax import lax
from jax.sharding import PartitionSpec as P

BLOCK = 128
JACOBI_STEPS = 2
INNER_STEPS = 2


def shifted(value, axis, steps):
    count = lax.axis_size(axis)
    leading, last = (max(0, -steps), min(count, count - steps))
    return lax.ppermute(value, axis, [(source, source + steps) for source in range(leading, last)])


def pair_rotation(pair_gram):
    rotation = jnp.eye(pair_gram.shape[0], dtype=jnp.float32)
    for repeat_index in range(INNER_STEPS):
        product = jnp.dot(
            pair_gram, rotation, precision=lax.Precision.HIGHEST, preferred_element_type=jnp.float32
        )
        normal_matrix = lax.dot_general(
            product,
            product,
            (((0,), (0,)), ((), ())),
            precision=lax.Precision.HIGHEST,
            preferred_element_type=jnp.float32,
        )
        factor = jnp.linalg.cholesky(normal_matrix)
        rotation = lax.linalg.triangular_solve(factor, product.T, left_side=True, lower=True).T
    return rotation


def local_gram(pair_rows):
    return lax.dot_general(
        pair_rows,
        pair_rows,
        (((0,), (0,)), ((), ())),
        precision=lax.Precision.HIGHEST,
        preferred_element_type=jnp.float32,
    )


def row_total(partial_gram):
    return lax.psum(partial_gram, "row")


def send_down(lower_half):
    return shifted(lower_half, "col", -1)


def send_up(outgoing):
    return shifted(outgoing, "col", 1)


def turn_and_move(pair_rows, rotation, position, col_count):
    turned = jnp.dot(
        pair_rows, rotation, precision=lax.Precision.HIGHEST, preferred_element_type=jnp.float32
    )
    upper_half = turned[:, :BLOCK]
    lower_half = turned[:, BLOCK:]
    from_above = send_down(lower_half)
    from_below = send_up(jnp.where(position == 0, lower_half, upper_half))
    new_upper = jnp.where(position == 0, upper_half, from_below)
    new_lower = jnp.where(position == col_count - 1, upper_half, from_above)
    return jnp.concatenate([new_upper, new_lower], axis=1)


def local(diffs, pairing):
    col_count = lax.axis_size("col")
    position = lax.axis_index("col")
    pair_width = 2 * BLOCK
    local_rows = diffs.shape[0]
    blocks = diffs.reshape(local_rows, 2 * col_count, BLOCK)
    ordered = jnp.take(blocks, pairing, axis=1).reshape(local_rows, col_count, pair_width)
    pair_rows = lax.all_to_all(ordered, "col", split_axis=1, concat_axis=0, tiled=True).reshape(
        -1, pair_width
    )
    pair_gram = row_total(local_gram(pair_rows))
    for jacobi_step in range(JACOBI_STEPS):
        if jacobi_step > 0:
            pair_gram = row_total(local_gram(pair_rows))
        rotation = pair_rotation(pair_gram)
        if jacobi_step + 1 < JACOBI_STEPS:
            pair_rows = turn_and_move(pair_rows, rotation, position, col_count)
        else:
            pair_rows = jnp.dot(
                pair_rows,
                rotation,
                precision=lax.Precision.HIGHEST,
                preferred_element_type=jnp.float32,
            )
    return pair_rows.reshape(col_count, 1, local_rows, pair_width)


def solution(mesh):
    in_specs = (P(("col", "row"), None), P())
    out_specs = P(None, "row", None, "col")
    return jax.shard_map(local, mesh=mesh, in_specs=in_specs, out_specs=out_specs, check_vma=False)
```

profile of v0, /device:TPU:32, one launch (start us, length us, event | category | flops | bytes accessed | tf_op | source)
XLA Modules:
  0.0 664.9 jit_solution(18403592186833088471)
XLA Ops:
  33.7 9.0 %copy.19 = f32[256,64,128]{0,2,1:T(8,128)} copy(f32[256,64,128]{2,0,1:T(8,128)} %bitcast.165) | data formatting | bytes 16777216 | tf_op jit(solution)/shard_map/jit(_take)/gather | solution.py:76
  56.2 105.9 %all_to_all.15 = f32[256,32,256]{2,0,1:T(8,128)S(1)} all-to-all(f32[256,32,256]{2,0,1:T(8,128)S(1)} %broadcast_select_fusion), channel_id=1, replica_groups=mesh['col'=32,'row'=4] {'col'}, dimensions={1} | all-to-all | bytes 16777216 | tf_op jit(solution)/shard_map/all_to_all | solution.py:77
  165.5 14.9 %fusion.4 = f32[256,256]{1,0:T(8,128)} fusion(f32[256,32,256]{2,0,1:T(8,128)S(1)} %all_to_all.15), kind=kOutput, calls=%fused_computation.18 | convolution fusion | flops 6442450944 | bytes 8650752 | tf_op jit(solution)/shard_map/dot_general | solution.py:36
  180.5 34.1 %all-reduce.4.cloned.1.call-done = f32[256,256]{1,0:T(8,128)} async-done(((f32[256,256]{1,0:T(8,128)}), f32[256,256]{1,0:T(8,128)}) %all-reduce.4.cloned.1.call-update) | async-done | bytes 262160 | tf_op jit(solution)/shard_map/psum | solution.py:46
  216.6 11.7 %cholesky.214 = f32[128,128]{1,0:T(8,128)S(1)} custom-call(f32[128,128]{1,0:T(8,128)S(1)} %cholesky.346), custom_call_target="Cholesky" | custom-call | tf_op jit(solution)/shard_map/jit(cholesky)/cholesky | solution.py:30
  228.4 9.8 %custom-call.17 = f32[1,128,128]{1,2,0:T(8,128)S(1)} custom-call(f32[1,128,128]{2,1,0:T(8,128)S(1)} %get-tuple-element.96), custom_call_target="InvertDiagBlocksLowerTriangular" | custom-call | tf_op jit(solution)/shard_map/jit(cholesky)/cholesky | solution.py:30
  238.7 11.7 %cholesky.231 = f32[128,128]{1,0:T(8,128)S(1)} custom-call(f32[128,128]{1,0:T(8,128)S(1)} %convolution_subtract_fusion.7), custom_call_target="Cholesky" | custom-call | tf_op jit(solution)/shard_map/jit(cholesky)/cholesky | solution.py:30
  256.8 19.7 %custom-call.18 = f32[2,128,128]{1,2,0:T(8,128)S(1)} custom-call(f32[2,128,128]{2,1,0:T(8,128)S(1)} %get-tuple-element.33), custom_call_target="InvertDiagBlocksLowerTriangular" | custom-call | tf_op jit(solution)/shard_map/triangular_solve/custom-call.0 | solution.py:31
  279.7 11.7 %cholesky.248 = f32[128,128]{1,0:T(8,128)S(1)} custom-call(f32[128,128]{1,0:T(8,128)S(1)} %cholesky.349), custom_call_target="Cholesky" | custom-call | tf_op jit(solution)/shard_map/jit(cholesky)/cholesky | solution.py:30
  291.4 9.8 %custom-call.19 = f32[1,128,128]{1,2,0:T(8,128)S(1)} custom-call(f32[1,128,128]{2,1,0:T(8,128)S(1)} %get-tuple-element.92), custom_call_target="InvertDiagBlocksLowerTriangular" | custom-call | tf_op jit(solution)/shard_map/jit(cholesky)/cholesky | solution.py:30
  301.7 11.7 %cholesky.265 = f32[128,128]{1,0:T(8,128)S(1)} custom-call(f32[128,128]{1,0:T(8,128)S(1)} %convolution_subtract_fusion.6), custom_call_target="Cholesky" | custom-call | tf_op jit(solution)/shard_map/jit(cholesky)/cholesky | solution.py:30
  320.4 19.7 %custom-call.20 = f32[2,128,128]{1,2,0:T(8,128)S(1)} custom-call(f32[2,128,128]{2,1,0:T(8,128)S(1)} %get-tuple-element.34), custom_call_target="InvertDiagBlocksLowerTriangular" | custom-call | tf_op jit(solution)/shard_map/triangular_solve/custom-call.0 | solution.py:31
  341.2 10.7 %fusion.11 = f32[8192,256]{0,1:T(8,128)S(1)} fusion(f32[8192,256]{1,0:T(8,128)} %bitcast.164, f32[128,256]{1,0:T(8,128)S(1)} %fusion.45, f32[128,256]{1,0:T(8,128)S(1)} %fusion.32), kind=kOutput, calls=%fused_computation.35 | convolution fusion | flops 6442516480 | bytes 17039360 | tf_op jit(solution)/shard_map/dot_general | solution.py:58
  368.6 88.7 %collective-permute-done = f32[8192,128]{0,1:T(8,128)} collective-permute-done((f32[8192,128]{0,1:T(8,128)}, f32[8192,128]{0,1:T(8,128)}, u32[]{:S(2)}, u32[]{:S(2)}) %collective-permute-start) | collective-permute-done | bytes 4194336 | tf_op jit(solution)/shard_map/ppermute | solution.py:14
  474.7 38.8 %all-reduce.6.cloned.1.call-done = f32[256,256]{1,0:T(8,128)} async-done(((f32[256,256]{1,0:T(8,128)}), f32[256,256]{1,0:T(8,128)}) %all-reduce.6.cloned.1.call-update) | async-done | bytes 262160 | tf_op jit(solution)/shard_map/psum | solution.py:46
  515.5 11.9 %cholesky.282 = f32[128,128]{1,0:T(8,128)S(1)} custom-call(f32[128,128]{1,0:T(8,128)S(1)} %cholesky.352), custom_call_target="Cholesky" | custom-call | tf_op jit(solution)/shard_map/jit(cholesky)/cholesky | solution.py:30
  527.4 9.8 %custom-call.21 = f32[1,128,128]{1,2,0:T(8,128)S(1)} custom-call(f32[1,128,128]{2,1,0:T(8,128)S(1)} %get-tuple-element.88), custom_call_target="InvertDiagBlocksLowerTriangular" | custom-call | tf_op jit(solution)/shard_map/jit(cholesky)/cholesky | solution.py:30
  537.7 11.7 %cholesky.299 = f32[128,128]{1,0:T(8,128)S(1)} custom-call(f32[128,128]{1,0:T(8,128)S(1)} %convolution_subtract_fusion.5), custom_call_target="Cholesky" | custom-call | tf_op jit(solution)/shard_map/jit(cholesky)/cholesky | solution.py:30
  555.8 19.9 %custom-call.22 = f32[2,128,128]{1,2,0:T(8,128)S(1)} custom-call(f32[2,128,128]{2,1,0:T(8,128)S(1)} %get-tuple-element.35), custom_call_target="InvertDiagBlocksLowerTriangular" | custom-call | tf_op jit(solution)/shard_map/triangular_solve/custom-call.0 | solution.py:31
  578.9 11.7 %cholesky.316 = f32[128,128]{1,0:T(8,128)S(1)} custom-call(f32[128,128]{1,0:T(8,128)S(1)} %cholesky.355), custom_call_target="Cholesky" | custom-call | tf_op jit(solution)/shard_map/jit(cholesky)/cholesky | solution.py:30
  590.7 9.8 %custom-call.23 = f32[1,128,128]{1,2,0:T(8,128)S(1)} custom-call(f32[1,128,128]{2,1,0:T(8,128)S(1)} %get-tuple-element.84), custom_call_target="InvertDiagBlocksLowerTriangular" | custom-call | tf_op jit(solution)/shard_map/jit(cholesky)/cholesky | solution.py:30
  601.0 11.7 %cholesky.333 = f32[128,128]{1,0:T(8,128)S(1)} custom-call(f32[128,128]{1,0:T(8,128)S(1)} %convolution_subtract_fusion.4), custom_call_target="Cholesky" | custom-call | tf_op jit(solution)/shard_map/jit(cholesky)/cholesky | solution.py:30
  619.4 19.7 %custom-call.24 = f32[2,128,128]{1,2,0:T(8,128)S(1)} custom-call(f32[2,128,128]{2,1,0:T(8,128)S(1)} %get-tuple-element.36), custom_call_target="InvertDiagBlocksLowerTriangular" | custom-call | tf_op jit(solution)/shard_map/triangular_solve/custom-call.0 | solution.py:31
  640.1 17.7 %fusion.2 = f32[8192,256]{1,0:T(8,128)} fusion(f32[8192,128]{0,1:T(8,128)} %copy-done.3, f32[8192,128]{0,1:T(8,128)} %copy-done.2, f32[128,256]{1,0:T(8,128)S(1)} %fusion.37, f32[128,256]{1,0:T(8,128)S(1)} %fusion.28), kind=kOutput, calls=%fused_computation.12 | convolution fusion | flops 6444613632 | bytes 17039360 | tf_op jit(solution)/shard_map/dot_general | solution.py:88
  (126 shorter events, 129.5 us)
Async XLA Ops:
  6.5 208.1 %all-reduce.4.cloned.1.call-start = ((), (), s32[]{:S(2)}) async-start(), calls=%async_computation.1 | async-start | bytes 524288 | tf_op jit(solution)/shard_map/psum | solution.py:46
  162.1 3.4 copy-start
  180.5 333.0 %all-reduce.6.cloned.1.call-start = ((), (), s32[]{:S(2)}) async-start(), calls=%async_computation.2 | async-start | bytes 524288 | tf_op jit(solution)/shard_map/psum | solution.py:46
  351.9 5.9 copy-start.1
  357.8 99.5 %collective-permute-start = (f32[8192,128]{0,1:T(8,128)}, f32[8192,128]{0,1:T(8,128)}, u32[]{:S(2)}, u32[]{:S(2)}) collective-permute-start(f32[8192,128]{0,1:T(8,128)} %get-tuple-element.79), channel_id=1, source_target_pairs={{0,4},{4,8},{8,12},{12,16},{16,20},{20,24},{24,28},{28,32},{32,36}... | collective-permute-start | bytes 12582920 | tf_op jit(solution)/shard_map/ppermute | solution.py:14
  361.2 97.3 %collective-permute-start.1 = (f32[8192,128]{0,1:T(8,128)}, f32[8192,128]{0,1:T(8,128)}, u32[]{:S(2)}, u32[]{:S(2)}) collective-permute-start(f32[8192,128]{0,1:T(8,128)} %get-tuple-element.80), channel_id=1, source_target_pairs={{4,0},{8,4},{12,8},{16,12},{20,16},{24,20},{28,24},{32,28},{36,32}... | collective-permute-start | bytes 12582920 | tf_op jit(solution)/shard_map/ppermute | solution.py:14
  463.9 2.0 copy-start.2
  463.9 3.2 copy-start.3
Sparse Core Ops, SparseCore 0:
  180.6 33.9 all-reduce.3
  474.8 38.6 all-reduce.5
where the time goes:
time: 671 us; the launch traced here: 665 us
  other arithmetic  232 us (35%)
  waiting for transfers between devices  163 us (24%)
  blocking collectives  106 us (16%)
  local copies, waits for them, and re-layouts  68.7 us (10%)
  matrix products  64.3 us (10%)
  between operations  19.2 us (3%)
  starting transfers between devices  10.8 us (2%)
    another operation x27, other arithmetic, pair_rotation(): factor = jnp.linalg.cholesky(normal_matrix)  138 us
    all_to_all x1, blocking collectives, local(): lax.all_to_all(ordered, 'col', split_axis=1, concat_axis=0, tiled=True)  106 us
    ppermute x2, waiting for transfers between devices, shifted(): lax.ppermute(value, axis, [(source, source + steps) for source in range(l...  89.9 us
    another operation x9, other arithmetic, pair_rotation(): lax.linalg.triangular_solve(factor, product.T, left_side=True, lower=True)  79 us
    psum x2, waiting for transfers between devices, row_total(): return lax.psum(partial_gram, 'row')  72.9 us
    gather x3, local copies, waits for them, and re-layouts, local(): jnp.take(blocks, pairing, axis=1).reshape(local_rows, col_count, pair_width)  25.8 us
    dot_general x2, matrix products, local_gram(): lax.dot_general(pair_rows, pair_rows, (((0,), (0,)), ((), ())), precision...  22.5 us
    dot_general x1, matrix products, local(): jnp.dot(pair_rows, rotation, precision=lax.Precision.HIGHEST, preferred_e...  17.7 us
  transfers between devices with their start and end apart: 4, of which 4 were waited for; matrix products, arithmetic and copies ran while one was open for 0% of the time, Pallas kernels for 0%

commit v1 on v0

v1 whole, which is shorter than its diff:
```python
import functools

import jax
import jax.numpy as jnp
from jax import lax
from jax.experimental import pallas as pl
from jax.experimental.pallas import tpu as pltpu
from jax.sharding import PartitionSpec as P

BLOCK = 128
WIDTH = 2 * BLOCK
TILE = 1024
PANEL = 32
HIGHEST = lax.Precision.HIGHEST
COLUMNS = (((0,), (0,)), ((), ()))
LANES = (((1,), (1,)), ((), ()))
F32 = jnp.float32
BF16 = jnp.bfloat16


def grant(megabytes):
    return pltpu.CompilerParams(vmem_limit_bytes=megabytes << 20)


def two_terms(value):
    high = value.astype(BF16)
    return high, (value - high.astype(F32)).astype(BF16)


def three_terms(value):
    high = value.astype(BF16)
    rest = value - high.astype(F32)
    middle = rest.astype(BF16)
    return high, middle, (rest - middle.astype(F32)).astype(BF16)


def order_kernel(pairing_ref, first_ref, second_ref, out_ref):
    out_ref[0, :, :BLOCK] = first_ref[...]
    out_ref[0, :, BLOCK:] = second_ref[...]


def order_pairs(diffs, pairing):
    rows, columns = diffs.shape
    count = columns // WIDTH
    return pl.pallas_call(
        order_kernel,
        grid_spec=pltpu.PrefetchScalarGridSpec(
            num_scalar_prefetch=1,
            grid=(count,),
            in_specs=[
                pl.BlockSpec((rows, BLOCK), lambda p, pairing: (0, pairing[2 * p])),
                pl.BlockSpec((rows, BLOCK), lambda p, pairing: (0, pairing[2 * p + 1])),
            ],
            out_specs=pl.BlockSpec((1, rows, WIDTH), lambda p, pairing: (p, 0, 0)),
        ),
        out_shape=jax.ShapeDtypeStruct((count, rows, WIDTH), F32),
        compiler_params=grant(16),
        name="order",
    )(pairing, diffs, diffs)


def add_gram(tile, total_ref, cross_ref):
    high, low = two_terms(tile)
    total_ref[...] += lax.dot_general(high, high, COLUMNS, preferred_element_type=F32)
    cross_ref[...] += lax.dot_general(high, low, COLUMNS, preferred_element_type=F32)


def gram_kernel(tile_ref, total_ref, cross_ref):
    @pl.when(pl.program_id(0) == 0)
    def _():
        total_ref[...] = jnp.zeros_like(total_ref)
        cross_ref[...] = jnp.zeros_like(cross_ref)

    add_gram(tile_ref[...], total_ref, cross_ref)

    @pl.when(pl.program_id(0) == pl.num_programs(0) - 1)
    def _():
        total_ref[...] += cross_ref[...] + cross_ref[...].T


def local_gram(pair_rows):
    rows = pair_rows.shape[0]
    return pl.pallas_call(
        gram_kernel,
        grid=(rows // TILE,),
        in_specs=[pl.BlockSpec((TILE, WIDTH), lambda i: (i, 0))],
        out_specs=pl.BlockSpec((WIDTH, WIDTH), lambda i: (0, 0)),
        out_shape=jax.ShapeDtypeStruct((WIDTH, WIDTH), F32),
        scratch_shapes=[pltpu.VMEM((WIDTH, WIDTH), F32)],
        compiler_params=grant(16),
        name="gram",
    )(pair_rows)


def moved_tile(ends, from_below, kept_second, from_above, kept_first):
    upper = jnp.where(ends[0] == 1, kept_second, from_below)
    lower = jnp.where(ends[1] == 1, kept_first, from_above)
    return jnp.concatenate([upper, lower], axis=1)


def moved_gram_kernel(ends, below_ref, second_ref, above_ref, first_ref, total_ref, cross_ref):
    @pl.when(pl.program_id(0) == 0)
    def _():
        total_ref[...] = jnp.zeros_like(total_ref)
        cross_ref[...] = jnp.zeros_like(cross_ref)

    tile = moved_tile(ends, below_ref[...], second_ref[...], above_ref[...], first_ref[...])
    add_gram(tile, total_ref, cross_ref)

    @pl.when(pl.program_id(0) == pl.num_programs(0) - 1)
    def _():
        total_ref[...] += cross_ref[...] + cross_ref[...].T


def moved_specs():
    return [
        pl.BlockSpec((TILE, BLOCK), lambda i, ends: (i, 0)),
        pl.BlockSpec((TILE, BLOCK), lambda i, ends: (i * ends[0], 0)),
        pl.BlockSpec((TILE, BLOCK), lambda i, ends: (i, 0)),
        pl.BlockSpec((TILE, BLOCK), lambda i, ends: (i * ends[1], 0)),
    ]


def moved_gram(ends, moved):
    rows = moved[0].shape[0]
    return pl.pallas_call(
        moved_gram_kernel,
        grid_spec=pltpu.PrefetchScalarGridSpec(
            num_scalar_prefetch=1,
            grid=(rows // TILE,),
            in_specs=moved_specs(),
            out_specs=pl.BlockSpec((WIDTH, WIDTH), lambda i, ends: (0, 0)),
            scratch_shapes=[pltpu.VMEM((WIDTH, WIDTH), F32)],
        ),
        out_shape=jax.ShapeDtypeStruct((WIDTH, WIDTH), F32),
        compiler_params=grant(24),
        name="moved_gram",
    )(ends, *moved)


def row_total(partial_gram):
    count = lax.axis_size("row")
    step = 1
    while step < count:
        swap = [(source, source ^ step) for source in range(count)]
        partial_gram = partial_gram + lax.ppermute(partial_gram, "row", swap)
        step *= 2
    return partial_gram


def outer_product(left, right):
    left1, left2, left3 = three_terms(left)
    right1, right2, right3 = three_terms(right)
    left = jnp.concatenate([left1, left1, left2, left2, left1, left3], axis=0)
    right = jnp.concatenate([right1, right2, right1, right2, right3, right1], axis=0)
    return lax.dot_general(left, right, COLUMNS, preferred_element_type=F32)


def eliminate(work_ref, factor_ref, width):
    for start in range(0, WIDTH, PANEL):
        end = start + PANEL
        rows = work_ref[start:end, :width]
        row_id = lax.broadcasted_iota(jnp.int32, (PANEL, 1), 0)
        pivots = jnp.zeros((PANEL, 1), F32)
        for j in range(PANEL):
            column = rows[:, start + j : start + j + 1]
            pivot = column[j : j + 1, :]
            multiple = jnp.where(row_id > j, column / pivot, 0.0)
            pivots = jnp.where(row_id == j, pivot, pivots)
            rows = rows - multiple * rows[j : j + 1, :]
        rows = rows * lax.rsqrt(pivots)
        row_at = lax.broadcasted_iota(jnp.int32, (PANEL, width), 0) + start
        rows = jnp.where(lax.broadcasted_iota(jnp.int32, (PANEL, width), 1) >= row_at, rows, 0.0)
        factor_ref[start:end, :width] = rows
        if end < WIDTH:
            work_ref[end:, :width] -= outer_product(rows[:, end:WIDTH], rows)


def rotation_kernel(gram_ref, out_ref, work_ref, factor_ref):
    gram = gram_ref[...]
    work_ref[:, :WIDTH] = jnp.dot(gram, gram, precision=HIGHEST, preferred_element_type=F32)
    eliminate(work_ref, factor_ref, WIDTH)
    factor = factor_ref[:, :WIDTH]
    work_ref[:, :WIDTH] = lax.dot_general(
        factor, factor, LANES, precision=HIGHEST, preferred_element_type=F32
    )
    work_ref[:, WIDTH:] = factor
    eliminate(work_ref, factor_ref, 2 * WIDTH)
    out_ref[...] = factor_ref[:, WIDTH:]


def pair_rotation(pair_gram):
    return pl.pallas_call(
        rotation_kernel,
        out_shape=jax.ShapeDtypeStruct((WIDTH, WIDTH), F32),
        scratch_shapes=[pltpu.VMEM((WIDTH, 2 * WIDTH), F32)] * 2,
        compiler_params=grant(32),
        name="rotation",
    )(pair_gram)


def product(rows, rotation_t):
    high, low = two_terms(rows)
    turn_high, turn_low = two_terms(rotation_t)
    turned = lax.dot_general(high, turn_high, LANES, preferred_element_type=F32)
    turned += lax.dot_general(low, turn_high, LANES, preferred_element_type=F32)
    return turned + lax.dot_general(high, turn_low, LANES, preferred_element_type=F32)


def turn_kernel(rows_ref, rotation_ref, first_ref, second_ref):
    turned = product(rows_ref[...], rotation_ref[...])
    first_ref[...] = turned[:, :BLOCK]
    second_ref[...] = turned[:, BLOCK:]


def turn(pair_rows, rotation_t):
    rows = pair_rows.shape[0]
    half = pl.BlockSpec((TILE, BLOCK), lambda i: (i, 0))
    return pl.pallas_call(
        turn_kernel,
        grid=(rows // TILE,),
        in_specs=[
            pl.BlockSpec((TILE, WIDTH), lambda i: (i, 0)),
            pl.BlockSpec((WIDTH, WIDTH), lambda i: (0, 0)),
        ],
        out_specs=[half, half],
        out_shape=[jax.ShapeDtypeStruct((rows, BLOCK), F32)] * 2,
        compiler_params=grant(24),
        name="turn",
    )(pair_rows, rotation_t)


def moved_turn_kernel(ends, below_ref, second_ref, above_ref, first_ref, rotation_ref, out_ref):
    tile = moved_tile(ends, below_ref[...], second_ref[...], above_ref[...], first_ref[...])
    out_ref[...] = product(tile, rotation_ref[...])


def moved_turn(ends, moved, rotation_t):
    rows = moved[0].shape[0]
    return pl.pallas_call(
        moved_turn_kernel,
        grid_spec=pltpu.PrefetchScalarGridSpec(
            num_scalar_prefetch=1,
            grid=(rows // TILE,),
            in_specs=moved_specs() + [pl.BlockSpec((WIDTH, WIDTH), lambda i, ends: (0, 0))],
            out_specs=pl.BlockSpec((TILE, WIDTH), lambda i, ends: (i, 0)),
        ),
        out_shape=jax.ShapeDtypeStruct((rows, WIDTH), F32),
        compiler_params=grant(24),
        name="moved_turn",
    )(ends, *moved, rotation_t)


def local(diffs, pairing):
    col_count = lax.axis_size("col")
    position = lax.axis_index("col")
    local_rows = diffs.shape[0]
    ends = jnp.stack([position == 0, position == col_count - 1]).astype(jnp.int32)
    ordered = order_pairs(diffs, pairing)
    pair_rows = lax.all_to_all(ordered, "col", split_axis=0, concat_axis=0, tiled=True)
    pair_rows = pair_rows.reshape(-1, WIDTH)

    rotation_t = pair_rotation(row_total(local_gram(pair_rows)))
    swapped = jnp.concatenate([rotation_t[BLOCK:], rotation_t[:BLOCK]])
    first, second = turn(pair_rows, jnp.where(position == 0, swapped, rotation_t))
    above = lax.ppermute(second, "col", [(p, p - 1) for p in range(1, col_count)])
    below = lax.ppermute(first, "col", [(p, p + 1) for p in range(col_count - 1)])

    moved = (below, second, above, first)
    rotation_t = pair_rotation(row_total(moved_gram(ends, moved)))
    return moved_turn(ends, moved, rotation_t).reshape(col_count, 1, local_rows, WIDTH)


def solution(mesh):
    in_specs = (P(("col", "row"), None), P())
    out_specs = P(None, "row", None, "col")
    return jax.shard_map(local, mesh=mesh, in_specs=in_specs, out_specs=out_specs, check_vma=False)
```

time: 671 us -> 370 us (0.55)
  other arithmetic: 232 us -> 0.25 us
  Pallas kernels: 0 us -> 130 us
  matrix products: 64.3 us -> 0 us
  local copies, waits for them, and re-layouts: 68.7 us -> 10.8 us
  waiting for transfers between devices: 163 us -> 107 us
  between operations: 19.2 us -> 0.11 us
    another operation x36 -> x0, other arithmetic: 217 us -> none  [the longest x27 138 us: pair_rotation(): factor = jnp.linalg.cholesky(normal_matrix)]
    pallas_call x0 -> x7, Pallas kernels: none -> 130 us  [the longest x2 96.2 us: pair_rotation(): pl.pallas_call(rotation_kernel, out_shape=jax.ShapeDtypeStruct((WIDTH, WI...]
    psum x2 -> x0, waiting for transfers between devices: 72.9 us -> none  [row_total(): return lax.psum(partial_gram, 'row')]
    dot_general x12 -> x0, matrix products: 58.4 us -> none  [the longest x2 22.5 us: local_gram(): lax.dot_general(pair_rows, pair_rows, (((0,), (0,)), ((), ())), precision...]
    gather x3 -> x0, local copies, waits for them, and re-layouts: 25.8 us -> none  [local(): jnp.take(blocks, pairing, axis=1).reshape(local_rows, col_count, pair_width)]
    ppermute x2 -> x6, waiting for transfers between devices: 89.9 us -> 107 us  [the longest x1 87.9 us: local(): lax.ppermute(first, 'col', [(p, p + 1) for p in range(col_count - 1)])]
    another operation x37 -> x0, local copies, waits for them, and re-layouts: 15.8 us -> none  [the longest x29 15.7 us: pair_rotation(): lax.linalg.triangular_solve(factor, product.T, left_side=True, lower=True)]
    select_n x4 -> x1, other arithmetic: 14.5 us -> 0.04 us  [local(): jnp.where(position == 0, swapped, rotation_t)]
  transfers between devices with their start and end apart: 4 -> 6, of which waited for: 4 -> 6; matrix products, arithmetic and copies ran while one was open for 0% -> 0% of each run, Pallas kernels for 0% -> 0%
where the time goes in v1:
time: 370 us; the launch traced here: 367 us
  Pallas kernels  130 us (35%)
  waiting for transfers between devices  107 us (29%)
  blocking collectives  106 us (29%)
  starting transfers between devices  12.1 us (3%)
  local copies, waits for them, and re-layouts  10.8 us (3%)
    all_to_all x1, blocking collectives, local(): lax.all_to_all(ordered, 'col', split_axis=0, concat_axis=0, tiled=True)  106 us
    pallas_call x2, Pallas kernels, pair_rotation(): pl.pallas_call(rotation_kernel, out_shape=jax.ShapeDtypeStruct((WIDTH, WI...  96.2 us
    ppermute x1, waiting for transfers between devices, local(): lax.ppermute(first, 'col', [(p, p + 1) for p in range(col_count - 1)])  87.9 us
    ppermute x4, waiting for transfers between devices, row_total(): partial_gram = partial_gram + lax.ppermute(partial_gram, 'row', swap)  18.4 us
    pallas_call x1, Pallas kernels, moved_turn(): pl.pallas_call(moved_turn_kernel, grid_spec=pltpu.PrefetchScalarGridSpec(...  11.2 us
    unnamed x8, local copies, waits for them, and re-layouts  10.8 us
    pallas_call x1, Pallas kernels, moved_gram(): pl.pallas_call(moved_gram_kernel, grid_spec=pltpu.PrefetchScalarGridSpec(...  8.65 us
    ppermute x1, starting transfers between devices, local(): lax.ppermute(second, 'col', [(p, p - 1) for p in range(1, col_count)])  7.41 us
  transfers between devices with their start and end apart: 6, of which 6 were waited for; matrix products, arithmetic and copies ran while one was open for 0% of the time, Pallas kernels for 0%

profile of v1, /device:TPU:32, one launch (start us, length us, event | category | flops | bytes accessed | tf_op | source)
XLA Modules:
  0.0 366.9 jit_solution(16569466402395491652)
XLA Ops:
  0.0 3.4 copy-done.2
  3.4 0.7 copy-done.3
  4.0 3.2 order.1
  7.3 105.9 %all_to_all.5 = f32[32,256,256]{2,1,0:T(8,128)S(1)} all-to-all(f32[32,256,256]{2,1,0:T(8,128)S(1)} %order.1), channel_id=1, replica_groups=mesh['col'=32,'row'=4] {'col'}, dimensions={0} | all-to-all | bytes 16777216 | tf_op jit(solution)/shard_map/all_to_all | solution.py:260
  113.1 4.0 %gram.1 = f32[256,256]{1,0:T(8,128)S(1)} custom-call(f32[8192,256]{1,0:T(8,128)S(1)} %bitcast.6), custom_call_target="tpu_custom_call" | custom-call | tf_op jit(solution)/shard_map/gram/pallas_call | solution.py:83
  117.1 3.4 copy-done
  120.5 1.5 collective-permute-done
  122.1 0.8 collective-permute-start.1
  122.8 7.7 %collective-permute-done.1 = f32[256,256]{1,0:T(8,128)S(1)} collective-permute-done((f32[256,256]{1,0:T(8,128)S(1)}, f32[256,256]{1,0:T(8,128)S(1)}, u32[]{:S(2)}, u32[]{:S(2)}) %collective-permute-start.1) | collective-permute-done | bytes 262176 | tf_op jit(solution)/shard_map/ppermute | solution.py:146
  130.5 48.1 %rotation.2 = f32[256,256]{1,0:T(8,128)S(1)} custom-call(f32[256,256]{1,0:T(8,128)S(1)} %add.13.gram_ref), custom_call_target="tpu_custom_call" | custom-call | tf_op jit(solution)/shard_map/rotation/pallas_call | solution.py:193
  178.7 3.4 copy-done.1
  182.1 7.1 %turn.1 = (f32[8192,128]{1,0:T(8,128)}, f32[8192,128]{1,0:T(8,128)}) custom-call(f32[8192,256]{1,0:T(8,128)S(1)} %bitcast.7, f32[256,256]{1,0:T(8,128)S(1)} %maximum_select_fusion.rotation_ref), custom_call_target="tpu_custom_call" | custom-call | tf_op jit(solution)/shard_map/turn/pallas_call | solution.py:219
  189.2 3.1 collective-permute-start.2
  192.3 7.4 %collective-permute-start.3 = (f32[8192,128]{1,0:T(8,128)}, f32[8192,128]{1,0:T(8,128)}, u32[]{:S(2)}, u32[]{:S(2)}) collective-permute-start(f32[8192,128]{1,0:T(8,128)} %get-tuple-element.8.second_ref), channel_id=1, source_target_pairs={{4,0},{8,4},{12,8},{16,12},{20,16},{24,20},{28,24},{32,28},{36,32}... | collective-permute-start | bytes 12582920 | tf_op jit(solution)/shard_map/ppermute | solution.py:266
  199.7 0.1 add_convert_fusion.ends
  199.8 87.9 %collective-permute-done.2.below_ref = f32[8192,128]{1,0:T(8,128)} collective-permute-done((f32[8192,128]{1,0:T(8,128)}, f32[8192,128]{1,0:T(8,128)}, u32[]{:S(2)}, u32[]{:S(2)}) %collective-permute-start.2) | collective-permute-done | bytes 4194336 | tf_op jit(solution)/shard_map/ppermute | solution.py:267
  287.7 1.2 collective-permute-done.3.above_ref
  288.8 8.6 %moved_gram.1 = f32[256,256]{1,0:T(8,128)S(1)} custom-call(s32[2]{0:T(128)S(1)} %add_convert_fusion.ends, f32[8192,128]{1,0:T(8,128)} %collective-permute-done.2.below_ref, f32[8192,128]{1,0:T(8,128)} %get-tuple-element.8.second_ref, f32[8192,128]{1,0:T(8,128)} %collective-permute-done.3.above_ref, f32[8192,128]{1,0:T(8,128)} %get-tuple-element.7.first_ref), custom_call_target="tpu_custom_call" | custom-call | tf_op jit(solution)/shard_map/moved_gram/pallas_call | solution.py:126
  297.5 0.1 collective-permute-start.4
  297.6 1.5 collective-permute-done.4
  299.2 0.8 collective-permute-start.5
  299.9 7.7 %collective-permute-done.5 = f32[256,256]{1,0:T(8,128)S(1)} collective-permute-done((f32[256,256]{1,0:T(8,128)S(1)}, f32[256,256]{1,0:T(8,128)S(1)}, u32[]{:S(2)}, u32[]{:S(2)}) %collective-permute-start.5) | collective-permute-done | bytes 262176 | tf_op jit(solution)/shard_map/ppermute | solution.py:146
  307.6 48.1 %rotation.3.rotation_ref = f32[256,256]{1,0:T(8,128)S(1)} custom-call(f32[256,256]{1,0:T(8,128)S(1)} %add.15.gram_ref), custom_call_target="tpu_custom_call" | custom-call | tf_op jit(solution)/shard_map/rotation/pallas_call | solution.py:193
  355.7 11.2 %moved_turn.1 = f32[8192,256]{1,0:T(8,128)} custom-call(s32[2]{0:T(128)S(1)} %add_convert_fusion.ends, f32[8192,128]{1,0:T(8,128)} %collective-permute-done.2.below_ref, f32[8192,128]{1,0:T(8,128)} %get-tuple-element.8.second_ref, f32[8192,128]{1,0:T(8,128)} %collective-permute-done.3.above_ref, f32[8192,128]{1,0:T(8,128)} %get-tuple-element.7.first_ref, ...), custom_call_target="tpu_custom_call" | custom-call | tf_op jit(solution)/shard_map/moved_turn/pallas_call | solution.py:240
  (11 shorter events, 0.2 us)
Async XLA Ops:
  0.0 3.4 copy-start.2
  3.4 0.7 copy-start.3
  117.1 3.4 copy-start
  120.5 1.5 collective-permute-start
  122.1 8.4 %collective-permute-start.1 = (f32[256,256]{1,0:T(8,128)S(1)}, f32[256,256]{1,0:T(8,128)S(1)}, u32[]{:S(2)}, u32[]{:S(2)}) collective-permute-start(f32[256,256]{1,0:T(8,128)S(1)} %add.12), channel_id=1, source_target_pairs={{0,2},{1,3},{2,0},{3,1},{4,6},{5,7},{6,4},{7,5},{8,10},{9,11},{10,... | collective-permute-start | bytes 786440 | tf_op jit(solution)/shard_map/ppermute | solution.py:146
  178.7 3.4 copy-start.1
  189.2 98.5 %collective-permute-start.2 = (f32[8192,128]{1,0:T(8,128)}, f32[8192,128]{1,0:T(8,128)}, u32[]{:S(2)}, u32[]{:S(2)}) collective-permute-start(f32[8192,128]{1,0:T(8,128)} %get-tuple-element.7.first_ref), channel_id=1, source_target_pairs={{0,4},{4,8},{8,12},{12,16},{16,20},{20,24},{24,28},{28,32},{32,36}... | collective-permute-start | bytes 12582920 | tf_op jit(solution)/shard_map/ppermute | solution.py:267
  192.3 96.6 %collective-permute-start.3 = (f32[8192,128]{1,0:T(8,128)}, f32[8192,128]{1,0:T(8,128)}, u32[]{:S(2)}, u32[]{:S(2)}) collective-permute-start(f32[8192,128]{1,0:T(8,128)} %get-tuple-element.8.second_ref), channel_id=1, source_target_pairs={{4,0},{8,4},{12,8},{16,12},{20,16},{24,20},{28,24},{32,28},{36,32}... | collective-permute-start | bytes 12582920 | tf_op jit(solution)/shard_map/ppermute | solution.py:266
  297.5 1.6 collective-permute-start.4
  299.2 8.4 %collective-permute-start.5 = (f32[256,256]{1,0:T(8,128)S(1)}, f32[256,256]{1,0:T(8,128)S(1)}, u32[]{:S(2)}, u32[]{:S(2)}) collective-permute-start(f32[256,256]{1,0:T(8,128)S(1)} %add.14), channel_id=1, source_target_pairs={{0,2},{1,3},{2,0},{3,1},{4,6},{5,7},{6,4},{7,5},{8,10},{9,11},{10,... | collective-permute-start | bytes 786440 | tf_op jit(solution)/shard_map/ppermute | solution.py:146

commit v2 on v1

--- a/solution.py
+++ b/solution.py
@@ -11,6 +11,7 @@
 WIDTH = 2 * BLOCK
 TILE = 1024
 PANEL = 32
+SUB = 8
 HIGHEST = lax.Precision.HIGHEST
 COLUMNS = (((0,), (0,)), ((), ()))
 LANES = (((1,), (1,)), ((), ()))
@@ -34,29 +35,38 @@
     return high, middle, (rest - middle.astype(F32)).astype(BF16)
 
 
-def order_kernel(pairing_ref, first_ref, second_ref, out_ref):
-    out_ref[0, :, :BLOCK] = first_ref[...]
-    out_ref[0, :, BLOCK:] = second_ref[...]
+def order_kernel(pairing_ref, diffs_ref, out_ref, sems):
+    count = pairing_ref.shape[0]
+
+    def copy(block):
+        column = pl.multiple_of(pairing_ref[block] * BLOCK, BLOCK)
+        half = pl.ds((block % 2) * BLOCK, BLOCK)
+        return pltpu.make_async_copy(
+            diffs_ref.at[:, pl.ds(column, BLOCK)],
+            out_ref.at[block // 2, :, half],
+            sems.at[block],
+        )
+
+    for block in range(count):
+        copy(block).start()
+    for block in range(count):
+        copy(block).wait()
 
 
 def order_pairs(diffs, pairing):
     rows, columns = diffs.shape
-    count = columns // WIDTH
     return pl.pallas_call(
         order_kernel,
-        grid_spec=pltpu.PrefetchScalarGridSpec(
-            num_scalar_prefetch=1,
-            grid=(count,),
-            in_specs=[
-                pl.BlockSpec((rows, BLOCK), lambda p, pairing: (0, pairing[2 * p])),
-                pl.BlockSpec((rows, BLOCK), lambda p, pairing: (0, pairing[2 * p + 1])),
-            ],
-            out_specs=pl.BlockSpec((1, rows, WIDTH), lambda p, pairing: (p, 0, 0)),
-        ),
-        out_shape=jax.ShapeDtypeStruct((count, rows, WIDTH), F32),
-        compiler_params=grant(16),
+        in_specs=[
+            pl.BlockSpec(memory_space=pltpu.SMEM),
+            pl.BlockSpec(memory_space=pltpu.HBM),
+        ],
+        out_specs=pl.BlockSpec(memory_space=pl.ANY),
+        out_shape=jax.ShapeDtypeStruct((columns // WIDTH, rows, WIDTH), F32),
+        scratch_shapes=[pltpu.SemaphoreType.DMA((columns // BLOCK,))],
+        compiler_params=grant(2),
         name="order",
-    )(pairing, diffs, diffs)
+    )(pairing, diffs)
 
 
 def add_gram(tile, total_ref, cross_ref):
@@ -87,7 +97,7 @@
         out_specs=pl.BlockSpec((WIDTH, WIDTH), lambda i: (0, 0)),
         out_shape=jax.ShapeDtypeStruct((WIDTH, WIDTH), F32),
         scratch_shapes=[pltpu.VMEM((WIDTH, WIDTH), F32)],
-        compiler_params=grant(16),
+        compiler_params=grant(8),
         name="gram",
     )(pair_rows)
 
@@ -133,7 +143,7 @@
             scratch_shapes=[pltpu.VMEM((WIDTH, WIDTH), F32)],
         ),
         out_shape=jax.ShapeDtypeStruct((WIDTH, WIDTH), F32),
-        compiler_params=grant(24),
+        compiler_params=grant(12),
         name="moved_gram",
     )(ends, *moved)
 
@@ -156,45 +166,120 @@
     return lax.dot_general(left, right, COLUMNS, preferred_element_type=F32)
 
 
-def eliminate(work_ref, factor_ref, width):
+def spread(value):
+    return jnp.broadcast_to(value, (SUB, BLOCK))
+
+
+def total(terms):
+    while len(terms) > 1:
+        paired = [a + b for a, b in zip(terms[::2], terms[1::2])]
+        terms = paired + terms[len(terms) - len(terms) % 2 :]
+    return terms[0]
+
+
+def small_inverse(tile, lane, spread_ref, base):
+    for j in range(SUB):
+        spread_ref[base + SUB * j : base + SUB * (j + 1), :] = spread(tile[:, lane + j : lane + j + 1])
+    entry = {
+        (i, j): spread_ref[pl.ds(base + SUB * j + i, SUB, stride=0), :]
+        for j in range(SUB)
+        for i in range(j, SUB)
+    }
+    lower, scales = {}, []
+    for j in range(SUB):
+        scale = lax.rsqrt(entry[j, j])
+        inverse = scale * scale
+        scales.append(scale)
+        for i in range(j + 1, SUB):
+            lower[i, j] = entry[i, j] * inverse
+        for m in range(j + 1, SUB):
+            for i in range(m, SUB):
+                entry[i, m] = entry[i, m] - lower[i, j] * entry[m, j]
+    solved = {}
+    for j in range(SUB):
+        for i in range(j + 1, SUB):
+            terms = [lower[i, j]] + [lower[i, m] * solved[m, j] for m in range(j + 1, i)]
+            solved[i, j] = -total(terms)
+    solved = {at: value * scales[at[0]] for at, value in solved.items()}
+    return solved | {(j, j): scales[j] for j in range(SUB)}
+
+
+def tiles_of(ref, start, end, first, last):
+    return jnp.concatenate([ref[t, start:end, :] for t in range(first, last)], axis=1)
+
+
+def put_tiles(ref, first, value):
+    for t in range(value.shape[1] // BLOCK):
+        ref[first + t] = value[:, BLOCK * t : BLOCK * (t + 1)]
+
+
+def eliminate(work_ref, factor_ref, spread_ref, tiles):
+    row = lax.broadcasted_iota(jnp.int32, (SUB, BLOCK), 0)
+    lane = lax.broadcasted_iota(jnp.int32, (SUB, BLOCK), 1)
+    zero = jnp.zeros((SUB, BLOCK), F32)
     for start in range(0, WIDTH, PANEL):
         end = start + PANEL
-        rows = work_ref[start:end, :width]
-        row_id = lax.broadcasted_iota(jnp.int32, (PANEL, 1), 0)
-        pivots = jnp.zeros((PANEL, 1), F32)
-        for j in range(PANEL):
-            column = rows[:, start + j : start + j + 1]
-            pivot = column[j : j + 1, :]
-            multiple = jnp.where(row_id > j, column / pivot, 0.0)
-            pivots = jnp.where(row_id == j, pivot, pivots)
-            rows = rows - multiple * rows[j : j + 1, :]
-        rows = rows * lax.rsqrt(pivots)
-        row_at = lax.broadcasted_iota(jnp.int32, (PANEL, width), 0) + start
-        rows = jnp.where(lax.broadcasted_iota(jnp.int32, (PANEL, width), 1) >= row_at, rows, 0.0)
-        factor_ref[start:end, :width] = rows
+        own = start // BLOCK
+        for top in range(start, end, SUB):
+            at = top % BLOCK
+            base = SUB * SUB * (top // SUB % 2)
+            small = small_inverse(work_ref[own, top : top + SUB, :], at, spread_ref, base)
+            columns = []
+            for j in range(SUB):
+                column = zero
+                for i in range(j, SUB):
+                    column = jnp.where(row == i, small[i, j], column)
+                columns.append(column)
+            for t in range(tiles):
+                if t < own:
+                    solved = zero
+                else:
+                    solved = total(
+                        [columns[j] * work_ref[t, pl.ds(top + j, SUB, stride=0), :] for j in range(SUB)]
+                    )
+                    if t == own:
+                        solved = jnp.where(lane >= row + at, solved, 0.0)
+                factor_ref[t, top : top + SUB, :] = solved
+            for below in range(top + SUB, end, SUB):
+                tile = work_ref[own, below : below + SUB, :]
+                entries = [spread(tile[:, at + j : at + j + 1]) for j in range(SUB)]
+                left = [total([entries[j] * small[i, j] for j in range(i + 1)]) for i in range(SUB)]
+                for t in range(own, tiles):
+                    work_ref[t, below : below + SUB, :] -= total(
+                        [left[i] * factor_ref[t, pl.ds(top + i, SUB, stride=0), :] for i in range(SUB)]
+                    )
         if end < WIDTH:
-            work_ref[end:, :width] -= outer_product(rows[:, end:WIDTH], rows)
-
-
-def rotation_kernel(gram_ref, out_ref, work_ref, factor_ref):
+            first = end // BLOCK
+            update = outer_product(
+                tiles_of(factor_ref, start, end, first, WIDTH // BLOCK),
+                tiles_of(factor_ref, start, end, first, tiles),
+            )
+            for t in range(first, tiles):
+                here = BLOCK * (t - first)
+                work_ref[t, end:, :] -= update[end - BLOCK * first :, here : here + BLOCK]
+
+
+def rotation_kernel(gram_ref, out_ref, work_ref, factor_ref, spread_ref):
     gram = gram_ref[...]
-    work_ref[:, :WIDTH] = jnp.dot(gram, gram, precision=HIGHEST, preferred_element_type=F32)
-    eliminate(work_ref, factor_ref, WIDTH)
-    factor = factor_ref[:, :WIDTH]
-    work_ref[:, :WIDTH] = lax.dot_general(
-        factor, factor, LANES, precision=HIGHEST, preferred_element_type=F32
-    )
-    work_ref[:, WIDTH:] = factor
-    eliminate(work_ref, factor_ref, 2 * WIDTH)
-    out_ref[...] = factor_ref[:, WIDTH:]
+    square = jnp.dot(gram, gram, precision=HIGHEST, preferred_element_type=F32)
+    put_tiles(work_ref, 0, square)
+    eliminate(work_ref, factor_ref, spread_ref, WIDTH // BLOCK)
+    factor = tiles_of(factor_ref, 0, WIDTH, 0, WIDTH // BLOCK)
+    square = lax.dot_general(factor, factor, LANES, precision=HIGHEST, preferred_element_type=F32)
+    put_tiles(work_ref, 0, square)
+    put_tiles(work_ref, WIDTH // BLOCK, factor)
+    eliminate(work_ref, factor_ref, spread_ref, 2 * WIDTH // BLOCK)
+    out_ref[...] = tiles_of(factor_ref, 0, WIDTH, WIDTH // BLOCK, 2 * WIDTH // BLOCK)
 
 
 def pair_rotation(pair_gram):
+    tiles = pltpu.VMEM((2 * WIDTH // BLOCK, WIDTH, BLOCK), F32)
     return pl.pallas_call(
         rotation_kernel,
         out_shape=jax.ShapeDtypeStruct((WIDTH, WIDTH), F32),
-        scratch_shapes=[pltpu.VMEM((WIDTH, 2 * WIDTH), F32)] * 2,
-        compiler_params=grant(32),
+        scratch_shapes=[tiles, tiles, pltpu.VMEM((2 * SUB * SUB, BLOCK), F32)],
+        compiler_params=grant(8),
+        cost_estimate=pl.CostEstimate(flops=20_000_000_000, bytes_accessed=1 << 19, transcendentals=0),
         name="rotation",
     )(pair_gram)
 
@@ -225,7 +310,7 @@
         ],
         out_specs=[half, half],
         out_shape=[jax.ShapeDtypeStruct((rows, BLOCK), F32)] * 2,
-        compiler_params=grant(24),
+        compiler_params=grant(12),
         name="turn",
     )(pair_rows, rotation_t)
 
@@ -246,7 +331,7 @@
             out_specs=pl.BlockSpec((TILE, WIDTH), lambda i, ends: (i, 0)),
         ),
         out_shape=jax.ShapeDtypeStruct((rows, WIDTH), F32),
-        compiler_params=grant(24),
+        compiler_params=grant(12),
         name="moved_turn",
     )(ends, *moved, rotation_t)
 

time: 370 us -> 301 us (0.81)
  Pallas kernels: 130 us -> 64.4 us
    pallas_call x2, Pallas kernels: 96.2 us -> 30.8 us  [pair_rotation(): pl.pallas_call(rotation_kernel, out_shape=jax.ShapeDtypeStruct((WIDTH, WI...]
    unnamed x8 -> x10, local copies, waits for them, and re-layouts: 10.8 us -> 7.44 us
where the time goes in v2:
time: 301 us; the launch traced here: 298 us
  waiting for transfers between devices  108 us (36%)
  blocking collectives  106 us (35%)
  Pallas kernels  64.4 us (21%)
  starting transfers between devices  12.3 us (4%)
  local copies, waits for them, and re-layouts  7.46 us (2%)
    all_to_all x1, blocking collectives, local(): lax.all_to_all(ordered, 'col', split_axis=0, concat_axis=0, tiled=True)  106 us
    ppermute x1, waiting for transfers between devices, local(): lax.ppermute(first, 'col', [(p, p + 1) for p in range(col_count - 1)])  88 us
    pallas_call x2, Pallas kernels, pair_rotation(): pl.pallas_call(rotation_kernel, out_shape=jax.ShapeDtypeStruct((WIDTH, WI...  30.8 us
    ppermute x4, waiting for transfers between devices, row_total(): partial_gram = partial_gram + lax.ppermute(partial_gram, 'row', swap)  18.4 us
    pallas_call x1, Pallas kernels, moved_turn(): pl.pallas_call(moved_turn_kernel, grid_spec=pltpu.PrefetchScalarGridSpec(...  11.2 us
    pallas_call x1, Pallas kernels, moved_gram(): pl.pallas_call(moved_gram_kernel, grid_spec=pltpu.PrefetchScalarGridSpec(...  8.65 us
    unnamed x10, local copies, waits for them, and re-layouts  7.44 us
    ppermute x1, starting transfers between devices, local(): lax.ppermute(second, 'col', [(p, p - 1) for p in range(1, col_count)])  7.23 us
  transfers between devices with their start and end apart: 6, of which 6 were waited for; matrix products, arithmetic and copies ran while one was open for 0% of the time, Pallas kernels for 0%

profile of v2, /device:TPU:32, one launch (start us, length us, event | category | flops | bytes accessed | tf_op | source)
XLA Modules:
  0.0 298.1 jit_solution(7004221311449552884)
XLA Ops:
  0.0 3.4 %copy-done.1 = f32[256,8192]{1,0:T(8,128)S(1)} copy-done((f32[256,8192]{1,0:T(8,128)S(1)}, f32[256,8192]{1,0:T(8,128)}, u32[]{:S(2)}) %copy-start.1) | copy-done | bytes 8388632
  3.4 0.7 copy-done.2
  4.0 2.7 order.1
  6.7 105.9 %all_to_all.5 = f32[32,256,256]{2,1,0:T(8,128)S(1)} all-to-all(f32[32,256,256]{2,1,0:T(8,128)S(1)} %order.1), channel_id=1, replica_groups=mesh['col'=32,'row'=4] {'col'}, dimensions={0} | all-to-all | bytes 16777216 | tf_op jit(solution)/shard_map/all_to_all | solution.py:345
  112.6 4.0 %gram.1 = f32[256,256]{1,0:T(8,128)S(1)} custom-call(f32[8192,256]{1,0:T(8,128)S(1)} %bitcast.6), custom_call_target="tpu_custom_call" | custom-call | tf_op jit(solution)/shard_map/gram/pallas_call | solution.py:93
  116.6 3.4 %copy-done = f32[32,256,256]{2,1,0:T(8,128)} copy-done((f32[32,256,256]{2,1,0:T(8,128)}, f32[32,256,256]{2,1,0:T(8,128)S(1)}, u32[]{:S(2)}) %copy-start) | copy-done | bytes 8388632
  120.0 1.5 collective-permute-done
  121.6 0.9 collective-permute-start.1
  122.5 7.7 %collective-permute-done.1 = f32[256,256]{1,0:T(8,128)S(1)} collective-permute-done((f32[256,256]{1,0:T(8,128)S(1)}, f32[256,256]{1,0:T(8,128)S(1)}, u32[]{:S(2)}, u32[]{:S(2)}) %collective-permute-start.1) | collective-permute-done | bytes 262176 | tf_op jit(solution)/shard_map/ppermute | solution.py:156
  130.2 0.0 slice-start.1
  130.2 15.4 %rotation.2 = f32[256,256]{1,0:T(8,128)S(1)} custom-call(f32[256,256]{1,0:T(8,128)S(1)} %add.13.gram_ref), custom_call_target="tpu_custom_call" | custom-call | flops 20000000000 | bytes 524288 | tf_op jit(solution)/shard_map/rotation/pallas_call | solution.py:277
  145.7 7.1 %turn.1 = (f32[8192,128]{1,0:T(8,128)}, f32[8192,128]{1,0:T(8,128)}) custom-call(f32[8192,256]{1,0:T(8,128)S(1)} %bitcast.9, f32[256,256]{1,0:T(8,128)S(1)} %maximum_select_fusion.rotation_ref), custom_call_target="tpu_custom_call" | custom-call | tf_op jit(solution)/shard_map/turn/pallas_call | solution.py:304
  152.8 3.1 %collective-permute-start.2 = (f32[8192,128]{1,0:T(8,128)}, f32[8192,128]{1,0:T(8,128)}, u32[]{:S(2)}, u32[]{:S(2)}) collective-permute-start(f32[8192,128]{1,0:T(8,128)} %get-tuple-element.7.first_ref), channel_id=1, source_target_pairs={{0,4},{4,8},{8,12},{12,16},{16,20},{20,24},{24,28},{28,32},{32,36}... | collective-permute-start | bytes 12582920 | tf_op jit(solution)/shard_map/ppermute | solution.py:352
  155.9 7.2 %collective-permute-start.3 = (f32[8192,128]{1,0:T(8,128)}, f32[8192,128]{1,0:T(8,128)}, u32[]{:S(2)}, u32[]{:S(2)}) collective-permute-start(f32[8192,128]{1,0:T(8,128)} %get-tuple-element.8.second_ref), channel_id=1, source_target_pairs={{4,0},{8,4},{12,8},{16,12},{20,16},{24,20},{28,24},{32,28},{36,32}... | collective-permute-start | bytes 12582920 | tf_op jit(solution)/shard_map/ppermute | solution.py:351
  163.2 0.1 add_convert_fusion.ends
  163.3 88.0 %collective-permute-done.2.below_ref = f32[8192,128]{1,0:T(8,128)} collective-permute-done((f32[8192,128]{1,0:T(8,128)}, f32[8192,128]{1,0:T(8,128)}, u32[]{:S(2)}, u32[]{:S(2)}) %collective-permute-start.2) | collective-permute-done | bytes 4194336 | tf_op jit(solution)/shard_map/ppermute | solution.py:352
  251.3 1.2 collective-permute-done.3.above_ref
  252.5 8.7 %moved_gram.1 = f32[256,256]{1,0:T(8,128)S(1)} custom-call(s32[2]{0:T(128)S(1)} %add_convert_fusion.ends, f32[8192,128]{1,0:T(8,128)} %collective-permute-done.2.below_ref, f32[8192,128]{1,0:T(8,128)} %get-tuple-element.8.second_ref, f32[8192,128]{1,0:T(8,128)} %collective-permute-done.3.above_ref, f32[8192,128]{1,0:T(8,128)} %get-tuple-element.7.first_ref), custom_call_target="tpu_custom_call" | custom-call | tf_op jit(solution)/shard_map/moved_gram/pallas_call | solution.py:136
  261.1 0.1 collective-permute-start.4
  261.2 1.5 collective-permute-done.4
  262.8 1.0 collective-permute-start.5
  263.8 7.7 %collective-permute-done.5 = f32[256,256]{1,0:T(8,128)S(1)} collective-permute-done((f32[256,256]{1,0:T(8,128)S(1)}, f32[256,256]{1,0:T(8,128)S(1)}, u32[]{:S(2)}, u32[]{:S(2)}) %collective-permute-start.5) | collective-permute-done | bytes 262176 | tf_op jit(solution)/shard_map/ppermute | solution.py:156
  271.5 15.4 %rotation.3.rotation_ref = f32[256,256]{1,0:T(8,128)S(1)} custom-call(f32[256,256]{1,0:T(8,128)S(1)} %add.15.gram_ref), custom_call_target="tpu_custom_call" | custom-call | flops 20000000000 | bytes 524288 | tf_op jit(solution)/shard_map/rotation/pallas_call | solution.py:277
  286.9 11.2 %moved_turn.1 = f32[8192,256]{1,0:T(8,128)} custom-call(s32[2]{0:T(128)S(1)} %add_convert_fusion.ends, f32[8192,128]{1,0:T(8,128)} %collective-permute-done.2.below_ref, f32[8192,128]{1,0:T(8,128)} %get-tuple-element.8.second_ref, f32[8192,128]{1,0:T(8,128)} %collective-permute-done.3.above_ref, f32[8192,128]{1,0:T(8,128)} %get-tuple-element.7.first_ref, ...), custom_call_target="tpu_custom_call" | custom-call | tf_op jit(solution)/shard_map/moved_turn/pallas_call | solution.py:325
  (14 shorter events, 0.2 us)
Async XLA Ops:
  0.0 3.4 %copy-start.1 = (f32[256,8192]{1,0:T(8,128)S(1)}, f32[256,8192]{1,0:T(8,128)}, u32[]{:S(2)}) copy-start(f32[256,8192]{1,0:T(8,128)} %diffs_ref.1) | copy-start | bytes 25165828
  3.4 0.7 copy-start.2
  116.6 3.4 %copy-start = (f32[32,256,256]{2,1,0:T(8,128)}, f32[32,256,256]{2,1,0:T(8,128)S(1)}, u32[]{:S(2)}) copy-start(f32[32,256,256]{2,1,0:T(8,128)S(1)} %all_to_all.5) | copy-start | bytes 25165828
  120.0 1.5 collective-permute-start
  121.6 8.6 %collective-permute-start.1 = (f32[256,256]{1,0:T(8,128)S(1)}, f32[256,256]{1,0:T(8,128)S(1)}, u32[]{:S(2)}, u32[]{:S(2)}) collective-permute-start(f32[256,256]{1,0:T(8,128)S(1)} %add.12), channel_id=1, source_target_pairs={{0,2},{1,3},{2,0},{3,1},{4,6},{5,7},{6,4},{7,5},{8,10},{9,11},{10,... | collective-permute-start | bytes 786440 | tf_op jit(solution)/shard_map/ppermute | solution.py:156
  130.2 15.5 %slice-start = ((s8[8388608]{0:T(1024)(128)(4,1)}), s8[4194304]{0:T(1024)(128)(4,1)S(1)}, s32[]{:S(2)}) async-start(s8[8388608]{0:T(1024)(128)(4,1)} %bitcast.7), calls=%async_computation.1 | async-start | bytes 8388608
  130.2 15.5 %slice-start.1 = ((s8[8388608]{0:T(1024)(128)(4,1)}), s8[4194304]{0:T(1024)(128)(4,1)S(1)}, s32[]{:S(2)}) async-start(s8[8388608]{0:T(1024)(128)(4,1)} %bitcast.7), calls=%async_computation.2 | async-start | bytes 8388608
  152.8 98.5 %collective-permute-start.2 = (f32[8192,128]{1,0:T(8,128)}, f32[8192,128]{1,0:T(8,128)}, u32[]{:S(2)}, u32[]{:S(2)}) collective-permute-start(f32[8192,128]{1,0:T(8,128)} %get-tuple-element.7.first_ref), channel_id=1, source_target_pairs={{0,4},{4,8},{8,12},{12,16},{16,20},{20,24},{24,28},{28,32},{32,36}... | collective-permute-start | bytes 12582920 | tf_op jit(solution)/shard_map/ppermute | solution.py:352
  155.9 96.6 %collective-permute-start.3 = (f32[8192,128]{1,0:T(8,128)}, f32[8192,128]{1,0:T(8,128)}, u32[]{:S(2)}, u32[]{:S(2)}) collective-permute-start(f32[8192,128]{1,0:T(8,128)} %get-tuple-element.8.second_ref), channel_id=1, source_target_pairs={{4,0},{8,4},{12,8},{16,12},{20,16},{24,20},{28,24},{32,28},{36,32}... | collective-permute-start | bytes 12582920 | tf_op jit(solution)/shard_map/ppermute | solution.py:351
  261.1 1.6 collective-permute-start.4
  262.8 8.6 %collective-permute-start.5 = (f32[256,256]{1,0:T(8,128)S(1)}, f32[256,256]{1,0:T(8,128)S(1)}, u32[]{:S(2)}, u32[]{:S(2)}) collective-permute-start(f32[256,256]{1,0:T(8,128)S(1)} %add.14), channel_id=1, source_target_pairs={{0,2},{1,3},{2,0},{3,1},{4,6},{5,7},{6,4},{7,5},{8,10},{9,11},{10,... | collective-permute-start | bytes 786440 | tf_op jit(solution)/shard_map/ppermute | solution.py:156

commit v3 on v2

--- a/solution.py
+++ b/solution.py
@@ -9,7 +9,9 @@
 
 BLOCK = 128
 WIDTH = 2 * BLOCK
-TILE = 1024
+TILE = 512
+RAW = 2 * TILE
+MAIN = 10 * TILE
 PANEL = 32
 SUB = 8
 HIGHEST = lax.Precision.HIGHEST
@@ -21,6 +23,10 @@
 
 def grant(megabytes):
     return pltpu.CompilerParams(vmem_limit_bytes=megabytes << 20)
+
+
+def in_hbm(value):
+    return pltpu.with_memory_space_constraint(value, pltpu.HBM)
 
 
 def two_terms(value):
@@ -59,7 +65,7 @@
         order_kernel,
         in_specs=[
             pl.BlockSpec(memory_space=pltpu.SMEM),
-            pl.BlockSpec(memory_space=pltpu.HBM),
+            pl.BlockSpec(memory_space=pl.ANY),
         ],
         out_specs=pl.BlockSpec(memory_space=pl.ANY),
         out_shape=jax.ShapeDtypeStruct((columns // WIDTH, rows, WIDTH), F32),
@@ -75,87 +81,139 @@
     cross_ref[...] += lax.dot_general(high, low, COLUMNS, preferred_element_type=F32)
 
 
-def gram_kernel(tile_ref, total_ref, cross_ref):
-    @pl.when(pl.program_id(0) == 0)
-    def _():
-        total_ref[...] = jnp.zeros_like(total_ref)
-        cross_ref[...] = jnp.zeros_like(cross_ref)
-
-    add_gram(tile_ref[...], total_ref, cross_ref)
-
-    @pl.when(pl.program_id(0) == pl.num_programs(0) - 1)
-    def _():
-        total_ref[...] += cross_ref[...] + cross_ref[...].T
+def row_copy(source_ref, rows_ref, sems, tile, first=0):
+    source = source_ref.at[pl.ds(pl.multiple_of((tile + first) * TILE, TILE), TILE), :]
+    rows = rows_ref.at[pl.ds(pl.multiple_of(tile * TILE, TILE), TILE), :]
+    return pltpu.make_async_copy(source, rows, sems.at[tile])
+
+
+def pack(total_ref, cross_ref):
+    gram = total_ref[...] + (cross_ref[...] + cross_ref[...].T)
+    return jnp.concatenate([gram[:BLOCK, :BLOCK], gram[:BLOCK, BLOCK:], gram[BLOCK:, BLOCK:]])
+
+
+def unpack(packed):
+    corner, side, end = packed[:BLOCK], packed[BLOCK : 2 * BLOCK], packed[2 * BLOCK :]
+    upper = jnp.concatenate([corner, side], axis=1)
+    return jnp.concatenate([upper, jnp.concatenate([side.T, end], axis=1)])
+
+
+def gram_kernel(source_ref, out_ref, total_ref, cross_ref, rows_ref, sems):
+    tiles = rows_ref.shape[0] // TILE
+    for tile in range(tiles):
+        row_copy(source_ref, rows_ref, sems, tile).start()
+    total_ref[...] = jnp.zeros_like(total_ref)
+    cross_ref[...] = jnp.zeros_like(cross_ref)
+
+    @pl.loop(0, tiles)
+    def _(tile):
+        row_copy(source_ref, rows_ref, sems, tile).wait()
+        rows = rows_ref[pl.ds(pl.multiple_of(tile * TILE, TILE), TILE), :]
+        add_gram(rows, total_ref, cross_ref)
+
+    out_ref[...] = pack(total_ref, cross_ref)
 
 
 def local_gram(pair_rows):
     rows = pair_rows.shape[0]
+    whole = pl.BlockSpec(memory_space=pltpu.VMEM)
     return pl.pallas_call(
         gram_kernel,
-        grid=(rows // TILE,),
-        in_specs=[pl.BlockSpec((TILE, WIDTH), lambda i: (i, 0))],
-        out_specs=pl.BlockSpec((WIDTH, WIDTH), lambda i: (0, 0)),
-        out_shape=jax.ShapeDtypeStruct((WIDTH, WIDTH), F32),
-        scratch_shapes=[pltpu.VMEM((WIDTH, WIDTH), F32)],
-        compiler_params=grant(8),
+        in_specs=[pl.BlockSpec(memory_space=pltpu.HBM)],
+        out_specs=whole,
+        out_shape=jax.ShapeDtypeStruct((3 * BLOCK, BLOCK), F32),
+        scratch_shapes=[
+            pltpu.VMEM((WIDTH, WIDTH), F32),
+            pltpu.VMEM((WIDTH, WIDTH), F32),
+            pltpu.VMEM((rows, WIDTH), F32),
+            pltpu.SemaphoreType.DMA((rows // TILE,)),
+        ],
+        compiler_params=grant(14),
+        cost_estimate=pl.CostEstimate(flops=1000, bytes_accessed=1000, transcendentals=0),
         name="gram",
-    )(pair_rows)
-
-
-def moved_tile(ends, from_below, kept_second, from_above, kept_first):
-    upper = jnp.where(ends[0] == 1, kept_second, from_below)
-    lower = jnp.where(ends[1] == 1, kept_first, from_above)
-    return jnp.concatenate([upper, lower], axis=1)
-
-
-def moved_gram_kernel(ends, below_ref, second_ref, above_ref, first_ref, total_ref, cross_ref):
-    @pl.when(pl.program_id(0) == 0)
-    def _():
-        total_ref[...] = jnp.zeros_like(total_ref)
-        cross_ref[...] = jnp.zeros_like(cross_ref)
-
-    tile = moved_tile(ends, below_ref[...], second_ref[...], above_ref[...], first_ref[...])
-    add_gram(tile, total_ref, cross_ref)
-
-    @pl.when(pl.program_id(0) == pl.num_programs(0) - 1)
-    def _():
-        total_ref[...] += cross_ref[...] + cross_ref[...].T
-
-
-def moved_specs():
-    return [
-        pl.BlockSpec((TILE, BLOCK), lambda i, ends: (i, 0)),
-        pl.BlockSpec((TILE, BLOCK), lambda i, ends: (i * ends[0], 0)),
-        pl.BlockSpec((TILE, BLOCK), lambda i, ends: (i, 0)),
-        pl.BlockSpec((TILE, BLOCK), lambda i, ends: (i * ends[1], 0)),
-    ]
-
-
-def moved_gram(ends, moved):
+    )(in_hbm(pair_rows))
+
+
+def cost(rows):
+    return pl.CostEstimate(
+        flops=6 * rows * WIDTH * WIDTH, bytes_accessed=8 * rows * WIDTH, transcendentals=0
+    )
+
+
+def half_copies(source_ref, rows_ref, sems, tile, first, column):
+    rows = pl.ds(pl.multiple_of(tile * TILE, TILE), TILE)
+    source = source_ref.at[pl.ds(pl.multiple_of((tile - first) * TILE, TILE), TILE), :]
+    half = pl.ds(column * BLOCK, BLOCK)
+    return pltpu.make_async_copy(source, rows_ref.at[rows, half], sems.at[column, tile])
+
+
+def start_moved(ends, moved_refs, rows_ref, sems, first):
+    below_ref, second_ref, above_ref, first_ref = moved_refs
+    tiles = below_ref.shape[0] // TILE
+    for column, arrived_ref, kept_ref in ((0, below_ref, second_ref), (1, above_ref, first_ref)):
+
+        @pl.when(ends[column] == 1)
+        def _():
+            for tile in range(first, first + tiles):
+                half_copies(kept_ref, rows_ref, sems, tile, first, column).start()
+
+        @pl.when(ends[column] == 0)
+        def _():
+            for tile in range(first, first + tiles):
+                half_copies(arrived_ref, rows_ref, sems, tile, first, column).start()
+
+
+def wait_tile(like_ref, rows_ref, sems, tile):
+    rows = pl.ds(pl.multiple_of(tile * TILE, TILE), TILE)
+    for column in range(2):
+        half = rows_ref.at[rows, pl.ds(column * BLOCK, BLOCK)]
+        pltpu.make_async_copy(like_ref.at[pl.ds(0, TILE), :], half, sems.at[column, tile]).wait()
+    return rows_ref[rows, :]
+
+
+def moved_gram_kernel(ends, before_ref, *refs):
+    moved_refs, (out_ref, total_ref, cross_ref, rows_ref, sems) = refs[:4], refs[4:]
+    start_moved(ends, moved_refs, rows_ref, sems, 0)
+    total_ref[...] = jnp.zeros_like(total_ref)
+    cross_ref[...] = jnp.zeros_like(cross_ref)
+
+    @pl.loop(0, rows_ref.shape[0] // TILE)
+    def _(tile):
+        add_gram(wait_tile(moved_refs[0], rows_ref, sems, tile), total_ref, cross_ref)
+
+    out_ref[...] = before_ref[...] + pack(total_ref, cross_ref)
+
+
+def moved_gram(ends, before, moved):
     rows = moved[0].shape[0]
+    whole = pl.BlockSpec(memory_space=pltpu.VMEM)
     return pl.pallas_call(
         moved_gram_kernel,
-        grid_spec=pltpu.PrefetchScalarGridSpec(
-            num_scalar_prefetch=1,
-            grid=(rows // TILE,),
-            in_specs=moved_specs(),
-            out_specs=pl.BlockSpec((WIDTH, WIDTH), lambda i, ends: (0, 0)),
-            scratch_shapes=[pltpu.VMEM((WIDTH, WIDTH), F32)],
-        ),
-        out_shape=jax.ShapeDtypeStruct((WIDTH, WIDTH), F32),
+        in_specs=[pl.BlockSpec(memory_space=pltpu.SMEM), whole] + [pl.BlockSpec(memory_space=pl.ANY)] * 4,
+        out_specs=whole,
+        out_shape=jax.ShapeDtypeStruct((3 * BLOCK, BLOCK), F32),
+        scratch_shapes=[
+            pltpu.VMEM((WIDTH, WIDTH), F32),
+            pltpu.VMEM((WIDTH, WIDTH), F32),
+            pltpu.VMEM((rows, WIDTH), F32),
+            pltpu.SemaphoreType.DMA((2, rows // TILE)),
+        ],
         compiler_params=grant(12),
+        cost_estimate=cost(rows),
         name="moved_gram",
-    )(ends, *moved)
-
-
-def row_total(partial_gram):
+    )(ends, before, *moved)
+
+
+def row_parts(packed):
     count = lax.axis_size("row")
     step = 1
-    while step < count:
+    while True:
         swap = [(source, source ^ step) for source in range(count)]
-        partial_gram = partial_gram + lax.ppermute(partial_gram, "row", swap)
+        parts = (packed, lax.ppermute(packed, "row", swap))
         step *= 2
-    return partial_gram
+        if step >= count:
+            return parts
+        packed = parts[0] + parts[1]
 
 
 def outer_product(left, right):
@@ -259,8 +317,8 @@
                 work_ref[t, end:, :] -= update[end - BLOCK * first :, here : here + BLOCK]
 
 
-def rotation_kernel(gram_ref, out_ref, work_ref, factor_ref, spread_ref):
-    gram = gram_ref[...]
+def rotation_kernel(swap_ref, one_ref, two_ref, first_ref, second_ref, work_ref, factor_ref, spread_ref):
+    gram = unpack(one_ref[...] + two_ref[...])
     square = jnp.dot(gram, gram, precision=HIGHEST, preferred_element_type=F32)
     put_tiles(work_ref, 0, square)
     eliminate(work_ref, factor_ref, spread_ref, WIDTH // BLOCK)
@@ -269,19 +327,25 @@
     put_tiles(work_ref, 0, square)
     put_tiles(work_ref, WIDTH // BLOCK, factor)
     eliminate(work_ref, factor_ref, spread_ref, 2 * WIDTH // BLOCK)
-    out_ref[...] = tiles_of(factor_ref, 0, WIDTH, WIDTH // BLOCK, 2 * WIDTH // BLOCK)
-
-
-def pair_rotation(pair_gram):
+    halves = [
+        tiles_of(factor_ref, start, start + BLOCK, WIDTH // BLOCK, 2 * WIDTH // BLOCK)
+        for start in (0, BLOCK)
+    ]
+    first_ref[...] = jnp.where(swap_ref[0] == 1, halves[1], halves[0])
+    second_ref[...] = jnp.where(swap_ref[0] == 1, halves[0], halves[1])
+
+
+def pair_rotation(swap, parts):
     tiles = pltpu.VMEM((2 * WIDTH // BLOCK, WIDTH, BLOCK), F32)
     return pl.pallas_call(
         rotation_kernel,
-        out_shape=jax.ShapeDtypeStruct((WIDTH, WIDTH), F32),
+        in_specs=[pl.BlockSpec(memory_space=pltpu.SMEM)] + [pl.BlockSpec(memory_space=pltpu.VMEM)] * 2,
+        out_shape=[jax.ShapeDtypeStruct((BLOCK, WIDTH), F32)] * 2,
         scratch_shapes=[tiles, tiles, pltpu.VMEM((2 * SUB * SUB, BLOCK), F32)],
         compiler_params=grant(8),
-        cost_estimate=pl.CostEstimate(flops=20_000_000_000, bytes_accessed=1 << 19, transcendentals=0),
+        cost_estimate=pl.CostEstimate(flops=1000, bytes_accessed=1000, transcendentals=0),
         name="rotation",
-    )(pair_gram)
+    )(swap, *parts)
 
 
 def product(rows, rotation_t):
@@ -292,68 +356,167 @@
     return turned + lax.dot_general(high, turn_low, LANES, preferred_element_type=F32)
 
 
-def turn_kernel(rows_ref, rotation_ref, first_ref, second_ref):
-    turned = product(rows_ref[...], rotation_ref[...])
-    first_ref[...] = turned[:, :BLOCK]
-    second_ref[...] = turned[:, BLOCK:]
-
-
-def turn(pair_rows, rotation_t):
-    rows = pair_rows.shape[0]
-    half = pl.BlockSpec((TILE, BLOCK), lambda i: (i, 0))
-    return pl.pallas_call(
-        turn_kernel,
-        grid=(rows // TILE,),
-        in_specs=[
-            pl.BlockSpec((TILE, WIDTH), lambda i: (i, 0)),
-            pl.BlockSpec((WIDTH, WIDTH), lambda i: (0, 0)),
+def turn_kernel(start, source_ref, one_ref, two_ref, first_ref, second_ref, rows_ref, sems):
+    tiles = rows_ref.shape[0] // TILE
+    for tile in range(tiles):
+        row_copy(source_ref, rows_ref, sems, tile, start // TILE).start()
+    rotation_t = jnp.concatenate([one_ref[...], two_ref[...]])
+
+    @pl.loop(0, tiles)
+    def _(tile):
+        row_copy(source_ref, rows_ref, sems, tile, start // TILE).wait()
+        rows = pl.ds(pl.multiple_of(tile * TILE, TILE), TILE)
+        turned = product(rows_ref[rows, :], rotation_t)
+        first_ref[rows, :] = turned[:, :BLOCK]
+        second_ref[rows, :] = turned[:, BLOCK:]
+
+
+def turn(pair_rows, rotation_t, start, end):
+    rows = end - start
+    whole = pl.BlockSpec(memory_space=pltpu.VMEM)
+    return pl.pallas_call(
+        functools.partial(turn_kernel, start),
+        in_specs=[pl.BlockSpec(memory_space=pltpu.HBM), whole, whole],
+        out_specs=[whole, whole],
+        out_shape=[jax.ShapeDtypeStruct((rows, BLOCK), F32)] * 2,
+        scratch_shapes=[
+            pltpu.VMEM((rows, WIDTH), F32),
+            pltpu.SemaphoreType.DMA((rows // TILE,)),
         ],
-        out_specs=[half, half],
-        out_shape=[jax.ShapeDtypeStruct((rows, BLOCK), F32)] * 2,
-        compiler_params=grant(12),
+        compiler_params=grant(16),
+        cost_estimate=cost(rows),
         name="turn",
-    )(pair_rows, rotation_t)
-
-
-def moved_turn_kernel(ends, below_ref, second_ref, above_ref, first_ref, rotation_ref, out_ref):
-    tile = moved_tile(ends, below_ref[...], second_ref[...], above_ref[...], first_ref[...])
-    out_ref[...] = product(tile, rotation_ref[...])
-
-
-def moved_turn(ends, moved, rotation_t):
-    rows = moved[0].shape[0]
-    return pl.pallas_call(
-        moved_turn_kernel,
+    )(in_hbm(pair_rows), *rotation_t)
+
+
+def raw_turn_kernel(ends, *refs):
+    below_ref, above_ref, own_ref, first_ref, second_ref, below_t_ref, above_t_ref = refs[:7]
+    out_ref, packed_ref, total_ref, cross_ref = refs[7:]
+
+    @pl.when(pl.program_id(0) == 0)
+    def _():
+        total_ref[...] = jnp.zeros_like(total_ref)
+        cross_ref[...] = jnp.zeros_like(cross_ref)
+
+    own = own_ref[...]
+    upper_t = jnp.where(ends[0] == 1, second_ref[...], below_t_ref[...])
+    lower_t = jnp.where(ends[1] == 1, first_ref[...], above_t_ref[...])
+    upper = product(jnp.where(ends[0] == 1, own, below_ref[...]), upper_t)
+    lower = product(jnp.where(ends[1] == 1, own, above_ref[...]), lower_t)
+    tile = jnp.concatenate([upper, lower], axis=1)
+    out_ref[...] = tile
+    add_gram(tile, total_ref, cross_ref)
+
+    @pl.when(pl.program_id(0) == pl.num_programs(0) - 1)
+    def _():
+        packed_ref[...] = pack(total_ref, cross_ref)
+
+
+def raw_turn(ends, below, above, own, *rotations_t):
+    rows = below.shape[0]
+    tile = pl.BlockSpec((TILE, WIDTH), lambda i, ends: (i, 0))
+    half = pl.BlockSpec((BLOCK, WIDTH), lambda i, ends: (0, 0))
+    return pl.pallas_call(
+        raw_turn_kernel,
         grid_spec=pltpu.PrefetchScalarGridSpec(
             num_scalar_prefetch=1,
             grid=(rows // TILE,),
-            in_specs=moved_specs() + [pl.BlockSpec((WIDTH, WIDTH), lambda i, ends: (0, 0))],
-            out_specs=pl.BlockSpec((TILE, WIDTH), lambda i, ends: (i, 0)),
+            in_specs=[tile, tile, tile] + [half] * 4,
+            out_specs=[tile, pl.BlockSpec((3 * BLOCK, BLOCK), lambda i, ends: (0, 0))],
+            scratch_shapes=[pltpu.VMEM((WIDTH, WIDTH), F32)] * 2,
         ),
+        out_shape=[
+            jax.ShapeDtypeStruct((rows, WIDTH), F32),
+            jax.ShapeDtypeStruct((3 * BLOCK, BLOCK), F32),
+        ],
+        compiler_params=grant(12),
+        cost_estimate=cost(2 * rows),
+        name="raw_turn",
+    )(ends, below, above, own, *rotations_t)
+
+
+def last_turn_kernel(ends, one_ref, two_ref, raw_ref, *refs):
+    main_refs, rest_refs, (out_ref, rows_ref, turned_ref, sems, out_sems) = refs[:4], refs[4:8], refs[8:]
+    for tile in range(RAW // TILE):
+        for column in range(2):
+            half = raw_ref.at[:, pl.ds(column * BLOCK, BLOCK)]
+            half_copies(half, rows_ref, sems, tile, 0, column).start()
+    start_moved(ends, main_refs, rows_ref, sems, RAW // TILE)
+    start_moved(ends, rest_refs, rows_ref, sems, (RAW + MAIN) // TILE)
+
+    def out_copy(tile):
+        rows = pl.ds(pl.multiple_of(tile * TILE, TILE), TILE)
+        return pltpu.make_async_copy(turned_ref.at[rows, :], out_ref.at[rows, :], out_sems.at[tile])
+
+    tiles = rows_ref.shape[0] // TILE
+    rotation_t = jnp.concatenate([one_ref[...], two_ref[...]])
+
+    @pl.loop(0, tiles)
+    def _(tile):
+        rows = wait_tile(main_refs[0], rows_ref, sems, tile)
+        turned_ref[pl.ds(pl.multiple_of(tile * TILE, TILE), TILE), :] = product(rows, rotation_t)
+        out_copy(tile).start()
+
+    @pl.loop(0, tiles)
+    def _(tile):
+        out_copy(tile).wait()
+
+
+def last_turn(ends, rotation_t, raw, main, rest):
+    rows = raw.shape[0] + main[0].shape[0] + rest[0].shape[0]
+    return pl.pallas_call(
+        last_turn_kernel,
+        in_specs=[pl.BlockSpec(memory_space=pltpu.SMEM)]
+        + [pl.BlockSpec(memory_space=pltpu.VMEM)] * 2
+        + [pl.BlockSpec(memory_space=pl.ANY)] * 9,
+        out_specs=pl.BlockSpec(memory_space=pl.ANY),
         out_shape=jax.ShapeDtypeStruct((rows, WIDTH), F32),
-        compiler_params=grant(12),
-        name="moved_turn",
-    )(ends, *moved, rotation_t)
+        scratch_shapes=[pltpu.VMEM((rows, WIDTH), F32)] * 2
+        + [pltpu.SemaphoreType.DMA((2, rows // TILE)), pltpu.SemaphoreType.DMA((rows // TILE,))],
+        compiler_params=grant(24),
+        cost_estimate=cost(rows),
+        name="last_turn",
+    )(ends, *rotation_t, raw, *main, *rest)
+
+
+def send_up(value):
+    count = lax.axis_size("col")
+    return lax.ppermute(value, "col", [(p, p + 1) for p in range(count - 1)])
+
+
+def send_down(value):
+    count = lax.axis_size("col")
+    return lax.ppermute(value, "col", [(p, p - 1) for p in range(1, count)])
 
 
 def local(diffs, pairing):
     col_count = lax.axis_size("col")
     position = lax.axis_index("col")
     local_rows = diffs.shape[0]
-    ends = jnp.stack([position == 0, position == col_count - 1]).astype(jnp.int32)
+    rows = col_count * local_rows
+    bottom, top = position == 0, position == col_count - 1
+    ends = jnp.stack([bottom, top]).astype(jnp.int32)
     ordered = order_pairs(diffs, pairing)
     pair_rows = lax.all_to_all(ordered, "col", split_axis=0, concat_axis=0, tiled=True)
-    pair_rows = pair_rows.reshape(-1, WIDTH)
-
-    rotation_t = pair_rotation(row_total(local_gram(pair_rows)))
-    swapped = jnp.concatenate([rotation_t[BLOCK:], rotation_t[:BLOCK]])
-    first, second = turn(pair_rows, jnp.where(position == 0, swapped, rotation_t))
-    above = lax.ppermute(second, "col", [(p, p - 1) for p in range(1, col_count)])
-    below = lax.ppermute(first, "col", [(p, p + 1) for p in range(col_count - 1)])
-
-    moved = (below, second, above, first)
-    rotation_t = pair_rotation(row_total(moved_gram(ends, moved)))
-    return moved_turn(ends, moved, rotation_t).reshape(col_count, 1, local_rows, WIDTH)
+    pair_rows = pair_rows.reshape(rows, WIDTH)
+
+    parts = row_parts(local_gram(pair_rows))
+    *parts, own = lax.optimization_barrier((*parts, pair_rows[:RAW]))
+    below, above = send_up(own), send_down(own)
+    first_t, second_t = pair_rotation(ends[:1], parts)
+    sent = (below, above, send_up(first_t), send_down(second_t))
+    moved = []
+    for start, end in ((RAW, RAW + MAIN), (RAW + MAIN, rows)):
+        first, second = turn(pair_rows, (first_t, second_t), start, end)
+        if start == RAW:
+            first, second, *sent = lax.optimization_barrier((first, second, *sent))
+        moved.append((send_up(first), second, send_down(second), first))
+    below, above, below_t, above_t = sent
+    raw, gram = raw_turn(ends, below, above, own, first_t, second_t, below_t, above_t)
+    for part in moved:
+        gram = moved_gram(ends, gram, part)
+    rotation_t = pair_rotation(jnp.zeros((1,), jnp.int32), row_parts(gram))
+    return last_turn(ends, rotation_t, raw, *moved).reshape(col_count, 1, local_rows, WIDTH)
 
 
 def solution(mesh):

time: 301 us -> 292 us (0.970)
  waiting for transfers between devices: 108 us -> 70.7 us
  starting transfers between devices: 12.3 us -> 40 us
    ppermute x6 -> x12, waiting for transfers between devices: 108 us -> 70.7 us  [the longest x4 53.9 us: send_up(): return lax.ppermute(value, 'col', [(p, p + 1) for p in range(count - 1)])]
    ppermute x6 -> x12, starting transfers between devices: 12.3 us -> 40 us  [the longest x4 30.4 us: send_down(): return lax.ppermute(value, 'col', [(p, p - 1) for p in range(1, count)])]
    unnamed x10 -> x4, local copies, waits for them, and re-layouts: 7.44 us -> 4.04 us
    pallas_call x6 -> x9, Pallas kernels: 61.7 us -> 64.2 us  [the longest x2 31 us: pair_rotation(): pl.pallas_call(rotation_kernel, in_specs=[pl.BlockSpec(memory_space=pltpu...]
  transfers between devices with their start and end apart: 6 -> 12, of which waited for: 6 -> 8; matrix products, arithmetic and copies ran while one was open for 0% -> 0% of each run, Pallas kernels for 0% -> 11%
where the time goes in v3:
time: 292 us; the launch traced here: 289 us
  blocking collectives  106 us (36%)
  waiting for transfers between devices  70.7 us (24%)
  Pallas kernels  66.9 us (23%)
  starting transfers between devices  40 us (14%)
  local copies, waits for them, and re-layouts  5.33 us (2%)
    all_to_all x1, blocking collectives, local(): lax.all_to_all(ordered, 'col', split_axis=0, concat_axis=0, tiled=True)  106 us
    ppermute x4, waiting for transfers between devices, send_up(): return lax.ppermute(value, 'col', [(p, p + 1) for p in range(count - 1)])  53.9 us
    pallas_call x2, Pallas kernels, pair_rotation(): pl.pallas_call(rotation_kernel, in_specs=[pl.BlockSpec(memory_space=pltpu...  31 us
    ppermute x4, starting transfers between devices, send_down(): return lax.ppermute(value, 'col', [(p, p - 1) for p in range(1, count)])  30.4 us
    ppermute x4, waiting for transfers between devices, row_parts(): parts = (packed, lax.ppermute(packed, 'row', swap))  14.1 us
    pallas_call x1, Pallas kernels, last_turn(): pl.pallas_call(last_turn_kernel, in_specs=[pl.BlockSpec(memory_space=pltp...  9.23 us
    pallas_call x2, Pallas kernels, turn(): pl.pallas_call(functools.partial(turn_kernel, start), in_specs=[pl.BlockS...  8.07 us
    ppermute x4, starting transfers between devices, send_up(): return lax.ppermute(value, 'col', [(p, p + 1) for p in range(count - 1)])  8 us
  transfers between devices with their start and end apart: 12, of which 8 were waited for; matrix products, arithmetic and copies ran while one was open for 0% of the time, Pallas kernels for 11%

profile of v3, /device:TPU:32, one launch (start us, length us, event | category | flops | bytes accessed | tf_op | source)
XLA Modules:
  0.0 289.4 jit_solution(7130961941639268329)
XLA Ops:
  0.0 3.4 %copy-done = f32[256,8192]{1,0:T(8,128)S(1)} copy-done((f32[256,8192]{1,0:T(8,128)S(1)}, f32[256,8192]{1,0:T(8,128)}, u32[]{:S(2)}) %copy-start) | copy-done | bytes 8388632
  4.0 2.7 order.1
  6.7 106.0 %all_to_all.5 = f32[32,256,256]{2,1,0:T(8,128)} all-to-all(f32[32,256,256]{2,1,0:T(8,128)S(1)} %order.1), channel_id=1, replica_groups=mesh['col'=32,'row'=4] {'col'}, dimensions={0} | all-to-all | bytes 16777216 | tf_op jit(solution)/shard_map/all_to_all | solution.py:500
  112.7 6.5 %gram.1 = f32[384,128]{1,0:T(8,128)S(1)} custom-call(f32[8192,256]{1,0:T(8,128)} %bitcast.12), custom_call_target="tpu_custom_call" | custom-call | flops 1000 | bytes 1000 | tf_op jit(solution)/shard_map/gram/pallas_call | solution.py:120
  122.9 5.0 %collective-permute-done.1.two_ref = f32[384,128]{1,0:T(8,128)S(1)} collective-permute-done((f32[384,128]{1,0:T(8,128)S(1)}, f32[384,128]{1,0:T(8,128)S(1)}, u32[]{:S(2)}, u32[]{:S(2)}) %collective-permute-start.1) | collective-permute-done | bytes 196640 | tf_op jit(solution)/shard_map/ppermute | solution.py:212
  127.9 5.0 %collective-permute-start.3 = (f32[1024,256]{1,0:T(8,128)S(1)}, f32[1024,256]{1,0:T(8,128)S(1)}, u32[]{:S(2)}, u32[]{:S(2)}) collective-permute-start(f32[1024,256]{1,0:T(8,128)S(1)} %bitcast.8), channel_id=1, source_target_pairs={{4,0},{8,4},{12,8},{16,12},{20,16},{24,20},{28,24},{32,28},{36,32}... | collective-permute-start | bytes 3145736 | tf_op jit(solution)/shard_map/ppermute | solution.py:489
  132.8 2.1 collective-permute-start.2
  135.0 15.5 %rotation.2 = (f32[128,256]{1,0:T(8,128)S(1)}, f32[128,256]{1,0:T(8,128)S(1)}) custom-call(s32[1]{0:T(128)S(1)} %bitcast.11, f32[384,128]{1,0:T(8,128)S(1)} %add.6.one_ref, f32[384,128]{1,0:T(8,128)S(1)} %collective-permute-done.1.two_ref), custom_call_target="tpu_custom_call" | custom-call | flops 1000 | bytes 1000 | tf_op jit(solution)/shard_map/rotation/pallas_call | solution.py:340
  150.6 2.1 collective-permute-start.4
  152.6 8.3 %collective-permute-start.5 = (f32[128,256]{1,0:T(8,128)S(1)}, f32[128,256]{1,0:T(8,128)S(1)}, u32[]{:S(2)}, u32[]{:S(2)}) collective-permute-start(f32[128,256]{1,0:T(8,128)S(1)} %get-tuple-element.27.two_ref.refs_4_), channel_id=1, source_target_pairs={{4,0},{8,4},{12,8},{16,12},{20,16},{24,20},{28,24},{32,28},{36,32}... | collective-permute-start | bytes 393224 | tf_op jit(solution)/shard_map/ppermute | solution.py:489
  160.9 5.3 %turn.2 = (f32[5120,128]{1,0:T(8,128)S(1)}, f32[5120,128]{1,0:T(8,128)S(1)}) custom-call(f32[8192,256]{1,0:T(8,128)} %bitcast.13, f32[128,256]{1,0:T(8,128)S(1)} %get-tuple-element.26.one_ref.refs_3_, f32[128,256]{1,0:T(8,128)S(1)} %get-tuple-element.27.two_ref.refs_4_), custom_call_target="tpu_custom_call" | custom-call | flops 2013265920 | bytes 10485760 | tf_op jit(solution)/shard_map/turn/pallas_call | solution.py:377
  166.3 1.9 collective-permute-start.6
  168.2 8.4 %collective-permute-start.7 = (f32[5120,128]{1,0:T(8,128)S(1)}, f32[5120,128]{1,0:T(8,128)S(1)}, u32[]{:S(2)}, u32[]{:S(2)}) collective-permute-start(f32[5120,128]{1,0:T(8,128)S(1)} %get-tuple-element.37.refs_1_), channel_id=1, source_target_pairs={{4,0},{8,4},{12,8},{16,12},{20,16},{24,20},{28,24},{32,28},{36,32}... | collective-permute-start | bytes 7864328 | tf_op jit(solution)/shard_map/ppermute | solution.py:489
  176.7 2.8 turn.3
  179.4 1.9 collective-permute-start.8
  181.4 8.7 %collective-permute-start.9 = (f32[2048,128]{1,0:T(8,128)S(1)}, f32[2048,128]{1,0:T(8,128)S(1)}, u32[]{:S(2)}, u32[]{:S(2)}) collective-permute-start(f32[2048,128]{1,0:T(8,128)S(1)} %get-tuple-element.39.refs_1_.refs_5_), channel_id=1, source_target_pairs={{4,0},{8,4},{12,8},{16,12},{20,16},{24,20},{28,24},{32,28},{36,32}... | collective-permute-start | bytes 3145736 | tf_op jit(solution)/shard_map/ppermute | solution.py:489
  190.0 2.4 raw_turn.1
  192.5 40.0 %collective-permute-done.6.refs_0_ = f32[5120,128]{1,0:T(8,128)S(1)} collective-permute-done((f32[5120,128]{1,0:T(8,128)S(1)}, f32[5120,128]{1,0:T(8,128)S(1)}, u32[]{:S(2)}, u32[]{:S(2)}) %collective-permute-start.6) | collective-permute-done | bytes 2621472 | tf_op jit(solution)/shard_map/ppermute | solution.py:484
  234.0 4.6 %moved_gram.2.before_ref = f32[384,128]{1,0:T(8,128)S(1)} custom-call(s32[2]{0:T(128)S(1)} %add_convert_fusion.ends, f32[384,128]{1,0:T(8,128)S(1)} %get-tuple-element.35.before_ref, f32[5120,128]{1,0:T(8,128)S(1)} %collective-permute-done.6.refs_0_, f32[5120,128]{1,0:T(8,128)S(1)} %get-tuple-element.37.refs_1_, ...), custom_call_target="tpu_custom_call" | custom-call | flops 2013265920 | bytes 10485760 | tf_op jit(solution)/shard_map/moved_gram/pallas_call | solution.py:190
  238.6 13.8 %collective-permute-done.8.refs_0_.refs_4_ = f32[2048,128]{1,0:T(8,128)S(1)} collective-permute-done((f32[2048,128]{1,0:T(8,128)S(1)}, f32[2048,128]{1,0:T(8,128)S(1)}, u32[]{:S(2)}, u32[]{:S(2)}) %collective-permute-start.8) | collective-permute-done | bytes 1048608 | tf_op jit(solution)/shard_map/ppermute | solution.py:484
  253.6 2.3 moved_gram.3
  258.1 6.3 %collective-permute-done.11.two_ref = f32[384,128]{1,0:T(8,128)S(1)} collective-permute-done((f32[384,128]{1,0:T(8,128)S(1)}, f32[384,128]{1,0:T(8,128)S(1)}, u32[]{:S(2)}, u32[]{:S(2)}) %collective-permute-start.11) | collective-permute-done | bytes 196640 | tf_op jit(solution)/shard_map/ppermute | solution.py:212
  264.5 15.5 %rotation.3 = (f32[128,256]{1,0:T(8,128)S(1)}, f32[128,256]{1,0:T(8,128)S(1)}) custom-call(s32[1]{0:T(128)} %constant.11.clone.1.swap_ref, f32[384,128]{1,0:T(8,128)S(1)} %add.7.one_ref, f32[384,128]{1,0:T(8,128)S(1)} %collective-permute-done.11.two_ref), custom_call_target="tpu_custom_call" | custom-call | flops 1000 | bytes 1000 | tf_op jit(solution)/shard_map/rotation/pallas_call | solution.py:340
  279.9 9.2 %last_turn.1 = f32[8192,256]{1,0:T(8,128)} custom-call(s32[2]{0:T(128)S(1)} %add_convert_fusion.ends, f32[128,256]{1,0:T(8,128)S(1)} %get-tuple-element.40.one_ref, f32[128,256]{1,0:T(8,128)S(1)} %get-tuple-element.41.two_ref, f32[1024,256]{1,0:T(8,128)S(1)} %get-tuple-element.42.raw_ref, f32[5120,128]{1,0:T(8,128)S(1)} %collective-permute-done.6.refs_0_, ...), custom_call_target="tpu_custom_call" | custom-call | flops 3221225472 | bytes 16777216 | tf_op jit(solution)/shard_map/last_turn/pallas_call | solution.py:467
  (19 shorter events, 9.2 us)
Async XLA Ops:
  0.0 3.4 %copy-start = (f32[256,8192]{1,0:T(8,128)S(1)}, f32[256,8192]{1,0:T(8,128)}, u32[]{:S(2)}) copy-start(f32[256,8192]{1,0:T(8,128)} %diffs_ref.1) | copy-start | bytes 25165828
  3.4 0.7 copy-start.1
  119.3 1.5 collective-permute-start
  120.8 7.0 %collective-permute-start.1 = (f32[384,128]{1,0:T(8,128)S(1)}, f32[384,128]{1,0:T(8,128)S(1)}, u32[]{:S(2)}, u32[]{:S(2)}) collective-permute-start(f32[384,128]{1,0:T(8,128)S(1)} %add.6.one_ref), channel_id=1, source_target_pairs={{0,2},{1,3},{2,0},{3,1},{4,6},{5,7},{6,4},{7,5},{8,10},{9,11},{10,... | collective-permute-start | bytes 589832 | tf_op jit(solution)/shard_map/ppermute | solution.py:212
  127.9 38.4 %collective-permute-start.3 = (f32[1024,256]{1,0:T(8,128)S(1)}, f32[1024,256]{1,0:T(8,128)S(1)}, u32[]{:S(2)}, u32[]{:S(2)}) collective-permute-start(f32[1024,256]{1,0:T(8,128)S(1)} %bitcast.8), channel_id=1, source_target_pairs={{4,0},{8,4},{12,8},{16,12},{20,16},{24,20},{28,24},{32,28},{36,32}... | collective-permute-start | bytes 3145736 | tf_op jit(solution)/shard_map/ppermute | solution.py:489
  132.8 33.4 %collective-permute-start.2 = (f32[1024,256]{1,0:T(8,128)S(1)}, f32[1024,256]{1,0:T(8,128)S(1)}, u32[]{:S(2)}, u32[]{:S(2)}) collective-permute-start(f32[1024,256]{1,0:T(8,128)S(1)} %bitcast.9), channel_id=1, source_target_pairs={{0,4},{4,8},{8,12},{12,16},{16,20},{20,24},{24,28},{28,32},{32,36}... | collective-permute-start | bytes 3145736 | tf_op jit(solution)/shard_map/ppermute | solution.py:484
  150.6 15.7 %collective-permute-start.4 = (f32[128,256]{1,0:T(8,128)S(1)}, f32[128,256]{1,0:T(8,128)S(1)}, u32[]{:S(2)}, u32[]{:S(2)}) collective-permute-start(f32[128,256]{1,0:T(8,128)S(1)} %get-tuple-element.26.one_ref.refs_3_), channel_id=1, source_target_pairs={{0,4},{4,8},{8,12},{12,16},{16,20},{20,24},{24,28},{28,32},{32,36}... | collective-permute-start | bytes 393224 | tf_op jit(solution)/shard_map/ppermute | solution.py:484
  152.6 13.6 %collective-permute-start.5 = (f32[128,256]{1,0:T(8,128)S(1)}, f32[128,256]{1,0:T(8,128)S(1)}, u32[]{:S(2)}, u32[]{:S(2)}) collective-permute-start(f32[128,256]{1,0:T(8,128)S(1)} %get-tuple-element.27.two_ref.refs_4_), channel_id=1, source_target_pairs={{4,0},{8,4},{12,8},{16,12},{20,16},{24,20},{28,24},{32,28},{36,32}... | collective-permute-start | bytes 393224 | tf_op jit(solution)/shard_map/ppermute | solution.py:489
  166.3 66.2 %collective-permute-start.6 = (f32[5120,128]{1,0:T(8,128)S(1)}, f32[5120,128]{1,0:T(8,128)S(1)}, u32[]{:S(2)}, u32[]{:S(2)}) collective-permute-start(f32[5120,128]{1,0:T(8,128)S(1)} %get-tuple-element.36.refs_3_), channel_id=1, source_target_pairs={{0,4},{4,8},{8,12},{12,16},{16,20},{20,24},{24,28},{28,32},{32,36}... | collective-permute-start | bytes 7864328 | tf_op jit(solution)/shard_map/ppermute | solution.py:484
  168.2 65.7 %collective-permute-start.7 = (f32[5120,128]{1,0:T(8,128)S(1)}, f32[5120,128]{1,0:T(8,128)S(1)}, u32[]{:S(2)}, u32[]{:S(2)}) collective-permute-start(f32[5120,128]{1,0:T(8,128)S(1)} %get-tuple-element.37.refs_1_), channel_id=1, source_target_pairs={{4,0},{8,4},{12,8},{16,12},{20,16},{24,20},{28,24},{32,28},{36,32}... | collective-permute-start | bytes 7864328 | tf_op jit(solution)/shard_map/ppermute | solution.py:489
  179.4 73.0 %collective-permute-start.8 = (f32[2048,128]{1,0:T(8,128)S(1)}, f32[2048,128]{1,0:T(8,128)S(1)}, u32[]{:S(2)}, u32[]{:S(2)}) collective-permute-start(f32[2048,128]{1,0:T(8,128)S(1)} %get-tuple-element.38.refs_3_.refs_7_), channel_id=1, source_target_pairs={{0,4},{4,8},{8,12},{12,16},{16,20},{20,24},{24,28},{28,32},{32,36}... | collective-permute-start | bytes 3145736 | tf_op jit(solution)/shard_map/ppermute | solution.py:484
  181.4 72.2 %collective-permute-start.9 = (f32[2048,128]{1,0:T(8,128)S(1)}, f32[2048,128]{1,0:T(8,128)S(1)}, u32[]{:S(2)}, u32[]{:S(2)}) collective-permute-start(f32[2048,128]{1,0:T(8,128)S(1)} %get-tuple-element.39.refs_1_.refs_5_), channel_id=1, source_target_pairs={{4,0},{8,4},{12,8},{16,12},{20,16},{24,20},{28,24},{32,28},{36,32}... | collective-permute-start | bytes 3145736 | tf_op jit(solution)/shard_map/ppermute | solution.py:489
  255.9 1.5 collective-permute-start.10
  257.4 7.0 %collective-permute-start.11 = (f32[384,128]{1,0:T(8,128)S(1)}, f32[384,128]{1,0:T(8,128)S(1)}, u32[]{:S(2)}, u32[]{:S(2)}) collective-permute-start(f32[384,128]{1,0:T(8,128)S(1)} %add.7.one_ref), channel_id=1, source_target_pairs={{0,2},{1,3},{2,0},{3,1},{4,6},{5,7},{6,4},{7,5},{8,10},{9,11},{10,... | collective-permute-start | bytes 589832 | tf_op jit(solution)/shard_map/ppermute | solution.py:212

commit v4 on v3

--- a/solution.py
+++ b/solution.py
@@ -9,9 +9,9 @@
 
 BLOCK = 128
 WIDTH = 2 * BLOCK
-TILE = 512
-RAW = 2 * TILE
-MAIN = 10 * TILE
+TILE = 1024
+CHUNKS = (5 * TILE, 2 * TILE)
+STRIP = 64
 PANEL = 32
 SUB = 8
 HIGHEST = lax.Precision.HIGHEST
@@ -41,22 +41,27 @@
     return high, middle, (rest - middle.astype(F32)).astype(BF16)
 
 
-def order_kernel(pairing_ref, diffs_ref, out_ref, sems):
-    count = pairing_ref.shape[0]
-
-    def copy(block):
-        column = pl.multiple_of(pairing_ref[block] * BLOCK, BLOCK)
-        half = pl.ds((block % 2) * BLOCK, BLOCK)
-        return pltpu.make_async_copy(
-            diffs_ref.at[:, pl.ds(column, BLOCK)],
-            out_ref.at[block // 2, :, half],
-            sems.at[block],
-        )
-
-    for block in range(count):
-        copy(block).start()
-    for block in range(count):
-        copy(block).wait()
+def order_kernel(pairing_ref, diffs_ref, out_ref, rows_ref, sems):
+    strips = rows_ref.shape[0] // STRIP
+
+    def strip_copy(strip):
+        rows = pl.ds(pl.multiple_of(strip * STRIP, STRIP), STRIP)
+        return pltpu.make_async_copy(diffs_ref.at[rows, :], rows_ref.at[rows, :], sems.at[strip])
+
+    for strip in range(strips):
+        strip_copy(strip).start()
+
+    @pl.loop(0, strips)
+    def _(strip):
+        strip_copy(strip).wait()
+        rows = pl.ds(pl.multiple_of(strip * STRIP, STRIP), STRIP)
+
+        @pl.loop(0, out_ref.shape[0])
+        def _(pair):
+            for half in range(2):
+                column = pl.multiple_of(pairing_ref[2 * pair + half] * BLOCK, BLOCK)
+                block = rows_ref[rows, pl.ds(column, BLOCK)]
+                out_ref[pair, rows, half * BLOCK : (half + 1) * BLOCK] = block
 
 
 def order_pairs(diffs, pairing):
@@ -65,14 +70,17 @@
         order_kernel,
         in_specs=[
             pl.BlockSpec(memory_space=pltpu.SMEM),
-            pl.BlockSpec(memory_space=pl.ANY),
+            pl.BlockSpec(memory_space=pltpu.HBM),
         ],
-        out_specs=pl.BlockSpec(memory_space=pl.ANY),
+        out_specs=pl.BlockSpec(memory_space=pltpu.VMEM),
         out_shape=jax.ShapeDtypeStruct((columns // WIDTH, rows, WIDTH), F32),
-        scratch_shapes=[pltpu.SemaphoreType.DMA((columns // BLOCK,))],
-        compiler_params=grant(2),
+        scratch_shapes=[
+            pltpu.VMEM((rows, columns), F32),
+            pltpu.SemaphoreType.DMA((rows // STRIP,)),
+        ],
+        compiler_params=grant(24),
         name="order",
-    )(pairing, diffs)
+    )(pairing, in_hbm(diffs))
 
 
 def add_gram(tile, total_ref, cross_ref):
@@ -140,66 +148,45 @@
     )
 
 
-def half_copies(source_ref, rows_ref, sems, tile, first, column):
-    rows = pl.ds(pl.multiple_of(tile * TILE, TILE), TILE)
-    source = source_ref.at[pl.ds(pl.multiple_of((tile - first) * TILE, TILE), TILE), :]
-    half = pl.ds(column * BLOCK, BLOCK)
-    return pltpu.make_async_copy(source, rows_ref.at[rows, half], sems.at[column, tile])
-
-
-def start_moved(ends, moved_refs, rows_ref, sems, first):
-    below_ref, second_ref, above_ref, first_ref = moved_refs
-    tiles = below_ref.shape[0] // TILE
-    for column, arrived_ref, kept_ref in ((0, below_ref, second_ref), (1, above_ref, first_ref)):
-
-        @pl.when(ends[column] == 1)
-        def _():
-            for tile in range(first, first + tiles):
-                half_copies(kept_ref, rows_ref, sems, tile, first, column).start()
-
-        @pl.when(ends[column] == 0)
-        def _():
-            for tile in range(first, first + tiles):
-                half_copies(arrived_ref, rows_ref, sems, tile, first, column).start()
-
-
-def wait_tile(like_ref, rows_ref, sems, tile):
-    rows = pl.ds(pl.multiple_of(tile * TILE, TILE), TILE)
-    for column in range(2):
-        half = rows_ref.at[rows, pl.ds(column * BLOCK, BLOCK)]
-        pltpu.make_async_copy(like_ref.at[pl.ds(0, TILE), :], half, sems.at[column, tile]).wait()
-    return rows_ref[rows, :]
+def moved_rows(ends, moved_refs, start, count):
+    rows = pl.ds(start, count)
+    below, second, above, first = (ref[rows, :] for ref in moved_refs)
+    upper = jnp.where(ends[0] == 1, second, below)
+    lower = jnp.where(ends[1] == 1, first, above)
+    return upper, lower
+
+
+def moved_tile(ends, moved_refs, tile):
+    upper, lower = moved_rows(ends, moved_refs, pl.multiple_of(tile * TILE, TILE), TILE)
+    return jnp.concatenate([upper, lower], axis=1)
 
 
 def moved_gram_kernel(ends, before_ref, *refs):
-    moved_refs, (out_ref, total_ref, cross_ref, rows_ref, sems) = refs[:4], refs[4:]
-    start_moved(ends, moved_refs, rows_ref, sems, 0)
+    moved_refs, (out_ref, total_ref, cross_ref) = refs[:4], refs[4:]
     total_ref[...] = jnp.zeros_like(total_ref)
     cross_ref[...] = jnp.zeros_like(cross_ref)
 
-    @pl.loop(0, rows_ref.shape[0] // TILE)
+    @pl.loop(0, moved_refs[0].shape[0] // TILE)
     def _(tile):
-        add_gram(wait_tile(moved_refs[0], rows_ref, sems, tile), total_ref, cross_ref)
+        add_gram(moved_tile(ends, moved_refs, tile), total_ref, cross_ref)
 
     out_ref[...] = before_ref[...] + pack(total_ref, cross_ref)
 
 
+def in_vmem(count):
+    whole = pl.BlockSpec(memory_space=pltpu.VMEM)
+    return [pl.BlockSpec(memory_space=pltpu.SMEM)] + [whole] * count
+
+
 def moved_gram(ends, before, moved):
-    rows = moved[0].shape[0]
-    whole = pl.BlockSpec(memory_space=pltpu.VMEM)
     return pl.pallas_call(
         moved_gram_kernel,
-        in_specs=[pl.BlockSpec(memory_space=pltpu.SMEM), whole] + [pl.BlockSpec(memory_space=pl.ANY)] * 4,
-        out_specs=whole,
+        in_specs=in_vmem(5),
+        out_specs=pl.BlockSpec(memory_space=pltpu.VMEM),
         out_shape=jax.ShapeDtypeStruct((3 * BLOCK, BLOCK), F32),
-        scratch_shapes=[
-            pltpu.VMEM((WIDTH, WIDTH), F32),
-            pltpu.VMEM((WIDTH, WIDTH), F32),
-            pltpu.VMEM((rows, WIDTH), F32),
-            pltpu.SemaphoreType.DMA((2, rows // TILE)),
-        ],
-        compiler_params=grant(12),
-        cost_estimate=cost(rows),
+        scratch_shapes=[pltpu.VMEM((WIDTH, WIDTH), F32)] * 2,
+        compiler_params=grant(24),
+        cost_estimate=cost(moved[0].shape[0]),
         name="moved_gram",
     )(ends, before, *moved)
 
@@ -361,6 +348,11 @@
     for tile in range(tiles):
         row_copy(source_ref, rows_ref, sems, tile, start // TILE).start()
     rotation_t = jnp.concatenate([one_ref[...], two_ref[...]])
+    if first_ref.shape[0] > rows_ref.shape[0]:
+        for half_ref, out_ref in ((one_ref, first_ref), (two_ref, second_ref)):
+            end = rows_ref.shape[0]
+            out_ref[end : end + BLOCK, :] = half_ref[:, :BLOCK]
+            out_ref[end + BLOCK :, :] = half_ref[:, BLOCK:]
 
     @pl.loop(0, tiles)
     def _(tile):
@@ -371,112 +363,100 @@
         second_ref[rows, :] = turned[:, BLOCK:]
 
 
-def turn(pair_rows, rotation_t, start, end):
-    rows = end - start
+def turn(pair_rows, rotation_t, start, rows, extra):
     whole = pl.BlockSpec(memory_space=pltpu.VMEM)
     return pl.pallas_call(
         functools.partial(turn_kernel, start),
         in_specs=[pl.BlockSpec(memory_space=pltpu.HBM), whole, whole],
         out_specs=[whole, whole],
-        out_shape=[jax.ShapeDtypeStruct((rows, BLOCK), F32)] * 2,
+        out_shape=[jax.ShapeDtypeStruct((rows + extra, BLOCK), F32)] * 2,
         scratch_shapes=[
             pltpu.VMEM((rows, WIDTH), F32),
             pltpu.SemaphoreType.DMA((rows // TILE,)),
         ],
-        compiler_params=grant(16),
+        compiler_params=grant(24),
         cost_estimate=cost(rows),
         name="turn",
     )(in_hbm(pair_rows), *rotation_t)
 
 
-def raw_turn_kernel(ends, *refs):
-    below_ref, above_ref, own_ref, first_ref, second_ref, below_t_ref, above_t_ref = refs[:7]
-    out_ref, packed_ref, total_ref, cross_ref = refs[7:]
-
-    @pl.when(pl.program_id(0) == 0)
-    def _():
-        total_ref[...] = jnp.zeros_like(total_ref)
-        cross_ref[...] = jnp.zeros_like(cross_ref)
-
+def raw_gram_kernel(ends, below_ref, above_ref, own_ref, *refs):
+    moved_refs, (out_ref, packed_ref, total_ref, cross_ref) = refs[:4], refs[4:]
+    total_ref[...] = jnp.zeros_like(total_ref)
+    cross_ref[...] = jnp.zeros_like(cross_ref)
+    halves_t = [
+        jnp.concatenate([half[:BLOCK], half[BLOCK:]], axis=1)
+        for half in moved_rows(ends, moved_refs, CHUNKS[0], WIDTH)
+    ]
     own = own_ref[...]
-    upper_t = jnp.where(ends[0] == 1, second_ref[...], below_t_ref[...])
-    lower_t = jnp.where(ends[1] == 1, first_ref[...], above_t_ref[...])
-    upper = product(jnp.where(ends[0] == 1, own, below_ref[...]), upper_t)
-    lower = product(jnp.where(ends[1] == 1, own, above_ref[...]), lower_t)
+    upper = product(jnp.where(ends[0] == 1, own, below_ref[...]), halves_t[0])
+    lower = product(jnp.where(ends[1] == 1, own, above_ref[...]), halves_t[1])
     tile = jnp.concatenate([upper, lower], axis=1)
     out_ref[...] = tile
     add_gram(tile, total_ref, cross_ref)
-
-    @pl.when(pl.program_id(0) == pl.num_programs(0) - 1)
-    def _():
-        packed_ref[...] = pack(total_ref, cross_ref)
-
-
-def raw_turn(ends, below, above, own, *rotations_t):
-    rows = below.shape[0]
-    tile = pl.BlockSpec((TILE, WIDTH), lambda i, ends: (i, 0))
-    half = pl.BlockSpec((BLOCK, WIDTH), lambda i, ends: (0, 0))
-    return pl.pallas_call(
-        raw_turn_kernel,
-        grid_spec=pltpu.PrefetchScalarGridSpec(
-            num_scalar_prefetch=1,
-            grid=(rows // TILE,),
-            in_specs=[tile, tile, tile] + [half] * 4,
-            out_specs=[tile, pl.BlockSpec((3 * BLOCK, BLOCK), lambda i, ends: (0, 0))],
-            scratch_shapes=[pltpu.VMEM((WIDTH, WIDTH), F32)] * 2,
-        ),
+    packed_ref[...] = pack(total_ref, cross_ref)
+
+
+def raw_gram(ends, below, above, own, moved):
+    whole = pl.BlockSpec(memory_space=pltpu.VMEM)
+    return pl.pallas_call(
+        raw_gram_kernel,
+        in_specs=in_vmem(7),
+        out_specs=[whole, whole],
         out_shape=[
-            jax.ShapeDtypeStruct((rows, WIDTH), F32),
+            jax.ShapeDtypeStruct((TILE, WIDTH), F32),
             jax.ShapeDtypeStruct((3 * BLOCK, BLOCK), F32),
         ],
-        compiler_params=grant(12),
-        cost_estimate=cost(2 * rows),
-        name="raw_turn",
-    )(ends, below, above, own, *rotations_t)
+        scratch_shapes=[pltpu.VMEM((WIDTH, WIDTH), F32)] * 2,
+        compiler_params=grant(24),
+        cost_estimate=cost(2 * TILE),
+        name="raw_gram",
+    )(ends, below, above, own, *moved)
 
 
 def last_turn_kernel(ends, one_ref, two_ref, raw_ref, *refs):
-    main_refs, rest_refs, (out_ref, rows_ref, turned_ref, sems, out_sems) = refs[:4], refs[4:8], refs[8:]
-    for tile in range(RAW // TILE):
-        for column in range(2):
-            half = raw_ref.at[:, pl.ds(column * BLOCK, BLOCK)]
-            half_copies(half, rows_ref, sems, tile, 0, column).start()
-    start_moved(ends, main_refs, rows_ref, sems, RAW // TILE)
-    start_moved(ends, rest_refs, rows_ref, sems, (RAW + MAIN) // TILE)
+    moved, (out_ref, turned_ref, sems) = (refs[0:4], refs[4:8]), refs[8:]
+    rotation_t = jnp.concatenate([one_ref[...], two_ref[...]])
 
     def out_copy(tile):
         rows = pl.ds(pl.multiple_of(tile * TILE, TILE), TILE)
-        return pltpu.make_async_copy(turned_ref.at[rows, :], out_ref.at[rows, :], out_sems.at[tile])
-
-    tiles = rows_ref.shape[0] // TILE
-    rotation_t = jnp.concatenate([one_ref[...], two_ref[...]])
-
-    @pl.loop(0, tiles)
-    def _(tile):
-        rows = wait_tile(main_refs[0], rows_ref, sems, tile)
+        return pltpu.make_async_copy(turned_ref.at[rows, :], out_ref.at[rows, :], sems.at[tile])
+
+    def put(tile, rows):
         turned_ref[pl.ds(pl.multiple_of(tile * TILE, TILE), TILE), :] = product(rows, rotation_t)
         out_copy(tile).start()
 
-    @pl.loop(0, tiles)
+    put(0, raw_ref[...])
+    done = 1
+    for moved_refs, rows in zip(moved, CHUNKS):
+
+        @pl.loop(0, rows // TILE)
+        def _(tile, moved_refs=moved_refs, done=done):
+            put(done + tile, moved_tile(ends, moved_refs, tile))
+
+        done += rows // TILE
+
+    @pl.loop(0, done)
     def _(tile):
         out_copy(tile).wait()
 
 
-def last_turn(ends, rotation_t, raw, main, rest):
-    rows = raw.shape[0] + main[0].shape[0] + rest[0].shape[0]
+def last_turn(ends, rotation_t, raw, moved):
+    rows = TILE + sum(CHUNKS)
+    moved = [array for part in moved for array in part]
     return pl.pallas_call(
         last_turn_kernel,
-        in_specs=[pl.BlockSpec(memory_space=pltpu.SMEM)]
-        + [pl.BlockSpec(memory_space=pltpu.VMEM)] * 2
-        + [pl.BlockSpec(memory_space=pl.ANY)] * 9,
+        in_specs=in_vmem(3 + len(moved)),
         out_specs=pl.BlockSpec(memory_space=pl.ANY),
         out_shape=jax.ShapeDtypeStruct((rows, WIDTH), F32),
-        scratch_shapes=[pltpu.VMEM((rows, WIDTH), F32)] * 2
-        + [pltpu.SemaphoreType.DMA((2, rows // TILE)), pltpu.SemaphoreType.DMA((rows // TILE,))],
+        scratch_shapes=[
+            pltpu.VMEM((rows, WIDTH), F32),
+            pltpu.SemaphoreType.DMA((rows // TILE,)),
+        ],
         compiler_params=grant(24),
         cost_estimate=cost(rows),
         name="last_turn",
-    )(ends, *rotation_t, raw, *main, *rest)
+    )(ends, *rotation_t, raw, *moved)
 
 
 def send_up(value):
@@ -501,22 +481,21 @@
     pair_rows = pair_rows.reshape(rows, WIDTH)
 
     parts = row_parts(local_gram(pair_rows))
-    *parts, own = lax.optimization_barrier((*parts, pair_rows[:RAW]))
+    *parts, own = lax.optimization_barrier((*parts, pair_rows[:TILE]))
     below, above = send_up(own), send_down(own)
-    first_t, second_t = pair_rotation(ends[:1], parts)
-    sent = (below, above, send_up(first_t), send_down(second_t))
-    moved = []
-    for start, end in ((RAW, RAW + MAIN), (RAW + MAIN, rows)):
-        first, second = turn(pair_rows, (first_t, second_t), start, end)
-        if start == RAW:
-            first, second, *sent = lax.optimization_barrier((first, second, *sent))
+    rotation_t = pair_rotation(ends[:1], parts)
+    moved, start = [], TILE
+    for chunk, count in enumerate(CHUNKS):
+        first, second = turn(pair_rows, rotation_t, start, count, 0 if chunk else WIDTH)
+        if chunk == 0:
+            first, second, below, above = lax.optimization_barrier((first, second, below, above))
         moved.append((send_up(first), second, send_down(second), first))
-    below, above, below_t, above_t = sent
-    raw, gram = raw_turn(ends, below, above, own, first_t, second_t, below_t, above_t)
+        start += count
+    raw, gram = raw_gram(ends, below, above, own, moved[0])
     for part in moved:
         gram = moved_gram(ends, gram, part)
     rotation_t = pair_rotation(jnp.zeros((1,), jnp.int32), row_parts(gram))
-    return last_turn(ends, rotation_t, raw, *moved).reshape(col_count, 1, local_rows, WIDTH)
+    return last_turn(ends, rotation_t, raw, moved).reshape(col_count, 1, local_rows, WIDTH)
 
 
 def solution(mesh):

time: 292 us -> 285 us (0.976)
  waiting for transfers between devices: 70.7 us -> 84 us
  starting transfers between devices: 40 us -> 29.4 us
  Pallas kernels: 66.9 us -> 61 us
  local copies, waits for them, and re-layouts: 5.33 us -> 1.95 us
    ppermute x4 -> x3, waiting for transfers between devices: 53.9 us -> 67.2 us  [send_up(): return lax.ppermute(value, 'col', [(p, p + 1) for p in range(count - 1)])]
    ppermute x4 -> x3, starting transfers between devices: 30.4 us -> 22 us  [send_down(): return lax.ppermute(value, 'col', [(p, p - 1) for p in range(1, count)])]
    pallas_call x4, Pallas kernels: 18.6 us -> 13.4 us  [the longest x1 6.63 us: last_turn(): pl.pallas_call(last_turn_kernel, in_specs=in_vmem(3 + len(moved)), out_sp...]
    unnamed x4 -> x2, local copies, waits for them, and re-layouts: 4.04 us -> 0.65 us
    ppermute x4 -> x3, starting transfers between devices: 8 us -> 5.75 us  [send_up(): return lax.ppermute(value, 'col', [(p, p + 1) for p in range(count - 1)])]
  transfers between devices with their start and end apart: 12 -> 10, of which waited for: 8 -> 9; matrix products, arithmetic and copies ran while one was open for 0% -> 0% of each run, Pallas kernels for 11% -> 10%
where the time goes in v4:
time: 285 us; the launch traced here: 283 us
  blocking collectives  106 us (37%)
  waiting for transfers between devices  84 us (29%)
  Pallas kernels  61 us (21%)
  starting transfers between devices  29.4 us (10%)
    all_to_all x1, blocking collectives, local(): lax.all_to_all(ordered, 'col', split_axis=0, concat_axis=0, tiled=True)  106 us
    ppermute x3, waiting for transfers between devices, send_up(): return lax.ppermute(value, 'col', [(p, p + 1) for p in range(count - 1)])  67.2 us
    pallas_call x2, Pallas kernels, pair_rotation(): pl.pallas_call(rotation_kernel, in_specs=[pl.BlockSpec(memory_space=pltpu...  31 us
    ppermute x3, starting transfers between devices, send_down(): return lax.ppermute(value, 'col', [(p, p - 1) for p in range(1, count)])  22 us
    ppermute x4, waiting for transfers between devices, row_parts(): parts = (packed, lax.ppermute(packed, 'row', swap))  14.1 us
    pallas_call x2, Pallas kernels, turn(): pl.pallas_call(functools.partial(turn_kernel, start), in_specs=[pl.BlockS...  6.88 us
    pallas_call x1, Pallas kernels, last_turn(): pl.pallas_call(last_turn_kernel, in_specs=in_vmem(3 + len(moved)), out_sp...  6.63 us
    ppermute x3, starting transfers between devices, send_up(): return lax.ppermute(value, 'col', [(p, p + 1) for p in range(count - 1)])  5.75 us
  transfers between devices with their start and end apart: 10, of which 9 were waited for; matrix products, arithmetic and copies ran while one was open for 0% of the time, Pallas kernels for 10%

profile of v4, /device:TPU:32, one launch (start us, length us, event | category | flops | bytes accessed | tf_op | source)
XLA Modules:
  0.0 282.8 jit_solution(2375655523418675382)
XLA Ops:
  0.7 4.5 %order.1 = f32[32,256,256]{2,1,0:T(8,128)S(1)} custom-call(s32[64]{0:T(128)S(1)} %copy-done, f32[256,8192]{1,0:T(8,128)} %diffs_ref.1), custom_call_target="tpu_custom_call" | custom-call | tf_op jit(solution)/shard_map/order/pallas_call | solution.py:69
  5.2 106.0 %all_to_all.5 = f32[32,256,256]{2,1,0:T(8,128)} all-to-all(f32[32,256,256]{2,1,0:T(8,128)S(1)} %order.1), channel_id=1, replica_groups=mesh['col'=32,'row'=4] {'col'}, dimensions={0} | all-to-all | bytes 16777216 | tf_op jit(solution)/shard_map/all_to_all | solution.py:480
  111.2 5.2 %gram.1 = f32[384,128]{1,0:T(8,128)S(1)} custom-call(f32[8192,256]{1,0:T(8,128)} %bitcast.12), custom_call_target="tpu_custom_call" | custom-call | flops 1000 | bytes 1000 | tf_op jit(solution)/shard_map/gram/pallas_call | solution.py:128
  116.5 1.4 collective-permute-done
  120.0 5.0 %collective-permute-done.1.two_ref = f32[384,128]{1,0:T(8,128)S(1)} collective-permute-done((f32[384,128]{1,0:T(8,128)S(1)}, f32[384,128]{1,0:T(8,128)S(1)}, u32[]{:S(2)}, u32[]{:S(2)}) %collective-permute-start.1) | collective-permute-done | bytes 196640 | tf_op jit(solution)/shard_map/ppermute | solution.py:199
  125.0 5.0 %collective-permute-start.3 = (f32[1024,256]{1,0:T(8,128)S(1)}, f32[1024,256]{1,0:T(8,128)S(1)}, u32[]{:S(2)}, u32[]{:S(2)}) collective-permute-start(f32[1024,256]{1,0:T(8,128)S(1)} %bitcast.8), channel_id=1, source_target_pairs={{4,0},{8,4},{12,8},{16,12},{20,16},{24,20},{28,24},{32,28},{36,32}... | collective-permute-start | bytes 3145736 | tf_op jit(solution)/shard_map/ppermute | solution.py:469
  130.0 1.9 collective-permute-start.2
  132.0 15.5 %rotation.2 = (f32[128,256]{1,0:T(8,128)S(1)}, f32[128,256]{1,0:T(8,128)S(1)}) custom-call(s32[1]{0:T(128)S(1)} %bitcast.11, f32[384,128]{1,0:T(8,128)S(1)} %add.6.one_ref, f32[384,128]{1,0:T(8,128)S(1)} %collective-permute-done.1.two_ref), custom_call_target="tpu_custom_call" | custom-call | flops 1000 | bytes 1000 | tf_op jit(solution)/shard_map/rotation/pallas_call | solution.py:327
  147.5 4.4 %turn.2 = (f32[5376,128]{1,0:T(8,128)S(1)}, f32[5376,128]{1,0:T(8,128)S(1)}) custom-call(f32[8192,256]{1,0:T(8,128)} %bitcast.13, f32[128,256]{1,0:T(8,128)S(1)} %get-tuple-element.24.one_ref, f32[128,256]{1,0:T(8,128)S(1)} %get-tuple-element.25.two_ref), custom_call_target="tpu_custom_call" | custom-call | flops 2013265920 | bytes 10485760 | tf_op jit(solution)/shard_map/turn/pallas_call | solution.py:368
  151.9 8.6 %collective-permute-done.2.below_ref = f32[1024,256]{1,0:T(8,128)S(1)} collective-permute-done((f32[1024,256]{1,0:T(8,128)S(1)}, f32[1024,256]{1,0:T(8,128)S(1)}, u32[]{:S(2)}, u32[]{:S(2)}) %collective-permute-start.2) | collective-permute-done | bytes 1048608 | tf_op jit(solution)/shard_map/ppermute | solution.py:464
  160.5 1.9 collective-permute-start.4
  162.4 8.4 %collective-permute-start.5 = (f32[5376,128]{1,0:T(8,128)S(1)}, f32[5376,128]{1,0:T(8,128)S(1)}, u32[]{:S(2)}, u32[]{:S(2)}) collective-permute-start(f32[5376,128]{1,0:T(8,128)S(1)} %get-tuple-element.32.refs_1_), channel_id=1, source_target_pairs={{4,0},{8,4},{12,8},{16,12},{20,16},{24,20},{28,24},{32,28},{36,32}... | collective-permute-start | bytes 8257544 | tf_op jit(solution)/shard_map/ppermute | solution.py:469
  170.9 2.5 turn.3
  173.4 1.9 collective-permute-start.6
  175.3 8.6 %collective-permute-start.7 = (f32[2048,128]{1,0:T(8,128)S(1)}, f32[2048,128]{1,0:T(8,128)S(1)}, u32[]{:S(2)}, u32[]{:S(2)}) collective-permute-start(f32[2048,128]{1,0:T(8,128)S(1)} %get-tuple-element.35.refs_1_.refs_5_), channel_id=1, source_target_pairs={{4,0},{8,4},{12,8},{16,12},{20,16},{24,20},{28,24},{32,28},{36,32}... | collective-permute-start | bytes 3145736 | tf_op jit(solution)/shard_map/ppermute | solution.py:469
  183.9 45.6 %collective-permute-done.4.refs_0_ = f32[5376,128]{1,0:T(8,128)S(1)} collective-permute-done((f32[5376,128]{1,0:T(8,128)S(1)}, f32[5376,128]{1,0:T(8,128)S(1)}, u32[]{:S(2)}, u32[]{:S(2)}) %collective-permute-start.4) | collective-permute-done | bytes 2752544 | tf_op jit(solution)/shard_map/ppermute | solution.py:464
  229.5 1.5 collective-permute-done.5.refs_2_
  231.0 1.9 raw_gram.1
  232.9 3.2 %moved_gram.2.before_ref = f32[384,128]{1,0:T(8,128)S(1)} custom-call(s32[2]{0:T(128)S(1)} %add_convert_fusion.ends, f32[384,128]{1,0:T(8,128)S(1)} %get-tuple-element.33.before_ref, f32[5376,128]{1,0:T(8,128)S(1)} %collective-permute-done.4.refs_0_, f32[5376,128]{1,0:T(8,128)S(1)} %get-tuple-element.32.refs_1_, ...), custom_call_target="tpu_custom_call" | custom-call | flops 2113929216 | bytes 11010048 | tf_op jit(solution)/shard_map/moved_gram/pallas_call | solution.py:182
  236.0 13.0 %collective-permute-done.6.refs_0_.refs_4_ = f32[2048,128]{1,0:T(8,128)S(1)} collective-permute-done((f32[2048,128]{1,0:T(8,128)S(1)}, f32[2048,128]{1,0:T(8,128)S(1)}, u32[]{:S(2)}, u32[]{:S(2)}) %collective-permute-start.6) | collective-permute-done | bytes 1048608 | tf_op jit(solution)/shard_map/ppermute | solution.py:464
  250.2 1.7 moved_gram.3
  254.2 6.3 %collective-permute-done.9.two_ref = f32[384,128]{1,0:T(8,128)S(1)} collective-permute-done((f32[384,128]{1,0:T(8,128)S(1)}, f32[384,128]{1,0:T(8,128)S(1)}, u32[]{:S(2)}, u32[]{:S(2)}) %collective-permute-start.9) | collective-permute-done | bytes 196640 | tf_op jit(solution)/shard_map/ppermute | solution.py:199
  260.5 15.5 %rotation.3 = (f32[128,256]{1,0:T(8,128)S(1)}, f32[128,256]{1,0:T(8,128)S(1)}) custom-call(s32[1]{0:T(128)} %constant.11.clone.1.swap_ref, f32[384,128]{1,0:T(8,128)S(1)} %add.7.one_ref, f32[384,128]{1,0:T(8,128)S(1)} %collective-permute-done.9.two_ref), custom_call_target="tpu_custom_call" | custom-call | flops 1000 | bytes 1000 | tf_op jit(solution)/shard_map/rotation/pallas_call | solution.py:327
  276.0 6.6 %last_turn.1 = f32[8192,256]{1,0:T(8,128)} custom-call(s32[2]{0:T(128)S(1)} %add_convert_fusion.ends, f32[128,256]{1,0:T(8,128)S(1)} %get-tuple-element.36.one_ref, f32[128,256]{1,0:T(8,128)S(1)} %get-tuple-element.37.two_ref, f32[1024,256]{1,0:T(8,128)S(1)} %get-tuple-element.38.raw_ref, f32[5376,128]{1,0:T(8,128)S(1)} %collective-permute-done.4.refs_0_, ...), custom_call_target="tpu_custom_call" | custom-call | flops 3221225472 | bytes 16777216 | tf_op jit(solution)/shard_map/last_turn/pallas_call | solution.py:447
  (13 shorter events, 6.3 us)
Async XLA Ops:
  0.0 0.7 copy-start
  116.4 1.5 collective-permute-start
  118.0 7.0 %collective-permute-start.1 = (f32[384,128]{1,0:T(8,128)S(1)}, f32[384,128]{1,0:T(8,128)S(1)}, u32[]{:S(2)}, u32[]{:S(2)}) collective-permute-start(f32[384,128]{1,0:T(8,128)S(1)} %add.6.one_ref), channel_id=1, source_target_pairs={{0,2},{1,3},{2,0},{3,1},{4,6},{5,7},{6,4},{7,5},{8,10},{9,11},{10,... | collective-permute-start | bytes 589832 | tf_op jit(solution)/shard_map/ppermute | solution.py:199
  125.0 26.9 %collective-permute-start.3 = (f32[1024,256]{1,0:T(8,128)S(1)}, f32[1024,256]{1,0:T(8,128)S(1)}, u32[]{:S(2)}, u32[]{:S(2)}) collective-permute-start(f32[1024,256]{1,0:T(8,128)S(1)} %bitcast.8), channel_id=1, source_target_pairs={{4,0},{8,4},{12,8},{16,12},{20,16},{24,20},{28,24},{32,28},{36,32}... | collective-permute-start | bytes 3145736 | tf_op jit(solution)/shard_map/ppermute | solution.py:469
  130.0 30.5 %collective-permute-start.2 = (f32[1024,256]{1,0:T(8,128)S(1)}, f32[1024,256]{1,0:T(8,128)S(1)}, u32[]{:S(2)}, u32[]{:S(2)}) collective-permute-start(f32[1024,256]{1,0:T(8,128)S(1)} %bitcast.9), channel_id=1, source_target_pairs={{0,4},{4,8},{8,12},{12,16},{16,20},{20,24},{24,28},{28,32},{32,36}... | collective-permute-start | bytes 3145736 | tf_op jit(solution)/shard_map/ppermute | solution.py:464
  160.5 69.0 %collective-permute-start.4 = (f32[5376,128]{1,0:T(8,128)S(1)}, f32[5376,128]{1,0:T(8,128)S(1)}, u32[]{:S(2)}, u32[]{:S(2)}) collective-permute-start(f32[5376,128]{1,0:T(8,128)S(1)} %get-tuple-element.31.refs_3_), channel_id=1, source_target_pairs={{0,4},{4,8},{8,12},{12,16},{16,20},{20,24},{24,28},{28,32},{32,36}... | collective-permute-start | bytes 8257544 | tf_op jit(solution)/shard_map/ppermute | solution.py:464
  162.4 68.5 %collective-permute-start.5 = (f32[5376,128]{1,0:T(8,128)S(1)}, f32[5376,128]{1,0:T(8,128)S(1)}, u32[]{:S(2)}, u32[]{:S(2)}) collective-permute-start(f32[5376,128]{1,0:T(8,128)S(1)} %get-tuple-element.32.refs_1_), channel_id=1, source_target_pairs={{4,0},{8,4},{12,8},{16,12},{20,16},{24,20},{28,24},{32,28},{36,32}... | collective-permute-start | bytes 8257544 | tf_op jit(solution)/shard_map/ppermute | solution.py:469
  173.4 75.7 %collective-permute-start.6 = (f32[2048,128]{1,0:T(8,128)S(1)}, f32[2048,128]{1,0:T(8,128)S(1)}, u32[]{:S(2)}, u32[]{:S(2)}) collective-permute-start(f32[2048,128]{1,0:T(8,128)S(1)} %get-tuple-element.34.refs_3_.refs_7_), channel_id=1, source_target_pairs={{0,4},{4,8},{8,12},{12,16},{16,20},{20,24},{24,28},{28,32},{32,36}... | collective-permute-start | bytes 3145736 | tf_op jit(solution)/shard_map/ppermute | solution.py:464
  175.3 74.9 %collective-permute-start.7 = (f32[2048,128]{1,0:T(8,128)S(1)}, f32[2048,128]{1,0:T(8,128)S(1)}, u32[]{:S(2)}, u32[]{:S(2)}) collective-permute-start(f32[2048,128]{1,0:T(8,128)S(1)} %get-tuple-element.35.refs_1_.refs_5_), channel_id=1, source_target_pairs={{4,0},{8,4},{12,8},{16,12},{20,16},{24,20},{28,24},{32,28},{36,32}... | collective-permute-start | bytes 3145736 | tf_op jit(solution)/shard_map/ppermute | solution.py:469
  251.9 1.5 collective-permute-start.8
  253.5 7.0 %collective-permute-start.9 = (f32[384,128]{1,0:T(8,128)S(1)}, f32[384,128]{1,0:T(8,128)S(1)}, u32[]{:S(2)}, u32[]{:S(2)}) collective-permute-start(f32[384,128]{1,0:T(8,128)S(1)} %add.7.one_ref), channel_id=1, source_target_pairs={{0,2},{1,3},{2,0},{3,1},{4,6},{5,7},{6,4},{7,5},{8,10},{9,11},{10,... | collective-permute-start | bytes 589832 | tf_op jit(solution)/shard_map/ppermute | solution.py:199

commit v5 on v4

--- a/solution.py
+++ b/solution.py
@@ -10,7 +10,8 @@
 BLOCK = 128
 WIDTH = 2 * BLOCK
 TILE = 1024
-CHUNKS = (5 * TILE, 2 * TILE)
+RAW = 1536
+CHUNKS = (4608, 2048)
 STRIP = 64
 PANEL = 32
 SUB = 8
@@ -89,10 +90,26 @@
     cross_ref[...] += lax.dot_general(high, low, COLUMNS, preferred_element_type=F32)
 
 
-def row_copy(source_ref, rows_ref, sems, tile, first=0):
-    source = source_ref.at[pl.ds(pl.multiple_of((tile + first) * TILE, TILE), TILE), :]
-    rows = rows_ref.at[pl.ds(pl.multiple_of(tile * TILE, TILE), TILE), :]
-    return pltpu.make_async_copy(source, rows, sems.at[tile])
+def for_tiles(rows, body):
+    tiles, rest = divmod(rows, TILE)
+
+    @pl.loop(0, tiles)
+    def _(tile):
+        body(pl.multiple_of(tile * TILE, TILE), TILE, tile)
+
+    if rest:
+        body(tiles * TILE, rest, tiles)
+
+
+def row_copy(source_ref, rows_ref, sems, row, size, tile, start=0):
+    source = source_ref.at[pl.ds(pl.multiple_of(row + start, BLOCK), size), :]
+    return pltpu.make_async_copy(source, rows_ref.at[pl.ds(row, size), :], sems.at[tile])
+
+
+def start_rows(source_ref, rows_ref, sems, start=0):
+    for tile, row in enumerate(range(0, rows_ref.shape[0], TILE)):
+        size = min(TILE, rows_ref.shape[0] - row)
+        row_copy(source_ref, rows_ref, sems, row, size, tile, start).start()
 
 
 def pack(total_ref, cross_ref):
@@ -107,18 +124,15 @@
 
 
 def gram_kernel(source_ref, out_ref, total_ref, cross_ref, rows_ref, sems):
-    tiles = rows_ref.shape[0] // TILE
-    for tile in range(tiles):
-        row_copy(source_ref, rows_ref, sems, tile).start()
+    start_rows(source_ref, rows_ref, sems)
     total_ref[...] = jnp.zeros_like(total_ref)
     cross_ref[...] = jnp.zeros_like(cross_ref)
 
-    @pl.loop(0, tiles)
-    def _(tile):
-        row_copy(source_ref, rows_ref, sems, tile).wait()
-        rows = rows_ref[pl.ds(pl.multiple_of(tile * TILE, TILE), TILE), :]
-        add_gram(rows, total_ref, cross_ref)
-
+    def add(row, size, tile):
+        row_copy(source_ref, rows_ref, sems, row, size, tile).wait()
+        add_gram(rows_ref[pl.ds(row, size), :], total_ref, cross_ref)
+
+    for_tiles(rows_ref.shape[0], add)
     out_ref[...] = pack(total_ref, cross_ref)
 
 
@@ -156,19 +170,19 @@
     return upper, lower
 
 
-def moved_tile(ends, moved_refs, tile):
-    upper, lower = moved_rows(ends, moved_refs, pl.multiple_of(tile * TILE, TILE), TILE)
-    return jnp.concatenate([upper, lower], axis=1)
-
-
-def moved_gram_kernel(ends, before_ref, *refs):
+def moved_tile(ends, moved_refs, row, size):
+    return jnp.concatenate(moved_rows(ends, moved_refs, row, size), axis=1)
+
+
+def moved_gram_kernel(rows, ends, before_ref, *refs):
     moved_refs, (out_ref, total_ref, cross_ref) = refs[:4], refs[4:]
     total_ref[...] = jnp.zeros_like(total_ref)
     cross_ref[...] = jnp.zeros_like(cross_ref)
 
-    @pl.loop(0, moved_refs[0].shape[0] // TILE)
-    def _(tile):
-        add_gram(moved_tile(ends, moved_refs, tile), total_ref, cross_ref)
+    def add(row, size, tile):
+        add_gram(moved_tile(ends, moved_refs, row, size), total_ref, cross_ref)
+
+    for_tiles(rows, add)
 
     out_ref[...] = before_ref[...] + pack(total_ref, cross_ref)
 
@@ -178,15 +192,15 @@
     return [pl.BlockSpec(memory_space=pltpu.SMEM)] + [whole] * count
 
 
-def moved_gram(ends, before, moved):
-    return pl.pallas_call(
-        moved_gram_kernel,
+def moved_gram(ends, before, moved, chunk):
+    return pl.pallas_call(
+        functools.partial(moved_gram_kernel, chunk),
         in_specs=in_vmem(5),
         out_specs=pl.BlockSpec(memory_space=pltpu.VMEM),
         out_shape=jax.ShapeDtypeStruct((3 * BLOCK, BLOCK), F32),
         scratch_shapes=[pltpu.VMEM((WIDTH, WIDTH), F32)] * 2,
         compiler_params=grant(24),
-        cost_estimate=cost(moved[0].shape[0]),
+        cost_estimate=cost(chunk),
         name="moved_gram",
     )(ends, before, *moved)
 
@@ -344,9 +358,7 @@
 
 
 def turn_kernel(start, source_ref, one_ref, two_ref, first_ref, second_ref, rows_ref, sems):
-    tiles = rows_ref.shape[0] // TILE
-    for tile in range(tiles):
-        row_copy(source_ref, rows_ref, sems, tile, start // TILE).start()
+    start_rows(source_ref, rows_ref, sems, start)
     rotation_t = jnp.concatenate([one_ref[...], two_ref[...]])
     if first_ref.shape[0] > rows_ref.shape[0]:
         for half_ref, out_ref in ((one_ref, first_ref), (two_ref, second_ref)):
@@ -354,13 +366,14 @@
             out_ref[end : end + BLOCK, :] = half_ref[:, :BLOCK]
             out_ref[end + BLOCK :, :] = half_ref[:, BLOCK:]
 
-    @pl.loop(0, tiles)
-    def _(tile):
-        row_copy(source_ref, rows_ref, sems, tile, start // TILE).wait()
-        rows = pl.ds(pl.multiple_of(tile * TILE, TILE), TILE)
+    def put(row, size, tile):
+        row_copy(source_ref, rows_ref, sems, row, size, tile, start).wait()
+        rows = pl.ds(row, size)
         turned = product(rows_ref[rows, :], rotation_t)
         first_ref[rows, :] = turned[:, :BLOCK]
         second_ref[rows, :] = turned[:, BLOCK:]
+
+    for_tiles(rows_ref.shape[0], put)
 
 
 def turn(pair_rows, rotation_t, start, rows, extra):
@@ -372,10 +385,10 @@
         out_shape=[jax.ShapeDtypeStruct((rows + extra, BLOCK), F32)] * 2,
         scratch_shapes=[
             pltpu.VMEM((rows, WIDTH), F32),
-            pltpu.SemaphoreType.DMA((rows // TILE,)),
+            pltpu.SemaphoreType.DMA((pl.cdiv(rows, TILE),)),
         ],
         compiler_params=grant(24),
-        cost_estimate=cost(rows),
+        cost_estimate=cost(rows if extra else 1000 * rows),
         name="turn",
     )(in_hbm(pair_rows), *rotation_t)
 
@@ -388,12 +401,17 @@
         jnp.concatenate([half[:BLOCK], half[BLOCK:]], axis=1)
         for half in moved_rows(ends, moved_refs, CHUNKS[0], WIDTH)
     ]
-    own = own_ref[...]
-    upper = product(jnp.where(ends[0] == 1, own, below_ref[...]), halves_t[0])
-    lower = product(jnp.where(ends[1] == 1, own, above_ref[...]), halves_t[1])
-    tile = jnp.concatenate([upper, lower], axis=1)
-    out_ref[...] = tile
-    add_gram(tile, total_ref, cross_ref)
+
+    def put(row, size, tile):
+        rows = pl.ds(row, size)
+        own = own_ref[rows, :]
+        upper = product(jnp.where(ends[0] == 1, own, below_ref[rows, :]), halves_t[0])
+        lower = product(jnp.where(ends[1] == 1, own, above_ref[rows, :]), halves_t[1])
+        turned = jnp.concatenate([upper, lower], axis=1)
+        out_ref[rows, :] = turned
+        add_gram(turned, total_ref, cross_ref)
+
+    for_tiles(RAW, put)
     packed_ref[...] = pack(total_ref, cross_ref)
 
 
@@ -404,12 +422,12 @@
         in_specs=in_vmem(7),
         out_specs=[whole, whole],
         out_shape=[
-            jax.ShapeDtypeStruct((TILE, WIDTH), F32),
+            jax.ShapeDtypeStruct((RAW, WIDTH), F32),
             jax.ShapeDtypeStruct((3 * BLOCK, BLOCK), F32),
         ],
         scratch_shapes=[pltpu.VMEM((WIDTH, WIDTH), F32)] * 2,
         compiler_params=grant(24),
-        cost_estimate=cost(2 * TILE),
+        cost_estimate=cost(2 * RAW),
         name="raw_gram",
     )(ends, below, above, own, *moved)
 
@@ -418,31 +436,35 @@
     moved, (out_ref, turned_ref, sems) = (refs[0:4], refs[4:8]), refs[8:]
     rotation_t = jnp.concatenate([one_ref[...], two_ref[...]])
 
-    def out_copy(tile):
-        rows = pl.ds(pl.multiple_of(tile * TILE, TILE), TILE)
-        return pltpu.make_async_copy(turned_ref.at[rows, :], out_ref.at[rows, :], sems.at[tile])
-
-    def put(tile, rows):
-        turned_ref[pl.ds(pl.multiple_of(tile * TILE, TILE), TILE), :] = product(rows, rotation_t)
-        out_copy(tile).start()
-
-    put(0, raw_ref[...])
-    done = 1
-    for moved_refs, rows in zip(moved, CHUNKS):
-
-        @pl.loop(0, rows // TILE)
-        def _(tile, moved_refs=moved_refs, done=done):
-            put(done + tile, moved_tile(ends, moved_refs, tile))
-
-        done += rows // TILE
-
-    @pl.loop(0, done)
-    def _(tile):
-        out_copy(tile).wait()
+    def out_copy(row, size, sem):
+        rows = pl.ds(pl.multiple_of(row, BLOCK), size)
+        return pltpu.make_async_copy(turned_ref.at[rows, :], out_ref.at[rows, :], sems.at[sem])
+
+    start, sem = 0, 0
+    copies = []
+    for moved_refs, count in zip((None, *moved), (RAW, *CHUNKS)):
+
+        def put(row, size, tile, moved_refs=moved_refs, start=start, sem=sem):
+            if moved_refs is None:
+                rows = raw_ref[pl.ds(row, size), :]
+            else:
+                rows = moved_tile(ends, moved_refs, row, size)
+            at = pl.ds(pl.multiple_of(start + row, BLOCK), size)
+            turned_ref[at, :] = product(rows, rotation_t)
+            out_copy(start + row, size, sem + tile).start()
+
+        for_tiles(count, put)
+        for row in range(0, count, TILE):
+            copies.append((start + row, min(TILE, count - row), sem))
+            sem += 1
+        start += count
+    for copy in copies:
+        out_copy(*copy).wait()
 
 
 def last_turn(ends, rotation_t, raw, moved):
-    rows = TILE + sum(CHUNKS)
+    rows = RAW + sum(CHUNKS)
+    tiles = sum(pl.cdiv(count, TILE) for count in (RAW, *CHUNKS))
     moved = [array for part in moved for array in part]
     return pl.pallas_call(
         last_turn_kernel,
@@ -451,7 +473,7 @@
         out_shape=jax.ShapeDtypeStruct((rows, WIDTH), F32),
         scratch_shapes=[
             pltpu.VMEM((rows, WIDTH), F32),
-            pltpu.SemaphoreType.DMA((rows // TILE,)),
+            pltpu.SemaphoreType.DMA((tiles,)),
         ],
         compiler_params=grant(24),
         cost_estimate=cost(rows),
@@ -481,19 +503,19 @@
     pair_rows = pair_rows.reshape(rows, WIDTH)
 
     parts = row_parts(local_gram(pair_rows))
-    *parts, own = lax.optimization_barrier((*parts, pair_rows[:TILE]))
+    *parts, own = lax.optimization_barrier((*parts, pair_rows[:RAW]))
     below, above = send_up(own), send_down(own)
     rotation_t = pair_rotation(ends[:1], parts)
-    moved, start = [], TILE
-    for chunk, count in enumerate(CHUNKS):
-        first, second = turn(pair_rows, rotation_t, start, count, 0 if chunk else WIDTH)
-        if chunk == 0:
+    moved, start = [], RAW
+    for number, chunk in enumerate(CHUNKS):
+        first, second = turn(pair_rows, rotation_t, start, chunk, 0 if number else WIDTH)
+        if number == 1:
             first, second, below, above = lax.optimization_barrier((first, second, below, above))
         moved.append((send_up(first), second, send_down(second), first))
-        start += count
+        start += chunk
     raw, gram = raw_gram(ends, below, above, own, moved[0])
-    for part in moved:
-        gram = moved_gram(ends, gram, part)
+    for part, chunk in zip(moved, CHUNKS):
+        gram = moved_gram(ends, gram, part, chunk)
     rotation_t = pair_rotation(jnp.zeros((1,), jnp.int32), row_parts(gram))
     return last_turn(ends, rotation_t, raw, moved).reshape(col_count, 1, local_rows, WIDTH)
 

time: 285 us -> 284 us (level)
  waiting for transfers between devices: 84 us -> 69.5 us
  Pallas kernels: 61 us -> 75 us
    ppermute x3, waiting for transfers between devices: 67.2 us -> 56.8 us  [send_up(): return lax.ppermute(value, 'col', [(p, p + 1) for p in range(count - 1)])]
    pallas_call x1, Pallas kernels: 1.89 us -> 7.26 us  [raw_gram(): pl.pallas_call(raw_gram_kernel, in_specs=in_vmem(7), out_specs=[whole, wh...]
    pallas_call x1, Pallas kernels: 6.63 us -> 10 us  [last_turn(): pl.pallas_call(last_turn_kernel, in_specs=in_vmem(3 + len(moved)), out_sp...]
    pallas_call x2, Pallas kernels: 4.84 us -> 8 us  [moved_gram(): pl.pallas_call(functools.partial(moved_gram_kernel, chunk), in_specs=in_v...]
  transfers between devices with their start and end apart: 10 -> 10, of which waited for: 9 -> 7; matrix products, arithmetic and copies ran while one was open for 0% -> 1% of each run, Pallas kernels for 10% -> 13%
where the time goes in v5:
time: 284 us
  blocking collectives  106 us (37%)
  Pallas kernels  75 us (26%)
  waiting for transfers between devices  69.5 us (24%)
  starting transfers between devices  29.4 us (10%)
  local copies, waits for them, and re-layouts  3.4 us (1%)
    all_to_all x1, blocking collectives, local(): lax.all_to_all(ordered, 'col', split_axis=0, concat_axis=0, tiled=True)  106 us
    ppermute x3, waiting for transfers between devices, send_up(): return lax.ppermute(value, 'col', [(p, p + 1) for p in range(count - 1)])  56.8 us
    pallas_call x2, Pallas kernels, pair_rotation(): pl.pallas_call(rotation_kernel, in_specs=[pl.BlockSpec(memory_space=pltpu...  31 us
    ppermute x3, starting transfers between devices, send_down(): return lax.ppermute(value, 'col', [(p, p - 1) for p in range(1, count)])  21.9 us
    ppermute x4, waiting for transfers between devices, row_parts(): parts = (packed, lax.ppermute(packed, 'row', swap))  12.6 us
    pallas_call x1, Pallas kernels, last_turn(): pl.pallas_call(last_turn_kernel, in_specs=in_vmem(3 + len(moved)), out_sp...  10 us
    pallas_call x2, Pallas kernels, turn(): pl.pallas_call(functools.partial(turn_kernel, start), in_specs=[pl.BlockS...  8.97 us
    pallas_call x2, Pallas kernels, moved_gram(): pl.pallas_call(functools.partial(moved_gram_kernel, chunk), in_specs=in_v...  8 us
  transfers between devices with their start and end apart: 10, of which 7 were waited for; matrix products, arithmetic and copies ran while one was open for 1% of the time, Pallas kernels for 13%

profile of v5, /device:TPU:32, one launch (start us, length us, event | category | flops | bytes accessed | tf_op | source)
XLA Modules:
  0.0 283.7 jit_solution(4961510898131799376)
XLA Ops:
  0.7 4.5 %order.1 = f32[32,256,256]{2,1,0:T(8,128)S(1)} custom-call(s32[64]{0:T(128)S(1)} %copy-done.2, f32[256,8192]{1,0:T(8,128)} %diffs_ref.1), custom_call_target="tpu_custom_call" | custom-call | tf_op jit(solution)/shard_map/order/pallas_call | solution.py:70
  5.2 106.0 %all_to_all.5 = f32[32,256,256]{2,1,0:T(8,128)} all-to-all(f32[32,256,256]{2,1,0:T(8,128)S(1)} %order.1), channel_id=1, replica_groups=mesh['col'=32,'row'=4] {'col'}, dimensions={0} | all-to-all | bytes 16777216 | tf_op jit(solution)/shard_map/all_to_all | solution.py:502
  111.2 5.2 %gram.1 = f32[384,128]{1,0:T(8,128)S(1)} custom-call(f32[8192,256]{1,0:T(8,128)} %bitcast.9), custom_call_target="tpu_custom_call" | custom-call | flops 1000 | bytes 1000 | tf_op jit(solution)/shard_map/gram/pallas_call | solution.py:142
  116.5 1.4 collective-permute-done
  118.8 2.7 slice.12
  121.6 3.5 %collective-permute-done.1.two_ref = f32[384,128]{1,0:T(8,128)S(1)} collective-permute-done((f32[384,128]{1,0:T(8,128)S(1)}, f32[384,128]{1,0:T(8,128)S(1)}, u32[]{:S(2)}, u32[]{:S(2)}) %collective-permute-start.1) | collective-permute-done | bytes 196640 | tf_op jit(solution)/shard_map/ppermute | solution.py:213
  125.0 5.0 %collective-permute-start.3 = (f32[1536,256]{1,0:T(8,128)}, f32[1536,256]{1,0:T(8,128)}, u32[]{:S(2)}, u32[]{:S(2)}) collective-permute-start(f32[1536,256]{1,0:T(8,128)} %bitcast.3.own_ref), channel_id=1, source_target_pairs={{4,0},{8,4},{12,8},{16,12},{20,16},{24,20},{28,24},{32,28},{36,32}... | collective-permute-start | bytes 4718600 | tf_op jit(solution)/shard_map/ppermute | solution.py:491
  130.0 1.9 collective-permute-start.2
  131.9 15.5 %rotation.2 = (f32[128,256]{1,0:T(8,128)S(1)}, f32[128,256]{1,0:T(8,128)S(1)}) custom-call(s32[1]{0:T(128)S(1)} %bitcast.8, f32[384,128]{1,0:T(8,128)S(1)} %add.6.one_ref, f32[384,128]{1,0:T(8,128)S(1)} %collective-permute-done.1.two_ref), custom_call_target="tpu_custom_call" | custom-call | flops 1000 | bytes 1000 | tf_op jit(solution)/shard_map/rotation/pallas_call | solution.py:341
  147.4 6.5 %turn.3 = (f32[4864,128]{1,0:T(8,128)}, f32[4864,128]{1,0:T(8,128)}) custom-call(f32[8192,256]{1,0:T(8,128)} %bitcast.10, f32[128,256]{1,0:T(8,128)S(1)} %get-tuple-element.24.one_ref, f32[128,256]{1,0:T(8,128)S(1)} %get-tuple-element.25.two_ref), custom_call_target="tpu_custom_call" | custom-call | flops 1811939328 | bytes 9437184 | tf_op jit(solution)/shard_map/turn/pallas_call | solution.py:381
  153.9 2.1 collective-permute-start.4
  156.0 8.3 %collective-permute-start.5 = (f32[4864,128]{1,0:T(8,128)}, f32[4864,128]{1,0:T(8,128)}, u32[]{:S(2)}, u32[]{:S(2)}) collective-permute-start(f32[4864,128]{1,0:T(8,128)} %get-tuple-element.32.refs_1_), channel_id=1, source_target_pairs={{4,0},{8,4},{12,8},{16,12},{20,16},{24,20},{28,24},{32,28},{36,32}... | collective-permute-start | bytes 7471112 | tf_op jit(solution)/shard_map/ppermute | solution.py:491
  164.3 2.5 turn.2
  166.8 7.2 %collective-permute-done.2.below_ref = f32[1536,256]{1,0:T(8,128)} collective-permute-done((f32[1536,256]{1,0:T(8,128)}, f32[1536,256]{1,0:T(8,128)}, u32[]{:S(2)}, u32[]{:S(2)}) %collective-permute-start.2) | collective-permute-done | bytes 1572896 | tf_op jit(solution)/shard_map/ppermute | solution.py:486
  174.1 1.9 collective-permute-start.6
  176.0 8.6 %collective-permute-start.7 = (f32[2048,128]{1,0:T(8,128)S(1)}, f32[2048,128]{1,0:T(8,128)S(1)}, u32[]{:S(2)}, u32[]{:S(2)}) collective-permute-start(f32[2048,128]{1,0:T(8,128)S(1)} %get-tuple-element.35.refs_1_.refs_5_), channel_id=1, source_target_pairs={{4,0},{8,4},{12,8},{16,12},{20,16},{24,20},{28,24},{32,28},{36,32}... | collective-permute-start | bytes 3145736 | tf_op jit(solution)/shard_map/ppermute | solution.py:491
  184.6 42.8 %collective-permute-done.4.refs_0_ = f32[4864,128]{1,0:T(8,128)} collective-permute-done((f32[4864,128]{1,0:T(8,128)}, f32[4864,128]{1,0:T(8,128)}, u32[]{:S(2)}, u32[]{:S(2)}) %collective-permute-start.4) | collective-permute-done | bytes 2490400 | tf_op jit(solution)/shard_map/ppermute | solution.py:486
  227.4 7.3 %raw_gram.1 = (f32[1536,256]{1,0:T(8,128)S(1)}, f32[384,128]{1,0:T(8,128)S(1)}) custom-call(s32[2]{0:T(128)S(1)} %copy-done.1, f32[1536,256]{1,0:T(8,128)} %collective-permute-done.2.below_ref, f32[1536,256]{1,0:T(8,128)} %collective-permute-done.3.above_ref, f32[1536,256]{1,0:T(8,128)} %bitcast.3.own_ref, f32[4864,128]{1,0:T(8,128)} %collective-permute-done.4.refs_0_, ...), custom_call_target="tpu_custom_call" | custom-call | flops 1207959552 | bytes 6291456 | tf_op jit(solution)/shard_map/raw_gram/pallas_call | solution.py:420
  234.7 6.3 %moved_gram.2.before_ref = f32[384,128]{1,0:T(8,128)S(1)} custom-call(s32[2]{0:T(128)S(1)} %copy-done.1, f32[384,128]{1,0:T(8,128)S(1)} %get-tuple-element.33.before_ref, f32[4864,128]{1,0:T(8,128)} %collective-permute-done.4.refs_0_, f32[4864,128]{1,0:T(8,128)} %get-tuple-element.32.refs_1_, f32[4864,128]{1,0:T(8,128)} %collective-permute-done.5.refs_2_, ...), custom_call_target="tpu_custom_call" | custom-call | flops 1811939328 | bytes 9437184 | tf_op jit(solution)/shard_map/moved_gram/pallas_call | solution.py:196
  241.0 6.8 %collective-permute-done.6.refs_0_.refs_4_ = f32[2048,128]{1,0:T(8,128)S(1)} collective-permute-done((f32[2048,128]{1,0:T(8,128)S(1)}, f32[2048,128]{1,0:T(8,128)S(1)}, u32[]{:S(2)}, u32[]{:S(2)}) %collective-permute-start.6) | collective-permute-done | bytes 1048608 | tf_op jit(solution)/shard_map/ppermute | solution.py:486
  247.8 1.7 moved_gram.3
  251.8 6.3 %collective-permute-done.9.two_ref = f32[384,128]{1,0:T(8,128)S(1)} collective-permute-done((f32[384,128]{1,0:T(8,128)S(1)}, f32[384,128]{1,0:T(8,128)S(1)}, u32[]{:S(2)}, u32[]{:S(2)}) %collective-permute-start.9) | collective-permute-done | bytes 196640 | tf_op jit(solution)/shard_map/ppermute | solution.py:213
  258.1 15.5 %rotation.3 = (f32[128,256]{1,0:T(8,128)S(1)}, f32[128,256]{1,0:T(8,128)S(1)}) custom-call(s32[1]{0:T(128)} %constant.11.clone.1.swap_ref, f32[384,128]{1,0:T(8,128)S(1)} %add.7.one_ref, f32[384,128]{1,0:T(8,128)S(1)} %collective-permute-done.9.two_ref), custom_call_target="tpu_custom_call" | custom-call | flops 1000 | bytes 1000 | tf_op jit(solution)/shard_map/rotation/pallas_call | solution.py:341
  273.6 10.0 %last_turn.1 = f32[8192,256]{1,0:T(8,128)} custom-call(s32[2]{0:T(128)S(1)} %copy-done.1, f32[128,256]{1,0:T(8,128)S(1)} %get-tuple-element.36.one_ref, f32[128,256]{1,0:T(8,128)S(1)} %get-tuple-element.37.two_ref, f32[1536,256]{1,0:T(8,128)S(1)} %get-tuple-element.38.raw_ref, f32[4864,128]{1,0:T(8,128)} %collective-permute-done.4.refs_0_, ...), custom_call_target="tpu_custom_call" | custom-call | flops 3221225472 | bytes 16777216 | tf_op jit(solution)/shard_map/last_turn/pallas_call | solution.py:469
  (17 shorter events, 3.8 us)
Async XLA Ops:
  0.0 0.7 copy-start.2
  116.4 1.5 collective-permute-start
  118.0 7.0 %collective-permute-start.1 = (f32[384,128]{1,0:T(8,128)S(1)}, f32[384,128]{1,0:T(8,128)S(1)}, u32[]{:S(2)}, u32[]{:S(2)}) collective-permute-start(f32[384,128]{1,0:T(8,128)S(1)} %add.6.one_ref), channel_id=1, source_target_pairs={{0,2},{1,3},{2,0},{3,1},{4,6},{5,7},{6,4},{7,5},{8,10},{9,11},{10,... | collective-permute-start | bytes 589832 | tf_op jit(solution)/shard_map/ppermute | solution.py:213
  118.8 35.1 %copy-start = (s32[2]{0:T(128)}, s32[2]{0:T(128)S(1)}, u32[]{:S(2)}) copy-start(s32[2]{0:T(128)S(1)} %add_convert_fusion.ends) | copy-start | bytes 28
  125.0 41.8 %collective-permute-start.3 = (f32[1536,256]{1,0:T(8,128)}, f32[1536,256]{1,0:T(8,128)}, u32[]{:S(2)}, u32[]{:S(2)}) collective-permute-start(f32[1536,256]{1,0:T(8,128)} %bitcast.3.own_ref), channel_id=1, source_target_pairs={{4,0},{8,4},{12,8},{16,12},{20,16},{24,20},{28,24},{32,28},{36,32}... | collective-permute-start | bytes 4718600 | tf_op jit(solution)/shard_map/ppermute | solution.py:491
  130.0 44.1 %collective-permute-start.2 = (f32[1536,256]{1,0:T(8,128)}, f32[1536,256]{1,0:T(8,128)}, u32[]{:S(2)}, u32[]{:S(2)}) collective-permute-start(f32[1536,256]{1,0:T(8,128)} %bitcast.3.own_ref), channel_id=1, source_target_pairs={{0,4},{4,8},{8,12},{12,16},{16,20},{20,24},{24,28},{28,32},{32,36}... | collective-permute-start | bytes 4718600 | tf_op jit(solution)/shard_map/ppermute | solution.py:486
  153.9 73.5 %collective-permute-start.4 = (f32[4864,128]{1,0:T(8,128)}, f32[4864,128]{1,0:T(8,128)}, u32[]{:S(2)}, u32[]{:S(2)}) collective-permute-start(f32[4864,128]{1,0:T(8,128)} %get-tuple-element.31.refs_3_), channel_id=1, source_target_pairs={{0,4},{4,8},{8,12},{12,16},{16,20},{20,24},{24,28},{28,32},{32,36}... | collective-permute-start | bytes 7471112 | tf_op jit(solution)/shard_map/ppermute | solution.py:486
  156.0 71.4 %collective-permute-start.5 = (f32[4864,128]{1,0:T(8,128)}, f32[4864,128]{1,0:T(8,128)}, u32[]{:S(2)}, u32[]{:S(2)}) collective-permute-start(f32[4864,128]{1,0:T(8,128)} %get-tuple-element.32.refs_1_), channel_id=1, source_target_pairs={{4,0},{8,4},{12,8},{16,12},{20,16},{24,20},{28,24},{32,28},{36,32}... | collective-permute-start | bytes 7471112 | tf_op jit(solution)/shard_map/ppermute | solution.py:491
  164.3 63.1 %copy-start.1 = (s32[2]{0:T(128)S(1)}, s32[2]{0:T(128)}, u32[]{:S(2)}) copy-start(s32[2]{0:T(128)} %copy-done) | copy-start | bytes 28
  174.1 73.7 %collective-permute-start.6 = (f32[2048,128]{1,0:T(8,128)S(1)}, f32[2048,128]{1,0:T(8,128)S(1)}, u32[]{:S(2)}, u32[]{:S(2)}) collective-permute-start(f32[2048,128]{1,0:T(8,128)S(1)} %get-tuple-element.34.refs_3_.refs_7_), channel_id=1, source_target_pairs={{0,4},{4,8},{8,12},{12,16},{16,20},{20,24},{24,28},{28,32},{32,36}... | collective-permute-start | bytes 3145736 | tf_op jit(solution)/shard_map/ppermute | solution.py:486
  176.0 71.8 %collective-permute-start.7 = (f32[2048,128]{1,0:T(8,128)S(1)}, f32[2048,128]{1,0:T(8,128)S(1)}, u32[]{:S(2)}, u32[]{:S(2)}) collective-permute-start(f32[2048,128]{1,0:T(8,128)S(1)} %get-tuple-element.35.refs_1_.refs_5_), channel_id=1, source_target_pairs={{4,0},{8,4},{12,8},{16,12},{20,16},{24,20},{28,24},{32,28},{36,32}... | collective-permute-start | bytes 3145736 | tf_op jit(solution)/shard_map/ppermute | solution.py:491
  249.5 1.5 collective-permute-start.8
  251.1 7.0 %collective-permute-start.9 = (f32[384,128]{1,0:T(8,128)S(1)}, f32[384,128]{1,0:T(8,128)S(1)}, u32[]{:S(2)}, u32[]{:S(2)}) collective-permute-start(f32[384,128]{1,0:T(8,128)S(1)} %add.7.one_ref), channel_id=1, source_target_pairs={{0,2},{1,3},{2,0},{3,1},{4,6},{5,7},{6,4},{7,5},{8,10},{9,11},{10,... | collective-permute-start | bytes 589832 | tf_op jit(solution)/shard_map/ppermute | solution.py:213

commit v6 on v5

--- a/solution.py
+++ b/solution.py
@@ -388,7 +388,7 @@
             pltpu.SemaphoreType.DMA((pl.cdiv(rows, TILE),)),
         ],
         compiler_params=grant(24),
-        cost_estimate=cost(rows if extra else 1000 * rows),
+        cost_estimate=cost(rows if extra else 30 * rows),
         name="turn",
     )(in_hbm(pair_rows), *rotation_t)
 

time: 284 us -> 280 us (0.986)
  Pallas kernels: 75 us -> 61.2 us
  waiting for transfers between devices: 69.5 us -> 80.9 us
    ppermute x3, waiting for transfers between devices: 56.8 us -> 66.7 us  [send_up(): return lax.ppermute(value, 'col', [(p, p + 1) for p in range(count - 1)])]
    pallas_call x1, Pallas kernels: 7.26 us -> 2.55 us  [raw_gram(): pl.pallas_call(raw_gram_kernel, in_specs=in_vmem(7), out_specs=[whole, wh...]
    pallas_call x2, Pallas kernels: 8 us -> 4.62 us  [moved_gram(): pl.pallas_call(functools.partial(moved_gram_kernel, chunk), in_specs=in_v...]
    pallas_call x1, Pallas kernels: 10 us -> 6.66 us  [last_turn(): pl.pallas_call(last_turn_kernel, in_specs=in_vmem(3 + len(moved)), out_sp...]
  transfers between devices with their start and end apart: 10 -> 10, of which waited for: 7 -> 8; matrix products, arithmetic and copies ran while one was open for 1% -> 1% of each run, Pallas kernels for 13% -> 10%
where the time goes in v6:
time: 280 us
  blocking collectives  106 us (38%)
  waiting for transfers between devices  80.9 us (29%)
  Pallas kernels  61.2 us (22%)
  starting transfers between devices  29.4 us (10%)
    all_to_all x1, blocking collectives, local(): lax.all_to_all(ordered, 'col', split_axis=0, concat_axis=0, tiled=True)  106 us
    ppermute x3, waiting for transfers between devices, send_up(): return lax.ppermute(value, 'col', [(p, p + 1) for p in range(count - 1)])  66.7 us
    pallas_call x2, Pallas kernels, pair_rotation(): pl.pallas_call(rotation_kernel, in_specs=[pl.BlockSpec(memory_space=pltpu...  31 us
    ppermute x3, starting transfers between devices, send_down(): return lax.ppermute(value, 'col', [(p, p - 1) for p in range(1, count)])  21.7 us
    ppermute x4, waiting for transfers between devices, row_parts(): parts = (packed, lax.ppermute(packed, 'row', swap))  13.9 us
    pallas_call x2, Pallas kernels, turn(): pl.pallas_call(functools.partial(turn_kernel, start), in_specs=[pl.BlockS...  6.67 us
    pallas_call x1, Pallas kernels, last_turn(): pl.pallas_call(last_turn_kernel, in_specs=in_vmem(3 + len(moved)), out_sp...  6.66 us
    ppermute x3, starting transfers between devices, send_up(): return lax.ppermute(value, 'col', [(p, p + 1) for p in range(count - 1)])  6.07 us
  transfers between devices with their start and end apart: 10, of which 8 were waited for; matrix products, arithmetic and copies ran while one was open for 1% of the time, Pallas kernels for 10%

profile of v6, /device:TPU:32, one launch (start us, length us, event | category | flops | bytes accessed | tf_op | source)
XLA Modules:
  0.0 280.1 jit_solution(4717479585620224207)
XLA Ops:
  0.7 4.5 %order.1 = f32[32,256,256]{2,1,0:T(8,128)S(1)} custom-call(s32[64]{0:T(128)S(1)} %copy-done, f32[256,8192]{1,0:T(8,128)} %diffs_ref.1), custom_call_target="tpu_custom_call" | custom-call | tf_op jit(solution)/shard_map/order/pallas_call | solution.py:70
  5.2 106.0 %all_to_all.5 = f32[32,256,256]{2,1,0:T(8,128)} all-to-all(f32[32,256,256]{2,1,0:T(8,128)S(1)} %order.1), channel_id=1, replica_groups=mesh['col'=32,'row'=4] {'col'}, dimensions={0} | all-to-all | bytes 16777216 | tf_op jit(solution)/shard_map/all_to_all | solution.py:502
  111.2 5.2 %gram.1 = f32[384,128]{1,0:T(8,128)S(1)} custom-call(f32[8192,256]{1,0:T(8,128)} %bitcast.12), custom_call_target="tpu_custom_call" | custom-call | flops 1000 | bytes 1000 | tf_op jit(solution)/shard_map/gram/pallas_call | solution.py:142
  116.5 1.4 collective-permute-done
  118.8 1.5 slice.12
  120.3 4.7 %collective-permute-done.1.two_ref = f32[384,128]{1,0:T(8,128)S(1)} collective-permute-done((f32[384,128]{1,0:T(8,128)S(1)}, f32[384,128]{1,0:T(8,128)S(1)}, u32[]{:S(2)}, u32[]{:S(2)}) %collective-permute-start.1) | collective-permute-done | bytes 196640 | tf_op jit(solution)/shard_map/ppermute | solution.py:213
  125.0 5.0 %collective-permute-start.3 = (f32[1536,256]{1,0:T(8,128)S(1)}, f32[1536,256]{1,0:T(8,128)S(1)}, u32[]{:S(2)}, u32[]{:S(2)}) collective-permute-start(f32[1536,256]{1,0:T(8,128)S(1)} %bitcast.8), channel_id=1, source_target_pairs={{4,0},{8,4},{12,8},{16,12},{20,16},{24,20},{28,24},{32,28},{36,32}... | collective-permute-start | bytes 4718600 | tf_op jit(solution)/shard_map/ppermute | solution.py:491
  130.0 1.9 collective-permute-start.2
  131.9 15.5 %rotation.2 = (f32[128,256]{1,0:T(8,128)S(1)}, f32[128,256]{1,0:T(8,128)S(1)}) custom-call(s32[1]{0:T(128)S(1)} %bitcast.11, f32[384,128]{1,0:T(8,128)S(1)} %add.6.one_ref, f32[384,128]{1,0:T(8,128)S(1)} %collective-permute-done.1.two_ref), custom_call_target="tpu_custom_call" | custom-call | flops 1000 | bytes 1000 | tf_op jit(solution)/shard_map/rotation/pallas_call | solution.py:341
  147.4 4.2 %turn.3 = (f32[4864,128]{1,0:T(8,128)S(1)}, f32[4864,128]{1,0:T(8,128)S(1)}) custom-call(f32[8192,256]{1,0:T(8,128)} %bitcast.13, f32[128,256]{1,0:T(8,128)S(1)} %get-tuple-element.24.one_ref, f32[128,256]{1,0:T(8,128)S(1)} %get-tuple-element.25.two_ref), custom_call_target="tpu_custom_call" | custom-call | flops 1811939328 | bytes 9437184 | tf_op jit(solution)/shard_map/turn/pallas_call | solution.py:381
  151.6 2.1 collective-permute-start.4
  153.7 8.3 %collective-permute-start.5 = (f32[4864,128]{1,0:T(8,128)S(1)}, f32[4864,128]{1,0:T(8,128)S(1)}, u32[]{:S(2)}, u32[]{:S(2)}) collective-permute-start(f32[4864,128]{1,0:T(8,128)S(1)} %get-tuple-element.32.refs_1_), channel_id=1, source_target_pairs={{4,0},{8,4},{12,8},{16,12},{20,16},{24,20},{28,24},{32,28},{36,32}... | collective-permute-start | bytes 7471112 | tf_op jit(solution)/shard_map/ppermute | solution.py:491
  162.0 2.5 turn.2
  164.8 8.9 %collective-permute-done.2.below_ref = f32[1536,256]{1,0:T(8,128)S(1)} collective-permute-done((f32[1536,256]{1,0:T(8,128)S(1)}, f32[1536,256]{1,0:T(8,128)S(1)}, u32[]{:S(2)}, u32[]{:S(2)}) %collective-permute-start.2) | collective-permute-done | bytes 1572896 | tf_op jit(solution)/shard_map/ppermute | solution.py:486
  173.7 2.1 collective-permute-start.6
  175.8 8.4 %collective-permute-start.7 = (f32[2048,128]{1,0:T(8,128)S(1)}, f32[2048,128]{1,0:T(8,128)S(1)}, u32[]{:S(2)}, u32[]{:S(2)}) collective-permute-start(f32[2048,128]{1,0:T(8,128)S(1)} %get-tuple-element.35.refs_1_.refs_5_), channel_id=1, source_target_pairs={{4,0},{8,4},{12,8},{16,12},{20,16},{24,20},{28,24},{32,28},{36,32}... | collective-permute-start | bytes 3145736 | tf_op jit(solution)/shard_map/ppermute | solution.py:491
  184.3 42.8 %collective-permute-done.4.refs_0_ = f32[4864,128]{1,0:T(8,128)S(1)} collective-permute-done((f32[4864,128]{1,0:T(8,128)S(1)}, f32[4864,128]{1,0:T(8,128)S(1)}, u32[]{:S(2)}, u32[]{:S(2)}) %collective-permute-start.4) | collective-permute-done | bytes 2490400 | tf_op jit(solution)/shard_map/ppermute | solution.py:486
  227.1 2.6 raw_gram.1
  229.7 2.9 %moved_gram.2.before_ref = f32[384,128]{1,0:T(8,128)S(1)} custom-call(s32[2]{0:T(128)S(1)} %add_convert_fusion.ends, f32[384,128]{1,0:T(8,128)S(1)} %get-tuple-element.33.before_ref, f32[4864,128]{1,0:T(8,128)S(1)} %collective-permute-done.4.refs_0_, f32[4864,128]{1,0:T(8,128)S(1)} %get-tuple-element.32.refs_1_, ...), custom_call_target="tpu_custom_call" | custom-call | flops 1811939328 | bytes 9437184 | tf_op jit(solution)/shard_map/moved_gram/pallas_call | solution.py:196
  232.6 15.0 %collective-permute-done.6.refs_0_.refs_4_ = f32[2048,128]{1,0:T(8,128)S(1)} collective-permute-done((f32[2048,128]{1,0:T(8,128)S(1)}, f32[2048,128]{1,0:T(8,128)S(1)}, u32[]{:S(2)}, u32[]{:S(2)}) %collective-permute-start.6) | collective-permute-done | bytes 1048608 | tf_op jit(solution)/shard_map/ppermute | solution.py:486
  247.6 1.7 moved_gram.3
  251.5 6.3 %collective-permute-done.9.two_ref = f32[384,128]{1,0:T(8,128)S(1)} collective-permute-done((f32[384,128]{1,0:T(8,128)S(1)}, f32[384,128]{1,0:T(8,128)S(1)}, u32[]{:S(2)}, u32[]{:S(2)}) %collective-permute-start.9) | collective-permute-done | bytes 196640 | tf_op jit(solution)/shard_map/ppermute | solution.py:213
  257.8 15.5 %rotation.3 = (f32[128,256]{1,0:T(8,128)S(1)}, f32[128,256]{1,0:T(8,128)S(1)}) custom-call(s32[1]{0:T(128)} %constant.11.clone.1.swap_ref, f32[384,128]{1,0:T(8,128)S(1)} %add.7.one_ref, f32[384,128]{1,0:T(8,128)S(1)} %collective-permute-done.9.two_ref), custom_call_target="tpu_custom_call" | custom-call | flops 1000 | bytes 1000 | tf_op jit(solution)/shard_map/rotation/pallas_call | solution.py:341
  273.3 6.7 %last_turn.1 = f32[8192,256]{1,0:T(8,128)} custom-call(s32[2]{0:T(128)S(1)} %add_convert_fusion.ends, f32[128,256]{1,0:T(8,128)S(1)} %get-tuple-element.36.one_ref, f32[128,256]{1,0:T(8,128)S(1)} %get-tuple-element.37.two_ref, f32[1536,256]{1,0:T(8,128)S(1)} %get-tuple-element.38.raw_ref, f32[4864,128]{1,0:T(8,128)S(1)} %collective-permute-done.4.refs_0_, ...), custom_call_target="tpu_custom_call" | custom-call | flops 3221225472 | bytes 16777216 | tf_op jit(solution)/shard_map/last_turn/pallas_call | solution.py:469
  (13 shorter events, 4.2 us)
Async XLA Ops:
  0.0 0.7 copy-start
  116.4 1.5 collective-permute-start
  118.0 7.0 %collective-permute-start.1 = (f32[384,128]{1,0:T(8,128)S(1)}, f32[384,128]{1,0:T(8,128)S(1)}, u32[]{:S(2)}, u32[]{:S(2)}) collective-permute-start(f32[384,128]{1,0:T(8,128)S(1)} %add.6.one_ref), channel_id=1, source_target_pairs={{0,2},{1,3},{2,0},{3,1},{4,6},{5,7},{6,4},{7,5},{8,10},{9,11},{10,... | collective-permute-start | bytes 589832 | tf_op jit(solution)/shard_map/ppermute | solution.py:213
  125.0 39.8 %collective-permute-start.3 = (f32[1536,256]{1,0:T(8,128)S(1)}, f32[1536,256]{1,0:T(8,128)S(1)}, u32[]{:S(2)}, u32[]{:S(2)}) collective-permute-start(f32[1536,256]{1,0:T(8,128)S(1)} %bitcast.8), channel_id=1, source_target_pairs={{4,0},{8,4},{12,8},{16,12},{20,16},{24,20},{28,24},{32,28},{36,32}... | collective-permute-start | bytes 4718600 | tf_op jit(solution)/shard_map/ppermute | solution.py:491
  130.0 43.7 %collective-permute-start.2 = (f32[1536,256]{1,0:T(8,128)S(1)}, f32[1536,256]{1,0:T(8,128)S(1)}, u32[]{:S(2)}, u32[]{:S(2)}) collective-permute-start(f32[1536,256]{1,0:T(8,128)S(1)} %bitcast.9), channel_id=1, source_target_pairs={{0,4},{4,8},{8,12},{12,16},{16,20},{20,24},{24,28},{28,32},{32,36}... | collective-permute-start | bytes 4718600 | tf_op jit(solution)/shard_map/ppermute | solution.py:486
  151.6 75.5 %collective-permute-start.4 = (f32[4864,128]{1,0:T(8,128)S(1)}, f32[4864,128]{1,0:T(8,128)S(1)}, u32[]{:S(2)}, u32[]{:S(2)}) collective-permute-start(f32[4864,128]{1,0:T(8,128)S(1)} %get-tuple-element.31.refs_3_), channel_id=1, source_target_pairs={{0,4},{4,8},{8,12},{12,16},{16,20},{20,24},{24,28},{28,32},{32,36}... | collective-permute-start | bytes 7471112 | tf_op jit(solution)/shard_map/ppermute | solution.py:486
  153.7 73.4 %collective-permute-start.5 = (f32[4864,128]{1,0:T(8,128)S(1)}, f32[4864,128]{1,0:T(8,128)S(1)}, u32[]{:S(2)}, u32[]{:S(2)}) collective-permute-start(f32[4864,128]{1,0:T(8,128)S(1)} %get-tuple-element.32.refs_1_), channel_id=1, source_target_pairs={{4,0},{8,4},{12,8},{16,12},{20,16},{24,20},{28,24},{32,28},{36,32}... | collective-permute-start | bytes 7471112 | tf_op jit(solution)/shard_map/ppermute | solution.py:491
  173.7 73.8 %collective-permute-start.6 = (f32[2048,128]{1,0:T(8,128)S(1)}, f32[2048,128]{1,0:T(8,128)S(1)}, u32[]{:S(2)}, u32[]{:S(2)}) collective-permute-start(f32[2048,128]{1,0:T(8,128)S(1)} %get-tuple-element.34.refs_3_.refs_7_), channel_id=1, source_target_pairs={{0,4},{4,8},{8,12},{12,16},{16,20},{20,24},{24,28},{28,32},{32,36}... | collective-permute-start | bytes 3145736 | tf_op jit(solution)/shard_map/ppermute | solution.py:486
  175.8 71.7 %collective-permute-start.7 = (f32[2048,128]{1,0:T(8,128)S(1)}, f32[2048,128]{1,0:T(8,128)S(1)}, u32[]{:S(2)}, u32[]{:S(2)}) collective-permute-start(f32[2048,128]{1,0:T(8,128)S(1)} %get-tuple-element.35.refs_1_.refs_5_), channel_id=1, source_target_pairs={{4,0},{8,4},{12,8},{16,12},{20,16},{24,20},{28,24},{32,28},{36,32}... | collective-permute-start | bytes 3145736 | tf_op jit(solution)/shard_map/ppermute | solution.py:491
  249.3 1.5 collective-permute-start.8
  250.8 7.0 %collective-permute-start.9 = (f32[384,128]{1,0:T(8,128)S(1)}, f32[384,128]{1,0:T(8,128)S(1)}, u32[]{:S(2)}, u32[]{:S(2)}) collective-permute-start(f32[384,128]{1,0:T(8,128)S(1)} %add.7.one_ref), channel_id=1, source_target_pairs={{0,2},{1,3},{2,0},{3,1},{4,6},{5,7},{6,4},{7,5},{8,10},{9,11},{10,... | collective-permute-start | bytes 589832 | tf_op jit(solution)/shard_map/ppermute | solution.py:213

commit v7 on v6

--- a/solution.py
+++ b/solution.py
@@ -10,8 +10,7 @@
 BLOCK = 128
 WIDTH = 2 * BLOCK
 TILE = 1024
-RAW = 1536
-CHUNKS = (4608, 2048)
+CHUNKS = (3072, 3072, 2048)
 STRIP = 64
 PANEL = 32
 SUB = 8
@@ -360,11 +359,6 @@
 def turn_kernel(start, source_ref, one_ref, two_ref, first_ref, second_ref, rows_ref, sems):
     start_rows(source_ref, rows_ref, sems, start)
     rotation_t = jnp.concatenate([one_ref[...], two_ref[...]])
-    if first_ref.shape[0] > rows_ref.shape[0]:
-        for half_ref, out_ref in ((one_ref, first_ref), (two_ref, second_ref)):
-            end = rows_ref.shape[0]
-            out_ref[end : end + BLOCK, :] = half_ref[:, :BLOCK]
-            out_ref[end + BLOCK :, :] = half_ref[:, BLOCK:]
 
     def put(row, size, tile):
         row_copy(source_ref, rows_ref, sems, row, size, tile, start).wait()
@@ -376,64 +370,27 @@
     for_tiles(rows_ref.shape[0], put)
 
 
-def turn(pair_rows, rotation_t, start, rows, extra):
+def turn(pair_rows, rotation_t, start, rows):
     whole = pl.BlockSpec(memory_space=pltpu.VMEM)
     return pl.pallas_call(
         functools.partial(turn_kernel, start),
         in_specs=[pl.BlockSpec(memory_space=pltpu.HBM), whole, whole],
         out_specs=[whole, whole],
-        out_shape=[jax.ShapeDtypeStruct((rows + extra, BLOCK), F32)] * 2,
+        out_shape=[jax.ShapeDtypeStruct((rows, BLOCK), F32)] * 2,
         scratch_shapes=[
             pltpu.VMEM((rows, WIDTH), F32),
             pltpu.SemaphoreType.DMA((pl.cdiv(rows, TILE),)),
         ],
         compiler_params=grant(24),
-        cost_estimate=cost(rows if extra else 30 * rows),
+        cost_estimate=cost(rows),
         name="turn",
     )(in_hbm(pair_rows), *rotation_t)
 
 
-def raw_gram_kernel(ends, below_ref, above_ref, own_ref, *refs):
-    moved_refs, (out_ref, packed_ref, total_ref, cross_ref) = refs[:4], refs[4:]
-    total_ref[...] = jnp.zeros_like(total_ref)
-    cross_ref[...] = jnp.zeros_like(cross_ref)
-    halves_t = [
-        jnp.concatenate([half[:BLOCK], half[BLOCK:]], axis=1)
-        for half in moved_rows(ends, moved_refs, CHUNKS[0], WIDTH)
-    ]
-
-    def put(row, size, tile):
-        rows = pl.ds(row, size)
-        own = own_ref[rows, :]
-        upper = product(jnp.where(ends[0] == 1, own, below_ref[rows, :]), halves_t[0])
-        lower = product(jnp.where(ends[1] == 1, own, above_ref[rows, :]), halves_t[1])
-        turned = jnp.concatenate([upper, lower], axis=1)
-        out_ref[rows, :] = turned
-        add_gram(turned, total_ref, cross_ref)
-
-    for_tiles(RAW, put)
-    packed_ref[...] = pack(total_ref, cross_ref)
-
-
-def raw_gram(ends, below, above, own, moved):
-    whole = pl.BlockSpec(memory_space=pltpu.VMEM)
-    return pl.pallas_call(
-        raw_gram_kernel,
-        in_specs=in_vmem(7),
-        out_specs=[whole, whole],
-        out_shape=[
-            jax.ShapeDtypeStruct((RAW, WIDTH), F32),
-            jax.ShapeDtypeStruct((3 * BLOCK, BLOCK), F32),
-        ],
-        scratch_shapes=[pltpu.VMEM((WIDTH, WIDTH), F32)] * 2,
-        compiler_params=grant(24),
-        cost_estimate=cost(2 * RAW),
-        name="raw_gram",
-    )(ends, below, above, own, *moved)
-
-
-def last_turn_kernel(ends, one_ref, two_ref, raw_ref, *refs):
-    moved, (out_ref, turned_ref, sems) = (refs[0:4], refs[4:8]), refs[8:]
+def last_turn_kernel(ends, one_ref, two_ref, *refs):
+    arrays = 4 * len(CHUNKS)
+    moved = [refs[at : at + 4] for at in range(0, arrays, 4)]
+    out_ref, turned_ref, sems = refs[arrays:]
     rotation_t = jnp.concatenate([one_ref[...], two_ref[...]])
 
     def out_copy(row, size, sem):
@@ -442,13 +399,10 @@
 
     start, sem = 0, 0
     copies = []
-    for moved_refs, count in zip((None, *moved), (RAW, *CHUNKS)):
+    for moved_refs, count in zip(moved, CHUNKS):
 
         def put(row, size, tile, moved_refs=moved_refs, start=start, sem=sem):
-            if moved_refs is None:
-                rows = raw_ref[pl.ds(row, size), :]
-            else:
-                rows = moved_tile(ends, moved_refs, row, size)
+            rows = moved_tile(ends, moved_refs, row, size)
             at = pl.ds(pl.multiple_of(start + row, BLOCK), size)
             turned_ref[at, :] = product(rows, rotation_t)
             out_copy(start + row, size, sem + tile).start()
@@ -462,13 +416,13 @@
         out_copy(*copy).wait()
 
 
-def last_turn(ends, rotation_t, raw, moved):
-    rows = RAW + sum(CHUNKS)
-    tiles = sum(pl.cdiv(count, TILE) for count in (RAW, *CHUNKS))
+def last_turn(ends, rotation_t, moved):
+    rows = sum(CHUNKS)
+    tiles = sum(pl.cdiv(count, TILE) for count in CHUNKS)
     moved = [array for part in moved for array in part]
     return pl.pallas_call(
         last_turn_kernel,
-        in_specs=in_vmem(3 + len(moved)),
+        in_specs=in_vmem(2 + len(moved)),
         out_specs=pl.BlockSpec(memory_space=pl.ANY),
         out_shape=jax.ShapeDtypeStruct((rows, WIDTH), F32),
         scratch_shapes=[
@@ -478,7 +432,7 @@
         compiler_params=grant(24),
         cost_estimate=cost(rows),
         name="last_turn",
-    )(ends, *rotation_t, raw, *moved)
+    )(ends, *rotation_t, *moved)
 
 
 def send_up(value):
@@ -502,22 +456,17 @@
     pair_rows = lax.all_to_all(ordered, "col", split_axis=0, concat_axis=0, tiled=True)
     pair_rows = pair_rows.reshape(rows, WIDTH)
 
-    parts = row_parts(local_gram(pair_rows))
-    *parts, own = lax.optimization_barrier((*parts, pair_rows[:RAW]))
-    below, above = send_up(own), send_down(own)
-    rotation_t = pair_rotation(ends[:1], parts)
-    moved, start = [], RAW
-    for number, chunk in enumerate(CHUNKS):
-        first, second = turn(pair_rows, rotation_t, start, chunk, 0 if number else WIDTH)
-        if number == 1:
-            first, second, below, above = lax.optimization_barrier((first, second, below, above))
+    rotation_t = pair_rotation(ends[:1], row_parts(local_gram(pair_rows)))
+    moved, start = [], 0
+    for chunk in CHUNKS:
+        first, second = turn(pair_rows, rotation_t, start, chunk)
         moved.append((send_up(first), second, send_down(second), first))
         start += chunk
-    raw, gram = raw_gram(ends, below, above, own, moved[0])
+    gram = jnp.zeros((3 * BLOCK, BLOCK), F32)
     for part, chunk in zip(moved, CHUNKS):
         gram = moved_gram(ends, gram, part, chunk)
     rotation_t = pair_rotation(jnp.zeros((1,), jnp.int32), row_parts(gram))
-    return last_turn(ends, rotation_t, raw, moved).reshape(col_count, 1, local_rows, WIDTH)
+    return last_turn(ends, rotation_t, moved).reshape(col_count, 1, local_rows, WIDTH)
 
 
 def solution(mesh):

time: 280 us -> 278 us (level)
  starting transfers between devices: 29.4 us -> 26.4 us
    ppermute x3, waiting for transfers between devices: 66.7 us -> 61.8 us  [send_up(): return lax.ppermute(value, 'col', [(p, p + 1) for p in range(count - 1)])]
    ppermute x3, starting transfers between devices: 21.7 us -> 17.6 us  [send_down(): return lax.ppermute(value, 'col', [(p, p - 1) for p in range(1, count)])]
    pallas_call x2 -> x1, Pallas kernels: 9.22 us -> 6.71 us  [last_turn(): pl.pallas_call(last_turn_kernel, in_specs=in_vmem(2 + len(moved)), out_sp...]
    pallas_call x2 -> x3, Pallas kernels: 6.67 us -> 8.73 us  [turn(): pl.pallas_call(functools.partial(turn_kernel, start), in_specs=[pl.BlockS...]
    pallas_call x2 -> x3, Pallas kernels: 4.62 us -> 6.03 us  [moved_gram(): pl.pallas_call(functools.partial(moved_gram_kernel, chunk), in_specs=in_v...]
  transfers between devices with their start and end apart: 10 -> 10, of which waited for: 8 -> 9; matrix products, arithmetic and copies ran while one was open for 1% -> 0% of each run, Pallas kernels for 10% -> 4%
where the time goes in v7:
time: 278 us; the launch traced here: 276 us
  blocking collectives  106 us (38%)
  waiting for transfers between devices  80.1 us (29%)
  Pallas kernels  62.2 us (22%)
  starting transfers between devices  26.4 us (9%)
    all_to_all x1, blocking collectives, local(): lax.all_to_all(ordered, 'col', split_axis=0, concat_axis=0, tiled=True)  106 us
    ppermute x3, waiting for transfers between devices, send_up(): return lax.ppermute(value, 'col', [(p, p + 1) for p in range(count - 1)])  61.8 us
    pallas_call x2, Pallas kernels, pair_rotation(): pl.pallas_call(rotation_kernel, in_specs=[pl.BlockSpec(memory_space=pltpu...  31 us
    ppermute x3, starting transfers between devices, send_down(): return lax.ppermute(value, 'col', [(p, p - 1) for p in range(1, count)])  17.6 us
    ppermute x4, waiting for transfers between devices, row_parts(): parts = (packed, lax.ppermute(packed, 'row', swap))  15.3 us
    pallas_call x3, Pallas kernels, turn(): pl.pallas_call(functools.partial(turn_kernel, start), in_specs=[pl.BlockS...  8.73 us
    ppermute x3, starting transfers between devices, send_up(): return lax.ppermute(value, 'col', [(p, p + 1) for p in range(count - 1)])  7.17 us
    pallas_call x1, Pallas kernels, last_turn(): pl.pallas_call(last_turn_kernel, in_specs=in_vmem(2 + len(moved)), out_sp...  6.71 us
  transfers between devices with their start and end apart: 10, of which 9 were waited for; matrix products, arithmetic and copies ran while one was open for 0% of the time, Pallas kernels for 4%

profile of v7, /device:TPU:32, one launch (start us, length us, event | category | flops | bytes accessed | tf_op | source)
XLA Modules:
  0.0 275.8 jit_solution(6470450792905115579)
XLA Ops:
  0.7 4.5 %order.1 = f32[32,256,256]{2,1,0:T(8,128)S(1)} custom-call(s32[64]{0:T(128)S(1)} %copy-done, f32[256,8192]{1,0:T(8,128)} %diffs_ref.1), custom_call_target="tpu_custom_call" | custom-call | tf_op jit(solution)/shard_map/order/pallas_call | solution.py:69
  5.2 106.0 %all_to_all.5 = f32[32,256,256]{2,1,0:T(8,128)} all-to-all(f32[32,256,256]{2,1,0:T(8,128)S(1)} %order.1), channel_id=1, replica_groups=mesh['col'=32,'row'=4] {'col'}, dimensions={0} | all-to-all | bytes 16777216 | tf_op jit(solution)/shard_map/all_to_all | solution.py:456
  111.2 5.2 %gram.1 = f32[384,128]{1,0:T(8,128)S(1)} custom-call(f32[8192,256]{1,0:T(8,128)} %bitcast.8), custom_call_target="tpu_custom_call" | custom-call | flops 1000 | bytes 1000 | tf_op jit(solution)/shard_map/gram/pallas_call | solution.py:141
  118.8 6.2 %collective-permute-done.1.two_ref = f32[384,128]{1,0:T(8,128)S(1)} collective-permute-done((f32[384,128]{1,0:T(8,128)S(1)}, f32[384,128]{1,0:T(8,128)S(1)}, u32[]{:S(2)}, u32[]{:S(2)}) %collective-permute-start.1) | collective-permute-done | bytes 196640 | tf_op jit(solution)/shard_map/ppermute | solution.py:212
  125.0 15.5 %rotation.2 = (f32[128,256]{1,0:T(8,128)S(1)}, f32[128,256]{1,0:T(8,128)S(1)}) custom-call(s32[1]{0:T(128)S(1)} %bitcast.7, f32[384,128]{1,0:T(8,128)S(1)} %add.6.one_ref, f32[384,128]{1,0:T(8,128)S(1)} %collective-permute-done.1.two_ref), custom_call_target="tpu_custom_call" | custom-call | flops 1000 | bytes 1000 | tf_op jit(solution)/shard_map/rotation/pallas_call | solution.py:340
  140.5 3.1 %turn.3 = (f32[3072,128]{1,0:T(8,128)S(1)}, f32[3072,128]{1,0:T(8,128)S(1)}) custom-call(f32[8192,256]{1,0:T(8,128)} %bitcast.9, f32[128,256]{1,0:T(8,128)S(1)} %get-tuple-element.15.one_ref, f32[128,256]{1,0:T(8,128)S(1)} %get-tuple-element.16.two_ref), custom_call_target="tpu_custom_call" | custom-call | flops 1207959552 | bytes 6291456 | tf_op jit(solution)/shard_map/turn/pallas_call | solution.py:375
  143.6 3.3 %collective-permute-start.2 = (f32[3072,128]{1,0:T(8,128)S(1)}, f32[3072,128]{1,0:T(8,128)S(1)}, u32[]{:S(2)}, u32[]{:S(2)}) collective-permute-start(f32[3072,128]{1,0:T(8,128)S(1)} %get-tuple-element.17.refs_3_), channel_id=1, source_target_pairs={{0,4},{4,8},{8,12},{12,16},{16,20},{20,24},{24,28},{28,32},{32,36}... | collective-permute-start | bytes 4718600 | tf_op jit(solution)/shard_map/ppermute | solution.py:440
  147.0 7.2 %collective-permute-start.3 = (f32[3072,128]{1,0:T(8,128)S(1)}, f32[3072,128]{1,0:T(8,128)S(1)}, u32[]{:S(2)}, u32[]{:S(2)}) collective-permute-start(f32[3072,128]{1,0:T(8,128)S(1)} %get-tuple-element.18.refs_1_), channel_id=1, source_target_pairs={{4,0},{8,4},{12,8},{16,12},{20,16},{24,20},{28,24},{32,28},{36,32}... | collective-permute-start | bytes 4718600 | tf_op jit(solution)/shard_map/ppermute | solution.py:445
  154.2 3.1 %turn.4 = (f32[3072,128]{1,0:T(8,128)S(1)}, f32[3072,128]{1,0:T(8,128)S(1)}) custom-call(f32[8192,256]{1,0:T(8,128)} %bitcast.10, f32[128,256]{1,0:T(8,128)S(1)} %get-tuple-element.15.one_ref, f32[128,256]{1,0:T(8,128)S(1)} %get-tuple-element.16.two_ref), custom_call_target="tpu_custom_call" | custom-call | flops 1207959552 | bytes 6291456 | tf_op jit(solution)/shard_map/turn/pallas_call | solution.py:375
  157.3 1.9 collective-permute-start.4
  159.2 8.4 %collective-permute-start.5 = (f32[3072,128]{1,0:T(8,128)S(1)}, f32[3072,128]{1,0:T(8,128)S(1)}, u32[]{:S(2)}, u32[]{:S(2)}) collective-permute-start(f32[3072,128]{1,0:T(8,128)S(1)} %get-tuple-element.20.refs_1_.refs_5_), channel_id=1, source_target_pairs={{4,0},{8,4},{12,8},{16,12},{20,16},{24,20},{28,24},{32,28},{36,32}... | collective-permute-start | bytes 4718600 | tf_op jit(solution)/shard_map/ppermute | solution.py:445
  167.7 2.5 turn.5
  170.2 1.9 collective-permute-start.6
  172.1 15.3 %collective-permute-done.2.refs_0_ = f32[3072,128]{1,0:T(8,128)S(1)} collective-permute-done((f32[3072,128]{1,0:T(8,128)S(1)}, f32[3072,128]{1,0:T(8,128)S(1)}, u32[]{:S(2)}, u32[]{:S(2)}) %collective-permute-start.2) | collective-permute-done | bytes 1572896 | tf_op jit(solution)/shard_map/ppermute | solution.py:440
  187.4 1.9 collective-permute-start.7
  189.3 2.2 moved_gram.3.before_ref
  191.5 29.6 %collective-permute-done.4.refs_0_.refs_4_ = f32[3072,128]{1,0:T(8,128)S(1)} collective-permute-done((f32[3072,128]{1,0:T(8,128)S(1)}, f32[3072,128]{1,0:T(8,128)S(1)}, u32[]{:S(2)}, u32[]{:S(2)}) %collective-permute-start.4) | collective-permute-done | bytes 1572896 | tf_op jit(solution)/shard_map/ppermute | solution.py:440
  221.1 1.6 collective-permute-done.5.refs_2_.refs_6_
  222.7 2.2 moved_gram.4.before_ref
  224.9 16.9 %collective-permute-done.6.refs_0_.refs_8_ = f32[2048,128]{1,0:T(8,128)S(1)} collective-permute-done((f32[2048,128]{1,0:T(8,128)S(1)}, f32[2048,128]{1,0:T(8,128)S(1)}, u32[]{:S(2)}, u32[]{:S(2)}) %collective-permute-start.6) | collective-permute-done | bytes 1048608 | tf_op jit(solution)/shard_map/ppermute | solution.py:440
  243.2 1.7 moved_gram.5
  247.2 6.3 %collective-permute-done.9.two_ref = f32[384,128]{1,0:T(8,128)S(1)} collective-permute-done((f32[384,128]{1,0:T(8,128)S(1)}, f32[384,128]{1,0:T(8,128)S(1)}, u32[]{:S(2)}, u32[]{:S(2)}) %collective-permute-start.9) | collective-permute-done | bytes 196640 | tf_op jit(solution)/shard_map/ppermute | solution.py:212
  253.5 15.5 %rotation.3 = (f32[128,256]{1,0:T(8,128)S(1)}, f32[128,256]{1,0:T(8,128)S(1)}) custom-call(s32[1]{0:T(128)} %constant.12.clone.1.swap_ref, f32[384,128]{1,0:T(8,128)S(1)} %add.7.one_ref, f32[384,128]{1,0:T(8,128)S(1)} %collective-permute-done.9.two_ref), custom_call_target="tpu_custom_call" | custom-call | flops 1000 | bytes 1000 | tf_op jit(solution)/shard_map/rotation/pallas_call | solution.py:340
  269.0 6.7 %last_turn.1 = f32[8192,256]{1,0:T(8,128)} custom-call(s32[2]{0:T(128)S(1)} %add_convert_fusion.ends, f32[128,256]{1,0:T(8,128)S(1)} %get-tuple-element.23.one_ref, f32[128,256]{1,0:T(8,128)S(1)} %get-tuple-element.24.two_ref, f32[3072,128]{1,0:T(8,128)S(1)} %collective-permute-done.2.refs_0_, f32[3072,128]{1,0:T(8,128)S(1)} %get-tuple-element.18.refs_1_, ...), custom_call_target="tpu_custom_call" | custom-call | flops 3221225472 | bytes 16777216 | tf_op jit(solution)/shard_map/last_turn/pallas_call | solution.py:423
  (14 shorter events, 6.7 us)
Async XLA Ops:
  0.0 0.7 copy-start
  116.4 1.5 collective-permute-start
  118.0 7.0 %collective-permute-start.1 = (f32[384,128]{1,0:T(8,128)S(1)}, f32[384,128]{1,0:T(8,128)S(1)}, u32[]{:S(2)}, u32[]{:S(2)}) collective-permute-start(f32[384,128]{1,0:T(8,128)S(1)} %add.6.one_ref), channel_id=1, source_target_pairs={{0,2},{1,3},{2,0},{3,1},{4,6},{5,7},{6,4},{7,5},{8,10},{9,11},{10,... | collective-permute-start | bytes 589832 | tf_op jit(solution)/shard_map/ppermute | solution.py:212
  143.6 43.7 %collective-permute-start.2 = (f32[3072,128]{1,0:T(8,128)S(1)}, f32[3072,128]{1,0:T(8,128)S(1)}, u32[]{:S(2)}, u32[]{:S(2)}) collective-permute-start(f32[3072,128]{1,0:T(8,128)S(1)} %get-tuple-element.17.refs_3_), channel_id=1, source_target_pairs={{0,4},{4,8},{8,12},{12,16},{16,20},{20,24},{24,28},{28,32},{32,36}... | collective-permute-start | bytes 4718600 | tf_op jit(solution)/shard_map/ppermute | solution.py:440
  147.0 42.3 %collective-permute-start.3 = (f32[3072,128]{1,0:T(8,128)S(1)}, f32[3072,128]{1,0:T(8,128)S(1)}, u32[]{:S(2)}, u32[]{:S(2)}) collective-permute-start(f32[3072,128]{1,0:T(8,128)S(1)} %get-tuple-element.18.refs_1_), channel_id=1, source_target_pairs={{4,0},{8,4},{12,8},{16,12},{20,16},{24,20},{28,24},{32,28},{36,32}... | collective-permute-start | bytes 4718600 | tf_op jit(solution)/shard_map/ppermute | solution.py:445
  157.3 63.8 %collective-permute-start.4 = (f32[3072,128]{1,0:T(8,128)S(1)}, f32[3072,128]{1,0:T(8,128)S(1)}, u32[]{:S(2)}, u32[]{:S(2)}) collective-permute-start(f32[3072,128]{1,0:T(8,128)S(1)} %get-tuple-element.19.refs_3_.refs_7_), channel_id=1, source_target_pairs={{0,4},{4,8},{8,12},{12,16},{16,20},{20,24},{24,28},{28,32},{32,36}... | collective-permute-start | bytes 4718600 | tf_op jit(solution)/shard_map/ppermute | solution.py:440
  159.2 63.5 %collective-permute-start.5 = (f32[3072,128]{1,0:T(8,128)S(1)}, f32[3072,128]{1,0:T(8,128)S(1)}, u32[]{:S(2)}, u32[]{:S(2)}) collective-permute-start(f32[3072,128]{1,0:T(8,128)S(1)} %get-tuple-element.20.refs_1_.refs_5_), channel_id=1, source_target_pairs={{4,0},{8,4},{12,8},{16,12},{20,16},{24,20},{28,24},{32,28},{36,32}... | collective-permute-start | bytes 4718600 | tf_op jit(solution)/shard_map/ppermute | solution.py:445
  170.2 71.7 %collective-permute-start.6 = (f32[2048,128]{1,0:T(8,128)S(1)}, f32[2048,128]{1,0:T(8,128)S(1)}, u32[]{:S(2)}, u32[]{:S(2)}) collective-permute-start(f32[2048,128]{1,0:T(8,128)S(1)} %get-tuple-element.21.refs_3_.refs_11_), channel_id=1, source_target_pairs={{0,4},{4,8},{8,12},{12,16},{16,20},{20,24},{24,28},{28,32},{32,36}... | collective-permute-start | bytes 3145736 | tf_op jit(solution)/shard_map/ppermute | solution.py:440
  187.4 55.8 %collective-permute-start.7 = (f32[2048,128]{1,0:T(8,128)S(1)}, f32[2048,128]{1,0:T(8,128)S(1)}, u32[]{:S(2)}, u32[]{:S(2)}) collective-permute-start(f32[2048,128]{1,0:T(8,128)S(1)} %get-tuple-element.22.refs_1_.refs_9_), channel_id=1, source_target_pairs={{4,0},{8,4},{12,8},{16,12},{20,16},{24,20},{28,24},{32,28},{36,32}... | collective-permute-start | bytes 3145736 | tf_op jit(solution)/shard_map/ppermute | solution.py:445
  244.9 1.5 collective-permute-start.8
  246.5 7.0 %collective-permute-start.9 = (f32[384,128]{1,0:T(8,128)S(1)}, f32[384,128]{1,0:T(8,128)S(1)}, u32[]{:S(2)}, u32[]{:S(2)}) collective-permute-start(f32[384,128]{1,0:T(8,128)S(1)} %add.7.one_ref), channel_id=1, source_target_pairs={{0,2},{1,3},{2,0},{3,1},{4,6},{5,7},{6,4},{7,5},{8,10},{9,11},{10,... | collective-permute-start | bytes 589832 | tf_op jit(solution)/shard_map/ppermute | solution.py:212

commit v8 on v7

--- a/solution.py
+++ b/solution.py
@@ -10,7 +10,7 @@
 BLOCK = 128
 WIDTH = 2 * BLOCK
 TILE = 1024
-CHUNKS = (3072, 3072, 2048)
+CHUNKS = (3584, 3584, 1024)
 STRIP = 64
 PANEL = 32
 SUB = 8

time: 278 us -> 278 us (level)
  no operation moved by 1% of the time
where the time goes in v8:
time: 278 us; the launch traced here: 275 us
  blocking collectives  106 us (38%)
  waiting for transfers between devices  79.7 us (29%)
  Pallas kernels  62.4 us (22%)
  starting transfers between devices  26.2 us (9%)
    all_to_all x1, blocking collectives, local(): lax.all_to_all(ordered, 'col', split_axis=0, concat_axis=0, tiled=True)  106 us
    ppermute x3, waiting for transfers between devices, send_up(): return lax.ppermute(value, 'col', [(p, p + 1) for p in range(count - 1)])  61.8 us
    pallas_call x2, Pallas kernels, pair_rotation(): pl.pallas_call(rotation_kernel, in_specs=[pl.BlockSpec(memory_space=pltpu...  31 us
    ppermute x3, starting transfers between devices, send_down(): return lax.ppermute(value, 'col', [(p, p - 1) for p in range(1, count)])  17.4 us
    ppermute x4, waiting for transfers between devices, row_parts(): parts = (packed, lax.ppermute(packed, 'row', swap))  15.3 us
    pallas_call x3, Pallas kernels, turn(): pl.pallas_call(functools.partial(turn_kernel, start), in_specs=[pl.BlockS...  8.96 us
    ppermute x3, starting transfers between devices, send_up(): return lax.ppermute(value, 'col', [(p, p + 1) for p in range(count - 1)])  7.16 us
    pallas_call x1, Pallas kernels, last_turn(): pl.pallas_call(last_turn_kernel, in_specs=in_vmem(2 + len(moved)), out_sp...  6.69 us
  transfers between devices with their start and end apart: 10, of which 9 were waited for; matrix products, arithmetic and copies ran while one was open for 0% of the time, Pallas kernels for 4%

profile of v8, /device:TPU:32, one launch (start us, length us, event | category | flops | bytes accessed | tf_op | source)
XLA Modules:
  0.0 275.5 jit_solution(8497868618983980748)
XLA Ops:
  0.7 4.5 %order.1 = f32[32,256,256]{2,1,0:T(8,128)S(1)} custom-call(s32[64]{0:T(128)S(1)} %copy-done, f32[256,8192]{1,0:T(8,128)} %diffs_ref.1), custom_call_target="tpu_custom_call" | custom-call | tf_op jit(solution)/shard_map/order/pallas_call | solution.py:69
  5.2 106.0 %all_to_all.5 = f32[32,256,256]{2,1,0:T(8,128)} all-to-all(f32[32,256,256]{2,1,0:T(8,128)S(1)} %order.1), channel_id=1, replica_groups=mesh['col'=32,'row'=4] {'col'}, dimensions={0} | all-to-all | bytes 16777216 | tf_op jit(solution)/shard_map/all_to_all | solution.py:456
  111.2 5.2 %gram.1 = f32[384,128]{1,0:T(8,128)S(1)} custom-call(f32[8192,256]{1,0:T(8,128)} %bitcast.8), custom_call_target="tpu_custom_call" | custom-call | flops 1000 | bytes 1000 | tf_op jit(solution)/shard_map/gram/pallas_call | solution.py:141
  116.5 1.4 collective-permute-done
  118.8 6.2 %collective-permute-done.1.two_ref = f32[384,128]{1,0:T(8,128)S(1)} collective-permute-done((f32[384,128]{1,0:T(8,128)S(1)}, f32[384,128]{1,0:T(8,128)S(1)}, u32[]{:S(2)}, u32[]{:S(2)}) %collective-permute-start.1) | collective-permute-done | bytes 196640 | tf_op jit(solution)/shard_map/ppermute | solution.py:212
  125.0 15.5 %rotation.2 = (f32[128,256]{1,0:T(8,128)S(1)}, f32[128,256]{1,0:T(8,128)S(1)}) custom-call(s32[1]{0:T(128)S(1)} %bitcast.7, f32[384,128]{1,0:T(8,128)S(1)} %add.6.one_ref, f32[384,128]{1,0:T(8,128)S(1)} %collective-permute-done.1.two_ref), custom_call_target="tpu_custom_call" | custom-call | flops 1000 | bytes 1000 | tf_op jit(solution)/shard_map/rotation/pallas_call | solution.py:340
  140.5 3.5 %turn.3 = (f32[3584,128]{1,0:T(8,128)S(1)}, f32[3584,128]{1,0:T(8,128)S(1)}) custom-call(f32[8192,256]{1,0:T(8,128)} %bitcast.9, f32[128,256]{1,0:T(8,128)S(1)} %get-tuple-element.15.one_ref, f32[128,256]{1,0:T(8,128)S(1)} %get-tuple-element.16.two_ref), custom_call_target="tpu_custom_call" | custom-call | flops 1409286144 | bytes 7340032 | tf_op jit(solution)/shard_map/turn/pallas_call | solution.py:375
  144.1 3.1 %collective-permute-start.2 = (f32[3584,128]{1,0:T(8,128)S(1)}, f32[3584,128]{1,0:T(8,128)S(1)}, u32[]{:S(2)}, u32[]{:S(2)}) collective-permute-start(f32[3584,128]{1,0:T(8,128)S(1)} %get-tuple-element.17.refs_3_), channel_id=1, source_target_pairs={{0,4},{4,8},{8,12},{12,16},{16,20},{20,24},{24,28},{28,32},{32,36}... | collective-permute-start | bytes 5505032 | tf_op jit(solution)/shard_map/ppermute | solution.py:440
  147.2 7.2 %collective-permute-start.3 = (f32[3584,128]{1,0:T(8,128)S(1)}, f32[3584,128]{1,0:T(8,128)S(1)}, u32[]{:S(2)}, u32[]{:S(2)}) collective-permute-start(f32[3584,128]{1,0:T(8,128)S(1)} %get-tuple-element.18.refs_1_), channel_id=1, source_target_pairs={{4,0},{8,4},{12,8},{16,12},{20,16},{24,20},{28,24},{32,28},{36,32}... | collective-permute-start | bytes 5505032 | tf_op jit(solution)/shard_map/ppermute | solution.py:445
  154.4 3.6 %turn.4 = (f32[3584,128]{1,0:T(8,128)S(1)}, f32[3584,128]{1,0:T(8,128)S(1)}) custom-call(f32[8192,256]{1,0:T(8,128)} %bitcast.10, f32[128,256]{1,0:T(8,128)S(1)} %get-tuple-element.15.one_ref, f32[128,256]{1,0:T(8,128)S(1)} %get-tuple-element.16.two_ref), custom_call_target="tpu_custom_call" | custom-call | flops 1409286144 | bytes 7340032 | tf_op jit(solution)/shard_map/turn/pallas_call | solution.py:375
  158.0 2.1 collective-permute-start.4
  160.1 8.3 %collective-permute-start.5 = (f32[3584,128]{1,0:T(8,128)S(1)}, f32[3584,128]{1,0:T(8,128)S(1)}, u32[]{:S(2)}, u32[]{:S(2)}) collective-permute-start(f32[3584,128]{1,0:T(8,128)S(1)} %get-tuple-element.20.refs_1_.refs_5_), channel_id=1, source_target_pairs={{4,0},{8,4},{12,8},{16,12},{20,16},{24,20},{28,24},{32,28},{36,32}... | collective-permute-start | bytes 5505032 | tf_op jit(solution)/shard_map/ppermute | solution.py:445
  168.4 1.9 turn.5
  170.2 1.9 collective-permute-start.6
  172.2 21.3 %collective-permute-done.2.refs_0_ = f32[3584,128]{1,0:T(8,128)S(1)} collective-permute-done((f32[3584,128]{1,0:T(8,128)S(1)}, f32[3584,128]{1,0:T(8,128)S(1)}, u32[]{:S(2)}, u32[]{:S(2)}) %collective-permute-start.2) | collective-permute-done | bytes 1835040 | tf_op jit(solution)/shard_map/ppermute | solution.py:440
  193.4 1.9 collective-permute-start.7
  195.4 2.4 moved_gram.3.before_ref
  197.8 34.9 %collective-permute-done.4.refs_0_.refs_4_ = f32[3584,128]{1,0:T(8,128)S(1)} collective-permute-done((f32[3584,128]{1,0:T(8,128)S(1)}, f32[3584,128]{1,0:T(8,128)S(1)}, u32[]{:S(2)}, u32[]{:S(2)}) %collective-permute-start.4) | collective-permute-done | bytes 1835040 | tf_op jit(solution)/shard_map/ppermute | solution.py:440
  232.8 1.5 collective-permute-done.5.refs_2_.refs_6_
  234.2 2.4 moved_gram.4.before_ref
  236.7 5.6 %collective-permute-done.6.refs_0_.refs_8_ = f32[1024,128]{1,0:T(8,128)S(1)} collective-permute-done((f32[1024,128]{1,0:T(8,128)S(1)}, f32[1024,128]{1,0:T(8,128)S(1)}, u32[]{:S(2)}, u32[]{:S(2)}) %collective-permute-start.6) | collective-permute-done | bytes 524320 | tf_op jit(solution)/shard_map/ppermute | solution.py:440
  246.9 6.3 %collective-permute-done.9.two_ref = f32[384,128]{1,0:T(8,128)S(1)} collective-permute-done((f32[384,128]{1,0:T(8,128)S(1)}, f32[384,128]{1,0:T(8,128)S(1)}, u32[]{:S(2)}, u32[]{:S(2)}) %collective-permute-start.9) | collective-permute-done | bytes 196640 | tf_op jit(solution)/shard_map/ppermute | solution.py:212
  253.1 15.5 %rotation.3 = (f32[128,256]{1,0:T(8,128)S(1)}, f32[128,256]{1,0:T(8,128)S(1)}) custom-call(s32[1]{0:T(128)} %constant.12.clone.1.swap_ref, f32[384,128]{1,0:T(8,128)S(1)} %add.7.one_ref, f32[384,128]{1,0:T(8,128)S(1)} %collective-permute-done.9.two_ref), custom_call_target="tpu_custom_call" | custom-call | flops 1000 | bytes 1000 | tf_op jit(solution)/shard_map/rotation/pallas_call | solution.py:340
  268.6 6.7 %last_turn.1 = f32[8192,256]{1,0:T(8,128)} custom-call(s32[2]{0:T(128)S(1)} %add_convert_fusion.ends, f32[128,256]{1,0:T(8,128)S(1)} %get-tuple-element.23.one_ref, f32[128,256]{1,0:T(8,128)S(1)} %get-tuple-element.24.two_ref, f32[3584,128]{1,0:T(8,128)S(1)} %collective-permute-done.2.refs_0_, f32[3584,128]{1,0:T(8,128)S(1)} %get-tuple-element.18.refs_1_, ...), custom_call_target="tpu_custom_call" | custom-call | flops 3221225472 | bytes 16777216 | tf_op jit(solution)/shard_map/last_turn/pallas_call | solution.py:423
  (14 shorter events, 6.2 us)
Async XLA Ops:
  0.0 0.7 copy-start
  116.4 1.5 collective-permute-start
  118.0 7.0 %collective-permute-start.1 = (f32[384,128]{1,0:T(8,128)S(1)}, f32[384,128]{1,0:T(8,128)S(1)}, u32[]{:S(2)}, u32[]{:S(2)}) collective-permute-start(f32[384,128]{1,0:T(8,128)S(1)} %add.6.one_ref), channel_id=1, source_target_pairs={{0,2},{1,3},{2,0},{3,1},{4,6},{5,7},{6,4},{7,5},{8,10},{9,11},{10,... | collective-permute-start | bytes 589832 | tf_op jit(solution)/shard_map/ppermute | solution.py:212
  144.1 49.4 %collective-permute-start.2 = (f32[3584,128]{1,0:T(8,128)S(1)}, f32[3584,128]{1,0:T(8,128)S(1)}, u32[]{:S(2)}, u32[]{:S(2)}) collective-permute-start(f32[3584,128]{1,0:T(8,128)S(1)} %get-tuple-element.17.refs_3_), channel_id=1, source_target_pairs={{0,4},{4,8},{8,12},{12,16},{16,20},{20,24},{24,28},{28,32},{32,36}... | collective-permute-start | bytes 5505032 | tf_op jit(solution)/shard_map/ppermute | solution.py:440
  147.2 48.1 %collective-permute-start.3 = (f32[3584,128]{1,0:T(8,128)S(1)}, f32[3584,128]{1,0:T(8,128)S(1)}, u32[]{:S(2)}, u32[]{:S(2)}) collective-permute-start(f32[3584,128]{1,0:T(8,128)S(1)} %get-tuple-element.18.refs_1_), channel_id=1, source_target_pairs={{4,0},{8,4},{12,8},{16,12},{20,16},{24,20},{28,24},{32,28},{36,32}... | collective-permute-start | bytes 5505032 | tf_op jit(solution)/shard_map/ppermute | solution.py:445
  158.0 74.7 %collective-permute-start.4 = (f32[3584,128]{1,0:T(8,128)S(1)}, f32[3584,128]{1,0:T(8,128)S(1)}, u32[]{:S(2)}, u32[]{:S(2)}) collective-permute-start(f32[3584,128]{1,0:T(8,128)S(1)} %get-tuple-element.19.refs_3_.refs_7_), channel_id=1, source_target_pairs={{0,4},{4,8},{8,12},{12,16},{16,20},{20,24},{24,28},{28,32},{32,36}... | collective-permute-start | bytes 5505032 | tf_op jit(solution)/shard_map/ppermute | solution.py:440
  160.1 74.1 %collective-permute-start.5 = (f32[3584,128]{1,0:T(8,128)S(1)}, f32[3584,128]{1,0:T(8,128)S(1)}, u32[]{:S(2)}, u32[]{:S(2)}) collective-permute-start(f32[3584,128]{1,0:T(8,128)S(1)} %get-tuple-element.20.refs_1_.refs_5_), channel_id=1, source_target_pairs={{4,0},{8,4},{12,8},{16,12},{20,16},{24,20},{28,24},{32,28},{36,32}... | collective-permute-start | bytes 5505032 | tf_op jit(solution)/shard_map/ppermute | solution.py:445
  170.2 72.0 %collective-permute-start.6 = (f32[1024,128]{1,0:T(8,128)S(1)}, f32[1024,128]{1,0:T(8,128)S(1)}, u32[]{:S(2)}, u32[]{:S(2)}) collective-permute-start(f32[1024,128]{1,0:T(8,128)S(1)} %get-tuple-element.21.refs_3_.refs_11_), channel_id=1, source_target_pairs={{0,4},{4,8},{8,12},{12,16},{16,20},{20,24},{24,28},{28,32},{32,36}... | collective-permute-start | bytes 1572872 | tf_op jit(solution)/shard_map/ppermute | solution.py:440
  193.4 50.0 %collective-permute-start.7 = (f32[1024,128]{1,0:T(8,128)S(1)}, f32[1024,128]{1,0:T(8,128)S(1)}, u32[]{:S(2)}, u32[]{:S(2)}) collective-permute-start(f32[1024,128]{1,0:T(8,128)S(1)} %get-tuple-element.22.refs_1_.refs_9_), channel_id=1, source_target_pairs={{4,0},{8,4},{12,8},{16,12},{20,16},{24,20},{28,24},{32,28},{36,32}... | collective-permute-start | bytes 1572872 | tf_op jit(solution)/shard_map/ppermute | solution.py:445
  244.6 1.5 collective-permute-start.8
  246.1 7.0 %collective-permute-start.9 = (f32[384,128]{1,0:T(8,128)S(1)}, f32[384,128]{1,0:T(8,128)S(1)}, u32[]{:S(2)}, u32[]{:S(2)}) collective-permute-start(f32[384,128]{1,0:T(8,128)S(1)} %add.7.one_ref), channel_id=1, source_target_pairs={{0,2},{1,3},{2,0},{3,1},{4,6},{5,7},{6,4},{7,5},{8,10},{9,11},{10,... | collective-permute-start | bytes 589832 | tf_op jit(solution)/shard_map/ppermute | solution.py:212
